TPU v7x, 256 devices: a whole 4x4x8 slice. The times are simulated.
256 devices in a mesh: tm: 32 (over x, z), space: 8 (over y, core).
Axes of the slice: x: 4, y: 4, z: 8, core: 2. Of those that a mesh axis runs over, the one named last changes fastest.
Arguments:
- queries: bfloat16 [32, 5120, 2240], P('tm', 'space'), may hold values from -6 to 6
- keys: bfloat16 [32, 5120, 2240], P('tm', 'space'), may hold values from -6 to 6
- values: bfloat16 [32, 5120, 2240], P('tm', 'space'), may hold values from -6 to 6
- gain: float32 [2240], replicated, may hold values from 0.1 to 1.9
- out_weight: bfloat16 [2240, 2240], P('tm'), may hold values from -0.125 to 0.125
Outputs:
- projected: bfloat16 [32, 5120, 2240], P('tm', 'space')
All inputs are finite; a program needn't handle non-finite values.
Results may differ from a plain program's by a relative error of at most 0.0075.
Values may be sent and summed in bfloat16 or wider, within the bound.
No kernel may reach another device: no remote copies, remote signals or barrier semaphores. Data moves between devices by JAX's collectives and lax.ppermute only.
A program may use at most 128 MiB of HBM per device.

v0:
```python
import jax
import jax.numpy as jnp
from jax import lax
from jax.experimental import pallas as pl
from jax.experimental.pallas import tpu as pltpu
from jax.sharding import Mesh
from jax.sharding import PartitionSpec as P

HEADS = 20
HEAD_DIM = 112
D = HEADS * HEAD_DIM
PAD = 128
GROUP = 4
FULL = 18
PART = 64
bf16 = jnp.bfloat16
f32 = jnp.float32
TM = ("x", "z")
PIECES = ("x", "y", "core")
NX, NZ, NY, NC = 4, 8, 4, 2
ROWS_X = D // NX
COLS = 2304
BIG = 40 * 1024 * 1024
SMALL = 12 * 1024 * 1024


def state_kernel(k_ref, v_ref, o_ref, norm_ref):
    tokens = k_ref.shape[1]
    step = pl.program_id(0)
    ones = jnp.ones((PAD - HEAD_DIM, tokens), bf16)

    def state_of(g):
        rows = pl.ds(g * HEAD_DIM, HEAD_DIM)
        fk = jnp.maximum(k_ref[rows, :], 0)
        vals = jnp.concatenate([v_ref[rows, :], ones], axis=0)
        state = lax.dot_general(vals, fk, (((1,), (1,)), ((), ())), preferred_element_type=f32)
        state = jnp.concatenate([state, jnp.zeros((PAD, PAD - HEAD_DIM), f32)], axis=1)
        norm_ref[pl.ds(step * GROUP + g, 1), :] = state[HEAD_DIM : HEAD_DIM + 1]
        return state[:HEAD_DIM]

    @pl.when(step == 0)
    def _():
        norm_ref[...] = jnp.zeros_like(norm_ref)

    for g in range(2):
        at = pl.multiple_of((step * GROUP + g) * HEAD_DIM, 16)
        o_ref[pl.ds(at, HEAD_DIM), :] = state_of(g).astype(bf16)
    rest = [state_of(g) for g in range(2, GROUP)]

    @pl.when(step < HEADS // GROUP - 1)
    def _():
        for g in range(2, GROUP):
            at = pl.multiple_of((step * GROUP + g) * HEAD_DIM, 16)
            o_ref[pl.ds(at, HEAD_DIM), :] = rest[g - 2].astype(bf16)

    @pl.when(step == HEADS // GROUP - 1)
    def _():
        for g in range(2):
            for m in range(7):
                turned = pltpu.roll(rest[g], (HEAD_DIM - 16 * m) % PAD, 1).astype(bf16)
                o_ref[pl.ds((7 * g + m) * HEAD_DIM, HEAD_DIM), HEAD_DIM:] = turned[:, HEAD_DIM:]
        o_ref[pl.ds(FULL * HEAD_DIM, 32), :] = norm_ref[...].astype(bf16)


def states(k_t, v_t):
    tokens = k_t.shape[1]
    spec = pl.BlockSpec((GROUP * HEAD_DIM, tokens), lambda i: (i, 0))
    return pl.pallas_call(
        state_kernel,
        grid=(HEADS // GROUP,),
        in_specs=[spec, spec],
        out_specs=pl.BlockSpec((2048, PAD), lambda i: (0, 0)),
        out_shape=jax.ShapeDtypeStruct((2048, PAD), bf16),
        scratch_shapes=[pltpu.VMEM((32, PAD), f32)],
        compiler_params=pltpu.CompilerParams(vmem_limit_bytes=SMALL),
        name="states",
        cost_estimate=pl.CostEstimate(
            flops=2 * HEADS * PAD * PAD * tokens, bytes_accessed=4 * D * tokens, transcendentals=0
        ),
    )(k_t, v_t)


def in_tile_kernel(z_ref, r_ref, o_ref):
    z = z_ref[0]
    inclusive = None
    for x in range(NX):
        own = r_ref[x * 8].astype(f32)
        for s in range(1, 8):
            own = own + r_ref[x * 8 + s].astype(f32)
        exclusive = jnp.zeros_like(own) if inclusive is None else inclusive
        inclusive = exclusive + own
        later, earlier = inclusive.astype(bf16), exclusive.astype(bf16)
        for t in range(NZ):
            keep = (jnp.full(later.shape, t, jnp.int32) >= z).astype(f32)
            o_ref[t, x] = jnp.where(keep > 0, later.astype(f32), earlier.astype(f32)).astype(bf16)


def small_call(kernel, shape, scalars, arrays, scratch=()):
    return pl.pallas_call(
        kernel,
        in_specs=[pl.BlockSpec(memory_space=pltpu.SMEM)] * len(scalars)
        + [pl.BlockSpec(memory_space=pltpu.VMEM)] * len(arrays),
        out_specs=jax.tree.map(lambda _: pl.BlockSpec(memory_space=pltpu.VMEM), shape),
        out_shape=shape,
        scratch_shapes=list(scratch),
        compiler_params=pltpu.CompilerParams(vmem_limit_bytes=SMALL),
        cost_estimate=pl.CostEstimate(flops=1000000, bytes_accessed=2000000, transcendentals=0),
    )(*scalars, *arrays)


def prefix_kernel(r_ref, o_ref):
    for x in range(NX):
        total = r_ref[0, x].astype(f32)
        for t in range(1, NZ):
            total = total + r_ref[t, x].astype(f32)
        total = total.astype(bf16)
        for s in range(8):
            o_ref[x, s] = total


def slab_kernel(at_ref, w_ref, o_ref):
    slab, core = at_ref[0], at_ref[1]
    main = w_ref[:, pl.ds(pl.multiple_of(slab * 256, 256), 256)]
    first = w_ref[:, 2048:2176].astype(f32)
    last = w_ref[:, 2176:2240].astype(f32)
    last = jnp.concatenate([last, jnp.zeros_like(last)], axis=1)
    pick = jnp.full(first.shape, core, jnp.int32) == 0
    rest = jnp.where(pick, first, last).astype(bf16)
    for t in range(NZ):
        o_ref[t, :, :256] = main
        o_ref[t, :, 256:] = rest


def compact_kernel(w_ref, x_ref, y_ref, rows_ref):
    rows = w_ref.shape[1]
    for t in range(NZ):
        rows_ref[pl.ds(t * rows, rows), :] = w_ref[t].astype(f32)
    slab = rows_ref[...].astype(bf16)
    x_ref[0] = slab[:, :128]
    x_ref[1] = slab[:, 256:]
    y_ref[...] = slab[:, 128:256]


def stack_kernel(*refs):
    by_x, by_y, (main_x, main_y, every) = refs[:4], refs[4:8], refs[8:]
    for k in range(4):
        main_x[k] = by_x[k][0]
        main_y[k] = by_y[k][...]
        every[k] = by_x[k][1]
        every[4 + k] = by_x[k][0]
        every[8 + k] = by_y[k][...]


def project_kernel(at_ref, q_ref, p_ref, g_ref, *refs):
    parts, (o_ref, w_ref, mixed_ref, normed_ref, sem) = refs[:14], refs[14:]
    x, y, core = at_ref[0], at_ref[1], at_ref[2]
    groups = []

    def fetch(source, block, column):
        rows = pl.ds(pl.multiple_of(block * ROWS_X, 16), ROWS_X)
        at = sum(len(g) for g in groups)
        copy = pltpu.make_async_copy(source, w_ref.at[rows, pl.ds(column, 128)], sem.at[at])
        copy.start()
        groups[-1].append(copy)

    for side in range(NC):
        every, *rest = parts[7 * side : 7 * side + 7]
        by_y, by_x = (every.at[pl.ds(4, 4)], *rest[:3]), (every.at[pl.ds(8, 4)], *rest[3:])
        for n in range(4):
            groups.append([])
            for k in range(4):
                block = lax.rem(x - k + NX, NX)
                fetch(by_y[n].at[k], block, side * 1152 + n * 256)
                fetch(by_x[k].at[n], block, side * 1152 + n * 256 + 128)
        groups.append([])
        for k in range(4):
            fetch(every.at[k], lax.rem(x - k + NX, NX), side * 1152 + 1024)
    tokens = q_ref.shape[1]
    squares = jnp.zeros((1, tokens), f32)
    lane = lax.broadcasted_iota(jnp.int32, (HEAD_DIM, PAD), 1) // 16
    for h in range(HEADS):
        rows = pl.ds(h * HEAD_DIM, HEAD_DIM)
        fq = jnp.maximum(q_ref[rows, :], 0)
        if h < FULL:
            state = p_ref[rows, :]
        else:
            state = jnp.zeros((HEAD_DIM, PAD), f32)
            for m in range(7):
                piece = p_ref[pl.ds((7 * (h - FULL) + m) * HEAD_DIM, HEAD_DIM), :].astype(f32)
                state = jnp.where(lane == m, pltpu.roll(piece, (16 + 16 * m) % PAD, 1), state)
            state = state.astype(bf16)
        norms = p_ref[pl.ds(FULL * HEAD_DIM + h // 16 * 16, 16), :]
        prefix = jnp.concatenate([state, norms], axis=0)[:, :HEAD_DIM]
        sums = jnp.dot(prefix, fq, preferred_element_type=f32)
        norm = sums[HEAD_DIM + h % 16 : HEAD_DIM + h % 16 + 1]
        mixed = sums[:HEAD_DIM] * (1.0 / (norm + 1.0))
        squares = squares + jnp.sum(mixed * mixed, axis=0, keepdims=True)
        mixed_ref[rows, :] = mixed
    scale = lax.rsqrt(squares * (1.0 / D) + 1e-06)
    for i in range(0, D, 256):
        width = min(256, D - i)
        rows = pl.ds(i, width)
        normed = (mixed_ref[rows, :] * scale * g_ref[rows, :]).astype(bf16)
        normed_ref[:, pl.ds(i, width)] = normed.T

    def product(group, column, width):
        for copy in group:
            copy.wait()
        total = jnp.dot(normed_ref[...], w_ref[:, pl.ds(column, width)], preferred_element_type=f32)
        return total.astype(bf16).T

    for side in range(NC):
        which = core if side == 0 else 1 - core
        for n in range(4):
            at = pl.multiple_of(which * 1024 + lax.rem(y - n + NY, NY) * 256, 256)
            o_ref[pl.ds(at, 256), :] = product(groups[5 * side + n], side * 1152 + n * 256, 256)
        total = product(groups[5 * side + 4], side * 1152 + 1024, 128)

        @pl.when(which == 0)
        def _():
            o_ref[2048:2176, :] = total

        @pl.when(which == 1)
        def _():
            o_ref[2176:, :] = total[:64]


def project(at, q_t, prefix, gain, parts):
    tokens = q_t.shape[1]
    vmem = pl.BlockSpec(memory_space=pltpu.VMEM)
    anyw = pl.BlockSpec(memory_space=pl.ANY)
    return pl.pallas_call(
        project_kernel,
        in_specs=[pl.BlockSpec(memory_space=pltpu.SMEM), vmem, vmem, vmem] + [anyw] * 14,
        out_specs=vmem,
        out_shape=jax.ShapeDtypeStruct((D, tokens), bf16),
        scratch_shapes=[
            pltpu.VMEM((D, COLS), bf16),
            pltpu.VMEM((D, tokens), f32),
            pltpu.VMEM((tokens, D), bf16),
            pltpu.SemaphoreType.DMA((72,)),
        ],
        compiler_params=pltpu.CompilerParams(vmem_limit_bytes=BIG),
        name="project",
        cost_estimate=pl.CostEstimate(
            flops=2 * D * D * tokens, bytes_accessed=2 * D * COLS + 4 * D * tokens, transcendentals=0
        ),
    )(at, q_t, prefix, gain, *parts)


def swap(value, axes):
    return lax.all_to_all(value, axes, split_axis=0, concat_axis=0, tiled=True)


def moved(value, axis, step):
    n = lax.axis_size(axis)
    return lax.ppermute(value, axis, [(i, (i + step) % n) for i in range(n)])


def shifted(value, axis):
    return [moved(value, axis, k) for k in range(1, lax.axis_size(axis))]


def after(value, *others):
    return lax.optimization_barrier((value, *others))[0]


def step(queries, keys, values, gain, out_weight):
    q_t, k_t, v_t = (jnp.swapaxes(a[0], 0, 1) for a in (queries, keys, values))
    z, y, core = lax.axis_index("z"), lax.axis_index("y"), lax.axis_index("core")
    rows = out_weight.shape[0]
    at = jnp.stack([core * NY + y, core]).astype(jnp.int32)
    zs = z.astype(jnp.int32).reshape(1)
    rows = out_weight.shape[0]
    slab = small_call(slab_kernel, jax.ShapeDtypeStruct((NZ, rows, 384), bf16), (at,), (out_weight,))
    w_z = swap(slab, "z")
    k_t, v_t = (pltpu.with_memory_space_constraint(a, pltpu.HBM) for a in (k_t, v_t))
    st = after(states(k_t, v_t), w_z)
    r1 = swap(st.reshape(32, PART, PAD), PIECES)
    x0, y0 = small_call(
        compact_kernel,
        (jax.ShapeDtypeStruct((2, ROWS_X, 128), bf16), jax.ShapeDtypeStruct((ROWS_X, 128), bf16)),
        (),
        (w_z,),
        (pltpu.VMEM((NZ * rows, 384), f32),),
    )
    by_x = [x0, *shifted(x0, "x")]
    by_y = [y0, *shifted(y0, "y")]
    r2 = small_call(in_tile_kernel, jax.ShapeDtypeStruct((NZ, NX, PART, PAD), bf16), (zs,), (r1,))
    r2s = swap(r2, "z")
    four = jax.ShapeDtypeStruct((4, ROWS_X, 128), bf16)
    main_x, main_y, every = small_call(
        stack_kernel,
        (four, four, jax.ShapeDtypeStruct((12, ROWS_X, 128), bf16)),
        (),
        (*by_x, *by_y),
    )
    parts = [every, *shifted(main_x, "y"), *shifted(main_y, "x")]
    r3 = small_call(prefix_kernel, jax.ShapeDtypeStruct((NX, 8, PART, PAD), bf16), (), (r2s,))
    prefix = swap(r3.reshape(32, PART, PAD), PIECES).reshape(2048, PAD)
    parts += [moved(part, "core", 1) for part in parts]
    at = jnp.stack([lax.axis_index("x"), y, core]).astype(jnp.int32)
    out = project(at, q_t, prefix, gain.reshape(D, 1), parts)
    return jnp.swapaxes(out, 0, 1)[None]


def solution(mesh):
    finer = Mesh(mesh.devices.reshape(NX, NZ, NY, NC), ("x", "z", "y", "core"))
    tokens = P(TM, ("y", "core"), None)
    return jax.shard_map(
        step,
        mesh=finer,
        in_specs=(tokens, tokens, tokens, P(), P(TM, None)),
        out_specs=tokens,
        check_vma=False,
    )
```

profile of v0, /device:TPU:1, one launch (start us, length us, event | category | flops | bytes accessed | tf_op | source)
XLA Modules:
  0.0 158.3 jit_solution(10681063020521130523)
XLA Ops:
  0.0 0.1 pad_add_fusion.1.at_ref
  0.1 1.0 copy-done
  1.1 0.6 shard_map.55
  1.6 23.1 %all_to_all.20.w_ref = bf16[8,70,384]{2,1,0:T(8,128)(2,1)S(1)} all-to-all(bf16[8,70,384]{2,1,0:T(8,128)(2,1)S(1)} %shard_map.55), channel_id=1, replica_groups=mesh['x'=4,'z'=8,'y'=4,'core'=2] {'z'}, dimensions={0} | all-to-all | bytes 860160 | tf_op jit(solution)/shard_map/all_to_all | solution.py:252
  24.8 0.1 shard_map.58
  24.9 2.8 %collective-permute-start.5 = (bf16[560,128]{1,0:T(8,128)(2,1)S(1)}, bf16[560,128]{1,0:T(8,128)(2,1)S(1)}, u32[]{:S(2)}, u32[]{:S(2)}) collective-permute-start(bf16[560,128]{1,0:T(8,128)(2,1)S(1)} %get-tuple-element.13.refs_4_), channel_id=1, source_target_pairs={{0,6},{2,0},{4,2},{6,4},{1,7},{3,1},{5,3},{7,5},{8,14},{10,8},{12,... | collective-permute-start | bytes 430088 | tf_op jit(solution)/shard_map/ppermute | solution.py:257
  27.7 2.5 %collective-permute-start.2 = (bf16[2,560,128]{2,1,0:T(8,128)(2,1)S(1)}, bf16[2,560,128]{2,1,0:T(8,128)(2,1)S(1)}, u32[]{:S(2)}, u32[]{:S(2)}) collective-permute-start(bf16[2,560,128]{2,1,0:T(8,128)(2,1)S(1)} %get-tuple-element.12.refs_0_), channel_id=1, source_target_pairs={{0,192},{64,0},{128,64},{192,128},{1,193},{65,1},{129,65},{193,129... | collective-permute-start | bytes 860168 | tf_op jit(solution)/shard_map/ppermute | solution.py:257
  30.2 0.5 collective-permute-start.1
  30.7 0.6 collective-permute-start
  31.3 5.8 %states.1 = bf16[2048,128]{1,0:T(8,128)(2,1)} custom-call(bf16[2240,640]{1,0:T(8,128)(2,1)} %bitcast.21, bf16[2240,640]{1,0:T(8,128)(2,1)} %bitcast.22), custom_call_target="tpu_custom_call" | custom-call | flops 419430400 | bytes 5734400 | tf_op jit(solution)/shard_map/states/pallas_call | solution.py:68
  37.1 7.4 %all-to-all-start.1 = ((bf16[32,64,128]{2,1,0:T(8,128)(2,1)}), bf16[32,64,128]{2,1,0:T(8,128)(2,1)S(1)}, u32[]{:S(2)}, u32[]{:S(2)}) async-start(bf16[32,64,128]{2,1,0:T(8,128)(2,1)} %bitcast.11), calls=%async_computation.1 | async-start | bytes 1048576 | tf_op jit(solution)/shard_map/all_to_all | solution.py:252
  44.5 0.0 copy-start.9
  44.5 2.9 %collective-permute-start.4 = (bf16[560,128]{1,0:T(8,128)(2,1)S(1)}, bf16[560,128]{1,0:T(8,128)(2,1)S(1)}, u32[]{:S(2)}, u32[]{:S(2)}) collective-permute-start(bf16[560,128]{1,0:T(8,128)(2,1)S(1)} %get-tuple-element.13.refs_4_), channel_id=1, source_target_pairs={{0,4},{2,6},{4,0},{6,2},{1,5},{3,7},{5,1},{7,3},{8,12},{10,14},{12... | collective-permute-start | bytes 430088 | tf_op jit(solution)/shard_map/ppermute | solution.py:257
  47.5 0.3 collective-permute-start.3
  47.8 9.1 %collective-permute-done.4.refs_6_ = bf16[560,128]{1,0:T(8,128)(2,1)S(1)} collective-permute-done((bf16[560,128]{1,0:T(8,128)(2,1)S(1)}, bf16[560,128]{1,0:T(8,128)(2,1)S(1)}, u32[]{:S(2)}, u32[]{:S(2)}) %collective-permute-start.4) | collective-permute-done | bytes 143392 | tf_op jit(solution)/shard_map/ppermute | solution.py:257
  56.8 3.4 %collective-permute-done.3.refs_5_ = bf16[560,128]{1,0:T(8,128)(2,1)S(1)} collective-permute-done((bf16[560,128]{1,0:T(8,128)(2,1)S(1)}, bf16[560,128]{1,0:T(8,128)(2,1)S(1)}, u32[]{:S(2)}, u32[]{:S(2)}) %collective-permute-start.3) | collective-permute-done | bytes 143392 | tf_op jit(solution)/shard_map/ppermute | solution.py:257
  60.3 1.9 %shard_map.59 = (bf16[4,560,128]{2,1,0:T(8,128)(2,1)}, bf16[4,560,128]{2,1,0:T(8,128)(2,1)}, bf16[12,560,128]{2,1,0:T(8,128)(2,1)}) custom-call(bf16[2,560,128]{2,1,0:T(8,128)(2,1)S(1)} %get-tuple-element.12.refs_0_, bf16[2,560,128]{2,1,0:T(8,128)(2,1)S(1)} %collective-permute-done.refs_1_, bf16[2,560,128]{2,1,0:T(8,128)(2,1)S(1)} %collective-permute-done.1.refs_2_, ...), custom_call_target="tpu_custom_call" | custom-call | flops 1000000 | bytes 2000000 | tf_op jit(solution)/shard_map/pallas_call | solution.py:99
  62.1 1.3 collective-permute-start.7
  63.5 0.1 collective-permute-start.6
  63.6 2.2 %collective-permute-start.11 = (bf16[4,560,128]{2,1,0:T(8,128)(2,1)}, bf16[4,560,128]{2,1,0:T(8,128)(2,1)}, u32[]{:S(2)}, u32[]{:S(2)}) collective-permute-start(bf16[4,560,128]{2,1,0:T(8,128)(2,1)} %get-tuple-element.16), channel_id=1, source_target_pairs={{0,192},{64,0},{128,64},{192,128},{1,193},{65,1},{129,65},{193,129... | collective-permute-start | bytes 1720328 | tf_op jit(solution)/shard_map/ppermute | solution.py:257
  65.8 1.6 %collective-permute-start.12 = (bf16[12,560,128]{2,1,0:T(8,128)(2,1)}, bf16[12,560,128]{2,1,0:T(8,128)(2,1)S(1)}, u32[]{:S(2)}, u32[]{:S(2)}) collective-permute-start(bf16[12,560,128]{2,1,0:T(8,128)(2,1)} %get-tuple-element.14.refs_0_), channel_id=1, source_target_pairs={{0,1},{1,0},{2,3},{3,2},{4,5},{5,4},{6,7},{7,6},{8,9},{9,8},{10,11... | collective-permute-start | bytes 5160968 | tf_op jit(solution)/shard_map/ppermute | solution.py:257
  67.5 0.9 shard_map.56
  68.4 3.5 %all-to-all-start.2 = ((bf16[8,4,64,128]{3,2,1,0:T(8,128)(2,1)}), bf16[8,4,64,128]{3,2,1,0:T(8,128)(2,1)S(1)}, u32[]{:S(2)}, u32[]{:S(2)}) async-start(bf16[8,4,64,128]{3,2,1,0:T(8,128)(2,1)} %shard_map.56), calls=%async_computation.2 | async-start | bytes 1048576 | tf_op jit(solution)/shard_map/all_to_all | solution.py:252
  71.9 4.6 %collective-permute-done.8.refs_3_ = bf16[4,560,128]{2,1,0:T(8,128)(2,1)S(1)} collective-permute-done((bf16[4,560,128]{2,1,0:T(8,128)(2,1)}, bf16[4,560,128]{2,1,0:T(8,128)(2,1)S(1)}, u32[]{:S(2)}, u32[]{:S(2)}) %collective-permute-start.8) | collective-permute-done | bytes 573472 | tf_op jit(solution)/shard_map/ppermute | solution.py:257
  76.5 2.4 %collective-permute-start.10 = (bf16[4,560,128]{2,1,0:T(8,128)(2,1)}, bf16[4,560,128]{2,1,0:T(8,128)(2,1)}, u32[]{:S(2)}, u32[]{:S(2)}) collective-permute-start(bf16[4,560,128]{2,1,0:T(8,128)(2,1)} %get-tuple-element.16), channel_id=1, source_target_pairs={{0,128},{64,192},{128,0},{192,64},{1,129},{65,193},{129,1},{193,65... | collective-permute-start | bytes 1720328 | tf_op jit(solution)/shard_map/ppermute | solution.py:257
  78.9 0.2 collective-permute-start.9
  79.1 12.0 %collective-permute-done.6.refs_1_ = bf16[4,560,128]{2,1,0:T(8,128)(2,1)} collective-permute-done((bf16[4,560,128]{2,1,0:T(8,128)(2,1)}, bf16[4,560,128]{2,1,0:T(8,128)(2,1)}, u32[]{:S(2)}, u32[]{:S(2)}) %collective-permute-start.6) | collective-permute-done | bytes 573472 | tf_op jit(solution)/shard_map/ppermute | solution.py:257
  91.1 0.5 collective-permute-start.15
  91.6 0.0 collective-permute-start.14
  91.7 0.8 copy-done.3
  92.5 3.9 %collective-permute-start.13 = (bf16[4,560,128]{2,1,0:T(8,128)(2,1)}, bf16[4,560,128]{2,1,0:T(8,128)(2,1)}, u32[]{:S(2)}, u32[]{:S(2)}) collective-permute-start(bf16[4,560,128]{2,1,0:T(8,128)(2,1)} %collective-permute-done.6.refs_1_), channel_id=1, source_target_pairs={{0,1},{1,0},{2,3},{3,2},{4,5},{5,4},{6,7},{7,6},{8,9},{9,8},{10,11... | collective-permute-start | bytes 1720328 | tf_op jit(solution)/shard_map/ppermute | solution.py:257
  96.4 9.1 %collective-permute-done.9.refs_4_ = bf16[4,560,128]{2,1,0:T(8,128)(2,1)} collective-permute-done((bf16[4,560,128]{2,1,0:T(8,128)(2,1)}, bf16[4,560,128]{2,1,0:T(8,128)(2,1)}, u32[]{:S(2)}, u32[]{:S(2)}) %collective-permute-start.9) | collective-permute-done | bytes 573472 | tf_op jit(solution)/shard_map/ppermute | solution.py:257
  105.5 0.5 collective-permute-start.18
  106.0 0.8 copy-done.5
  106.8 0.0 collective-permute-start.17
  106.9 0.8 copy-done.7
  107.7 0.5 collective-permute-start.16
  108.2 0.9 shard_map.57
  109.1 8.4 %all-to-all-start.3 = ((bf16[32,64,128]{2,1,0:T(8,128)(2,1)}), bf16[32,64,128]{2,1,0:T(8,128)(2,1)S(1)}, u32[]{:S(2)}, u32[]{:S(2)}) async-start(bf16[32,64,128]{2,1,0:T(8,128)(2,1)} %bitcast.12), calls=%async_computation.3 | async-start | bytes 1048576 | tf_op jit(solution)/shard_map/all_to_all | solution.py:252
  117.6 0.3 reshape.20.g_ref
  117.9 0.1 pad_add_fusion.at_ref
  118.0 0.0 collective-permute-done.17.refs_12_
  118.0 11.1 %all-to-all-done.3 = bf16[32,64,128]{2,1,0:T(8,128)(2,1)S(1)} async-done(((bf16[32,64,128]{2,1,0:T(8,128)(2,1)}), bf16[32,64,128]{2,1,0:T(8,128)(2,1)S(1)}, u32[]{:S(2)}, u32[]{:S(2)}) %all-to-all-start.3) | async-done | bytes 524320 | tf_op jit(solution)/shard_map/all_to_all | solution.py:252
  129.2 1.1 copy-done.2
  130.2 1.1 copy-done.4
  131.3 1.1 copy-done.6
  132.3 1.1 copy-done.8
  133.4 24.7 %project.1 = bf16[2240,640]{1,0:T(8,128)(2,1)} custom-call(s32[3]{0:T(128)S(1)} %pad_add_fusion.at_ref, bf16[2240,640]{1,0:T(8,128)(2,1)} %bitcast.23, bf16[2048,128]{1,0:T(8,128)(2,1)S(1)} %bitcast.20, f32[2240,1]{1,0:T(8,128)S(1)} %reshape.20.g_ref, bf16[12,560,128]{2,1,0:T(8,128)(2,1)} %get-tuple-element.14.refs_0_, ...), custom_call_target="tpu_custom_call" | custom-call | flops 6422528000 | bytes 16056320 | tf_op jit(solution)/shard_map/project/pallas_call | solution.py:232
  (27 shorter events, 0.1 us)
Async XLA Ops:
  0.1 1.0 copy-start
  24.9 22.6 %collective-permute-start.5 = (bf16[560,128]{1,0:T(8,128)(2,1)S(1)}, bf16[560,128]{1,0:T(8,128)(2,1)S(1)}, u32[]{:S(2)}, u32[]{:S(2)}) collective-permute-start(bf16[560,128]{1,0:T(8,128)(2,1)S(1)} %get-tuple-element.13.refs_4_), channel_id=1, source_target_pairs={{0,6},{2,0},{4,2},{6,4},{1,7},{3,1},{5,3},{7,5},{8,14},{10,8},{12,... | collective-permute-start | bytes 430088 | tf_op jit(solution)/shard_map/ppermute | solution.py:257
  27.7 32.6 %collective-permute-start.2 = (bf16[2,560,128]{2,1,0:T(8,128)(2,1)S(1)}, bf16[2,560,128]{2,1,0:T(8,128)(2,1)S(1)}, u32[]{:S(2)}, u32[]{:S(2)}) collective-permute-start(bf16[2,560,128]{2,1,0:T(8,128)(2,1)S(1)} %get-tuple-element.12.refs_0_), channel_id=1, source_target_pairs={{0,192},{64,0},{128,64},{192,128},{1,193},{65,1},{129,65},{193,129... | collective-permute-start | bytes 860168 | tf_op jit(solution)/shard_map/ppermute | solution.py:257
  30.2 30.1 %collective-permute-start.1 = (bf16[2,560,128]{2,1,0:T(8,128)(2,1)S(1)}, bf16[2,560,128]{2,1,0:T(8,128)(2,1)S(1)}, u32[]{:S(2)}, u32[]{:S(2)}) collective-permute-start(bf16[2,560,128]{2,1,0:T(8,128)(2,1)S(1)} %get-tuple-element.12.refs_0_), channel_id=1, source_target_pairs={{0,128},{64,192},{128,0},{192,64},{1,129},{65,193},{129,1},{193,65... | collective-permute-start | bytes 860168 | tf_op jit(solution)/shard_map/ppermute | solution.py:257
  30.7 29.6 %collective-permute-start = (bf16[2,560,128]{2,1,0:T(8,128)(2,1)S(1)}, bf16[2,560,128]{2,1,0:T(8,128)(2,1)S(1)}, u32[]{:S(2)}, u32[]{:S(2)}) collective-permute-start(bf16[2,560,128]{2,1,0:T(8,128)(2,1)S(1)} %get-tuple-element.12.refs_0_), channel_id=1, source_target_pairs={{0,64},{64,128},{128,192},{192,0},{1,65},{65,129},{129,193},{193,1... | collective-permute-start | bytes 860168 | tf_op jit(solution)/shard_map/ppermute | solution.py:257
  37.1 30.4 %all-to-all-start.1 = ((bf16[32,64,128]{2,1,0:T(8,128)(2,1)}), bf16[32,64,128]{2,1,0:T(8,128)(2,1)S(1)}, u32[]{:S(2)}, u32[]{:S(2)}) async-start(bf16[32,64,128]{2,1,0:T(8,128)(2,1)} %bitcast.11), calls=%async_computation.1 | async-start | bytes 1048576 | tf_op jit(solution)/shard_map/all_to_all | solution.py:252
  44.5 73.1 %copy-start.9 = (f32[2240]{0:T(1024)S(1)}, f32[2240]{0:T(1024)}, u32[]{:S(2)}) copy-start(f32[2240]{0:T(1024)} %param.8) | copy-start | bytes 26884
  44.5 12.3 %collective-permute-start.4 = (bf16[560,128]{1,0:T(8,128)(2,1)S(1)}, bf16[560,128]{1,0:T(8,128)(2,1)S(1)}, u32[]{:S(2)}, u32[]{:S(2)}) collective-permute-start(bf16[560,128]{1,0:T(8,128)(2,1)S(1)} %get-tuple-element.13.refs_4_), channel_id=1, source_target_pairs={{0,4},{2,6},{4,0},{6,2},{1,5},{3,7},{5,1},{7,3},{8,12},{10,14},{12... | collective-permute-start | bytes 430088 | tf_op jit(solution)/shard_map/ppermute | solution.py:257
  47.5 12.8 %collective-permute-start.3 = (bf16[560,128]{1,0:T(8,128)(2,1)S(1)}, bf16[560,128]{1,0:T(8,128)(2,1)S(1)}, u32[]{:S(2)}, u32[]{:S(2)}) collective-permute-start(bf16[560,128]{1,0:T(8,128)(2,1)S(1)} %get-tuple-element.13.refs_4_), channel_id=1, source_target_pairs={{0,2},{2,4},{4,6},{6,0},{1,3},{3,5},{5,7},{7,1},{8,10},{10,12},{12... | collective-permute-start | bytes 430088 | tf_op jit(solution)/shard_map/ppermute | solution.py:257
  62.1 14.4 %collective-permute-start.8 = (bf16[4,560,128]{2,1,0:T(8,128)(2,1)}, bf16[4,560,128]{2,1,0:T(8,128)(2,1)S(1)}, u32[]{:S(2)}, u32[]{:S(2)}) collective-permute-start(bf16[4,560,128]{2,1,0:T(8,128)(2,1)} %get-tuple-element.15), channel_id=1, source_target_pairs={{0,6},{2,0},{4,2},{6,4},{1,7},{3,1},{5,3},{7,5},{8,14},{10,8},{12,... | collective-permute-start | bytes 1720328 | tf_op jit(solution)/shard_map/ppermute | solution.py:257
  62.1 16.8 %collective-permute-start.7 = (bf16[4,560,128]{2,1,0:T(8,128)(2,1)}, bf16[4,560,128]{2,1,0:T(8,128)(2,1)S(1)}, u32[]{:S(2)}, u32[]{:S(2)}) collective-permute-start(bf16[4,560,128]{2,1,0:T(8,128)(2,1)} %get-tuple-element.15), channel_id=1, source_target_pairs={{0,4},{2,6},{4,0},{6,2},{1,5},{3,7},{5,1},{7,3},{8,12},{10,14},{12... | collective-permute-start | bytes 1720328 | tf_op jit(solution)/shard_map/ppermute | solution.py:257
  63.5 27.7 %collective-permute-start.6 = (bf16[4,560,128]{2,1,0:T(8,128)(2,1)}, bf16[4,560,128]{2,1,0:T(8,128)(2,1)}, u32[]{:S(2)}, u32[]{:S(2)}) collective-permute-start(bf16[4,560,128]{2,1,0:T(8,128)(2,1)} %get-tuple-element.15), channel_id=1, source_target_pairs={{0,2},{2,4},{4,6},{6,0},{1,3},{3,5},{5,7},{7,1},{8,10},{10,12},{12... | collective-permute-start | bytes 1720328 | tf_op jit(solution)/shard_map/ppermute | solution.py:257
  63.6 28.0 %collective-permute-start.11 = (bf16[4,560,128]{2,1,0:T(8,128)(2,1)}, bf16[4,560,128]{2,1,0:T(8,128)(2,1)}, u32[]{:S(2)}, u32[]{:S(2)}) collective-permute-start(bf16[4,560,128]{2,1,0:T(8,128)(2,1)} %get-tuple-element.16), channel_id=1, source_target_pairs={{0,192},{64,0},{128,64},{192,128},{1,193},{65,1},{129,65},{193,129... | collective-permute-start | bytes 1720328 | tf_op jit(solution)/shard_map/ppermute | solution.py:257
  65.8 63.3 %collective-permute-start.12 = (bf16[12,560,128]{2,1,0:T(8,128)(2,1)}, bf16[12,560,128]{2,1,0:T(8,128)(2,1)S(1)}, u32[]{:S(2)}, u32[]{:S(2)}) collective-permute-start(bf16[12,560,128]{2,1,0:T(8,128)(2,1)} %get-tuple-element.14.refs_0_), channel_id=1, source_target_pairs={{0,1},{1,0},{2,3},{3,2},{4,5},{5,4},{6,7},{7,6},{8,9},{9,8},{10,11... | collective-permute-start | bytes 5160968 | tf_op jit(solution)/shard_map/ppermute | solution.py:257
  68.4 39.8 %all-to-all-start.2 = ((bf16[8,4,64,128]{3,2,1,0:T(8,128)(2,1)}), bf16[8,4,64,128]{3,2,1,0:T(8,128)(2,1)S(1)}, u32[]{:S(2)}, u32[]{:S(2)}) async-start(bf16[8,4,64,128]{3,2,1,0:T(8,128)(2,1)} %shard_map.56), calls=%async_computation.2 | async-start | bytes 1048576 | tf_op jit(solution)/shard_map/all_to_all | solution.py:252
  76.5 41.1 %copy-start.1 = (bf16[4,560,128]{2,1,0:T(8,128)(2,1)}, bf16[4,560,128]{2,1,0:T(8,128)(2,1)S(1)}, u32[]{:S(2)}) copy-start(bf16[4,560,128]{2,1,0:T(8,128)(2,1)S(1)} %collective-permute-done.8.refs_3_) | copy-start | bytes 1720324
  76.5 16.0 %collective-permute-start.10 = (bf16[4,560,128]{2,1,0:T(8,128)(2,1)}, bf16[4,560,128]{2,1,0:T(8,128)(2,1)}, u32[]{:S(2)}, u32[]{:S(2)}) collective-permute-start(bf16[4,560,128]{2,1,0:T(8,128)(2,1)} %get-tuple-element.16), channel_id=1, source_target_pairs={{0,128},{64,192},{128,0},{192,64},{1,129},{65,193},{129,1},{193,65... | collective-permute-start | bytes 1720328 | tf_op jit(solution)/shard_map/ppermute | solution.py:257
  78.9 26.6 %collective-permute-start.9 = (bf16[4,560,128]{2,1,0:T(8,128)(2,1)}, bf16[4,560,128]{2,1,0:T(8,128)(2,1)}, u32[]{:S(2)}, u32[]{:S(2)}) collective-permute-start(bf16[4,560,128]{2,1,0:T(8,128)(2,1)} %get-tuple-element.16), channel_id=1, source_target_pairs={{0,64},{64,128},{128,192},{192,0},{1,65},{65,129},{129,193},{193,1... | collective-permute-start | bytes 1720328 | tf_op jit(solution)/shard_map/ppermute | solution.py:257
  91.1 14.9 %collective-permute-start.15 = (bf16[4,560,128]{2,1,0:T(8,128)(2,1)S(1)}, bf16[4,560,128]{2,1,0:T(8,128)(2,1)S(1)}, u32[]{:S(2)}, u32[]{:S(2)}) collective-permute-start(bf16[4,560,128]{2,1,0:T(8,128)(2,1)S(1)} %collective-permute-done.8.refs_3_), channel_id=1, source_target_pairs={{0,1},{1,0},{2,3},{3,2},{4,5},{5,4},{6,7},{7,6},{8,9},{9,8},{10,11... | collective-permute-start | bytes 1720328 | tf_op jit(solution)/shard_map/ppermute | solution.py:257
  91.6 15.2 %collective-permute-start.14 = (bf16[4,560,128]{2,1,0:T(8,128)(2,1)S(1)}, bf16[4,560,128]{2,1,0:T(8,128)(2,1)S(1)}, u32[]{:S(2)}, u32[]{:S(2)}) collective-permute-start(bf16[4,560,128]{2,1,0:T(8,128)(2,1)S(1)} %collective-permute-done.7.refs_2_), channel_id=1, source_target_pairs={{0,1},{1,0},{2,3},{3,2},{4,5},{5,4},{6,7},{7,6},{8,9},{9,8},{10,11... | collective-permute-start | bytes 1720328 | tf_op jit(solution)/shard_map/ppermute | solution.py:257
  91.7 0.8 copy-start.3
  92.5 25.5 %collective-permute-start.13 = (bf16[4,560,128]{2,1,0:T(8,128)(2,1)}, bf16[4,560,128]{2,1,0:T(8,128)(2,1)}, u32[]{:S(2)}, u32[]{:S(2)}) collective-permute-start(bf16[4,560,128]{2,1,0:T(8,128)(2,1)} %collective-permute-done.6.refs_1_), channel_id=1, source_target_pairs={{0,1},{1,0},{2,3},{3,2},{4,5},{5,4},{6,7},{7,6},{8,9},{9,8},{10,11... | collective-permute-start | bytes 1720328 | tf_op jit(solution)/shard_map/ppermute | solution.py:257
  105.5 12.5 %collective-permute-start.18 = (bf16[4,560,128]{2,1,0:T(8,128)(2,1)}, bf16[4,560,128]{2,1,0:T(8,128)(2,1)}, u32[]{:S(2)}, u32[]{:S(2)}) collective-permute-start(bf16[4,560,128]{2,1,0:T(8,128)(2,1)} %collective-permute-done.11.refs_6_), channel_id=1, source_target_pairs={{0,1},{1,0},{2,3},{3,2},{4,5},{5,4},{6,7},{7,6},{8,9},{9,8},{10,11... | collective-permute-start | bytes 1720328 | tf_op jit(solution)/shard_map/ppermute | solution.py:257
  106.0 0.8 copy-start.5
  106.8 11.2 %collective-permute-start.17 = (bf16[4,560,128]{2,1,0:T(8,128)(2,1)}, bf16[4,560,128]{2,1,0:T(8,128)(2,1)}, u32[]{:S(2)}, u32[]{:S(2)}) collective-permute-start(bf16[4,560,128]{2,1,0:T(8,128)(2,1)} %collective-permute-done.10.refs_5_), channel_id=1, source_target_pairs={{0,1},{1,0},{2,3},{3,2},{4,5},{5,4},{6,7},{7,6},{8,9},{9,8},{10,11... | collective-permute-start | bytes 1720328 | tf_op jit(solution)/shard_map/ppermute | solution.py:257
  106.9 0.9 copy-start.7
  107.7 10.3 %collective-permute-start.16 = (bf16[4,560,128]{2,1,0:T(8,128)(2,1)}, bf16[4,560,128]{2,1,0:T(8,128)(2,1)}, u32[]{:S(2)}, u32[]{:S(2)}) collective-permute-start(bf16[4,560,128]{2,1,0:T(8,128)(2,1)} %collective-permute-done.9.refs_4_), channel_id=1, source_target_pairs={{0,1},{1,0},{2,3},{3,2},{4,5},{5,4},{6,7},{7,6},{8,9},{9,8},{10,11... | collective-permute-start | bytes 1720328 | tf_op jit(solution)/shard_map/ppermute | solution.py:257
  109.1 20.1 %all-to-all-start.3 = ((bf16[32,64,128]{2,1,0:T(8,128)(2,1)}), bf16[32,64,128]{2,1,0:T(8,128)(2,1)S(1)}, u32[]{:S(2)}, u32[]{:S(2)}) async-start(bf16[32,64,128]{2,1,0:T(8,128)(2,1)} %bitcast.12), calls=%async_computation.3 | async-start | bytes 1048576 | tf_op jit(solution)/shard_map/all_to_all | solution.py:252
  129.2 1.1 copy-start.2
  130.2 1.1 copy-start.4
  131.3 1.1 copy-start.6
  132.3 1.1 copy-start.8
where the time goes:
time: 159 us; the launch traced here: 158 us
  waiting for transfers between devices  49.4 us (31%)
  starting transfers between devices  42.4 us (27%)
  Pallas kernels  34.8 us (22%)
  blocking collectives  23.1 us (15%)
  local copies, waits for them, and re-layouts  8.04 us (5%)
    ppermute x19, waiting for transfers between devices, moved(): return lax.ppermute(value, axis, [(i, (i + step) % n) for i in range(n)])  38.3 us
    pallas_call x1, Pallas kernels, project(): pl.pallas_call(project_kernel, in_specs=[pl.BlockSpec(memory_space=pltpu....  24.7 us
    all_to_all x1, blocking collectives, swap(): return lax.all_to_all(value, axes, split_axis=0, concat_axis=0, tiled=True)  23.1 us
    ppermute x19, starting transfers between devices, moved(): return lax.ppermute(value, axis, [(i, (i + step) % n) for i in range(n)])  23 us
    all_to_all x3, starting transfers between devices, swap(): return lax.all_to_all(value, axes, split_axis=0, concat_axis=0, tiled=True)  19.4 us
    all_to_all x3, waiting for transfers between devices, swap(): return lax.all_to_all(value, axes, split_axis=0, concat_axis=0, tiled=True)  11.1 us
    unnamed x20, local copies, waits for them, and re-layouts  7.69 us
    pallas_call x1, Pallas kernels, states(): pl.pallas_call(state_kernel, grid=(HEADS // GROUP,), in_specs=[spec, spec...  5.78 us
  transfers between devices with their start and end apart: 22, of which 6 were waited for; matrix products, arithmetic and copies ran while one was open for 0% of the time, Pallas kernels for 6%

commit v1 on v0

--- a/solution.py
+++ b/solution.py
@@ -154,27 +154,27 @@
 def project_kernel(at_ref, q_ref, p_ref, g_ref, *refs):
     parts, (o_ref, w_ref, mixed_ref, normed_ref, sem) = refs[:14], refs[14:]
     x, y, core = at_ref[0], at_ref[1], at_ref[2]
-    groups = []
+    copies = []
 
     def fetch(source, block, column):
         rows = pl.ds(pl.multiple_of(block * ROWS_X, 16), ROWS_X)
-        at = sum(len(g) for g in groups)
-        copy = pltpu.make_async_copy(source, w_ref.at[rows, pl.ds(column, 128)], sem.at[at])
-        copy.start()
-        groups[-1].append(copy)
+        target = w_ref.at[rows, pl.ds(pl.multiple_of(column, 128), 128)]
+        copies.append(pltpu.make_async_copy(source, target, sem.at[len(copies)]))
+        copies[-1].start()
 
     for side in range(NC):
+        which = core if side == 0 else 1 - core
         every, *rest = parts[7 * side : 7 * side + 7]
         by_y, by_x = (every.at[pl.ds(4, 4)], *rest[:3]), (every.at[pl.ds(8, 4)], *rest[3:])
-        for n in range(4):
-            groups.append([])
-            for k in range(4):
-                block = lax.rem(x - k + NX, NX)
-                fetch(by_y[n].at[k], block, side * 1152 + n * 256)
-                fetch(by_x[k].at[n], block, side * 1152 + n * 256 + 128)
-        groups.append([])
         for k in range(4):
-            fetch(every.at[k], lax.rem(x - k + NX, NX), side * 1152 + 1024)
+            block = lax.rem(x - k + NX, NX)
+            column = which * 1024 + lax.rem(y - k + NY, NY) * 256
+            fetch(every.at[k], block, 2048 + which * 128)
+            for n in range(4):
+                turn = lax.rem(y - n + NY, NY)
+                fetch(by_y[n].at[k], block, which * 1024 + turn * 256)
+                turn = lax.rem(x - n + NX, NX)
+                fetch(by_x[n].at[k], turn, column + 128)
     tokens = q_ref.shape[1]
     squares = jnp.zeros((1, tokens), f32)
     lane = lax.broadcasted_iota(jnp.int32, (HEAD_DIM, PAD), 1) // 16
@@ -202,27 +202,12 @@
         rows = pl.ds(i, width)
         normed = (mixed_ref[rows, :] * scale * g_ref[rows, :]).astype(bf16)
         normed_ref[:, pl.ds(i, width)] = normed.T
-
-    def product(group, column, width):
-        for copy in group:
-            copy.wait()
-        total = jnp.dot(normed_ref[...], w_ref[:, pl.ds(column, width)], preferred_element_type=f32)
-        return total.astype(bf16).T
-
-    for side in range(NC):
-        which = core if side == 0 else 1 - core
-        for n in range(4):
-            at = pl.multiple_of(which * 1024 + lax.rem(y - n + NY, NY) * 256, 256)
-            o_ref[pl.ds(at, 256), :] = product(groups[5 * side + n], side * 1152 + n * 256, 256)
-        total = product(groups[5 * side + 4], side * 1152 + 1024, 128)
-
-        @pl.when(which == 0)
-        def _():
-            o_ref[2048:2176, :] = total
-
-        @pl.when(which == 1)
-        def _():
-            o_ref[2176:, :] = total[:64]
+    for copy in copies:
+        copy.wait()
+    for j in range(0, D, 256):
+        width = min(256, D - j)
+        total = jnp.dot(normed_ref[...], w_ref[:, pl.ds(j, 256)], preferred_element_type=f32)
+        o_ref[pl.ds(j, width), :] = total.astype(bf16).T[:width]
 
 
 def project(at, q_t, prefix, gain, parts):

time: 159 us -> 149 us (0.937)
  Pallas kernels: 34.8 us -> 25.2 us
    pallas_call x1, Pallas kernels: 24.7 us -> 15 us  [project(): pl.pallas_call(project_kernel, in_specs=[pl.BlockSpec(memory_space=pltpu....]
where the time goes in v1:
time: 149 us
  waiting for transfers between devices  49.4 us (33%)
  starting transfers between devices  42.4 us (28%)
  Pallas kernels  25.2 us (17%)
  blocking collectives  23.1 us (16%)
  local copies, waits for them, and re-layouts  8.04 us (5%)
    ppermute x19, waiting for transfers between devices, moved(): return lax.ppermute(value, axis, [(i, (i + step) % n) for i in range(n)])  38.3 us
    all_to_all x1, blocking collectives, swap(): return lax.all_to_all(value, axes, split_axis=0, concat_axis=0, tiled=True)  23.1 us
    ppermute x19, starting transfers between devices, moved(): return lax.ppermute(value, axis, [(i, (i + step) % n) for i in range(n)])  23 us
    all_to_all x3, starting transfers between devices, swap(): return lax.all_to_all(value, axes, split_axis=0, concat_axis=0, tiled=True)  19.4 us
    pallas_call x1, Pallas kernels, project(): pl.pallas_call(project_kernel, in_specs=[pl.BlockSpec(memory_space=pltpu....  15 us
    all_to_all x3, waiting for transfers between devices, swap(): return lax.all_to_all(value, axes, split_axis=0, concat_axis=0, tiled=True)  11.1 us
    unnamed x20, local copies, waits for them, and re-layouts  7.69 us
    pallas_call x1, Pallas kernels, states(): pl.pallas_call(state_kernel, grid=(HEADS // GROUP,), in_specs=[spec, spec...  5.78 us
  transfers between devices with their start and end apart: 22, of which 6 were waited for; matrix products, arithmetic and copies ran while one was open for 0% of the time, Pallas kernels for 6%

profile of v1, /device:TPU:1, one launch (start us, length us, event | category | flops | bytes accessed | tf_op | source)
XLA Modules:
  0.0 148.6 jit_solution(10352718043311054882)
XLA Ops:
  0.0 0.1 pad_add_fusion.1.at_ref
  0.1 1.0 copy-done
  1.1 0.6 shard_map.55
  1.6 23.1 %all_to_all.20.w_ref = bf16[8,70,384]{2,1,0:T(8,128)(2,1)S(1)} all-to-all(bf16[8,70,384]{2,1,0:T(8,128)(2,1)S(1)} %shard_map.55), channel_id=1, replica_groups=mesh['x'=4,'z'=8,'y'=4,'core'=2] {'z'}, dimensions={0} | all-to-all | bytes 860160 | tf_op jit(solution)/shard_map/all_to_all | solution.py:237
  24.8 0.1 shard_map.58
  24.9 2.8 %collective-permute-start.5 = (bf16[560,128]{1,0:T(8,128)(2,1)S(1)}, bf16[560,128]{1,0:T(8,128)(2,1)S(1)}, u32[]{:S(2)}, u32[]{:S(2)}) collective-permute-start(bf16[560,128]{1,0:T(8,128)(2,1)S(1)} %get-tuple-element.13.refs_4_), channel_id=1, source_target_pairs={{0,6},{2,0},{4,2},{6,4},{1,7},{3,1},{5,3},{7,5},{8,14},{10,8},{12,... | collective-permute-start | bytes 430088 | tf_op jit(solution)/shard_map/ppermute | solution.py:242
  27.7 2.5 %collective-permute-start.2 = (bf16[2,560,128]{2,1,0:T(8,128)(2,1)S(1)}, bf16[2,560,128]{2,1,0:T(8,128)(2,1)S(1)}, u32[]{:S(2)}, u32[]{:S(2)}) collective-permute-start(bf16[2,560,128]{2,1,0:T(8,128)(2,1)S(1)} %get-tuple-element.12.refs_0_), channel_id=1, source_target_pairs={{0,192},{64,0},{128,64},{192,128},{1,193},{65,1},{129,65},{193,129... | collective-permute-start | bytes 860168 | tf_op jit(solution)/shard_map/ppermute | solution.py:242
  30.2 0.5 collective-permute-start.1
  30.7 0.6 collective-permute-start
  31.3 5.8 %states.1 = bf16[2048,128]{1,0:T(8,128)(2,1)} custom-call(bf16[2240,640]{1,0:T(8,128)(2,1)} %bitcast.21, bf16[2240,640]{1,0:T(8,128)(2,1)} %bitcast.22), custom_call_target="tpu_custom_call" | custom-call | flops 419430400 | bytes 5734400 | tf_op jit(solution)/shard_map/states/pallas_call | solution.py:68
  37.1 7.4 %all-to-all-start.1 = ((bf16[32,64,128]{2,1,0:T(8,128)(2,1)}), bf16[32,64,128]{2,1,0:T(8,128)(2,1)S(1)}, u32[]{:S(2)}, u32[]{:S(2)}) async-start(bf16[32,64,128]{2,1,0:T(8,128)(2,1)} %bitcast.11), calls=%async_computation.1 | async-start | bytes 1048576 | tf_op jit(solution)/shard_map/all_to_all | solution.py:237
  44.5 0.0 copy-start.9
  44.5 2.9 %collective-permute-start.4 = (bf16[560,128]{1,0:T(8,128)(2,1)S(1)}, bf16[560,128]{1,0:T(8,128)(2,1)S(1)}, u32[]{:S(2)}, u32[]{:S(2)}) collective-permute-start(bf16[560,128]{1,0:T(8,128)(2,1)S(1)} %get-tuple-element.13.refs_4_), channel_id=1, source_target_pairs={{0,4},{2,6},{4,0},{6,2},{1,5},{3,7},{5,1},{7,3},{8,12},{10,14},{12... | collective-permute-start | bytes 430088 | tf_op jit(solution)/shard_map/ppermute | solution.py:242
  47.5 0.3 collective-permute-start.3
  47.8 9.1 %collective-permute-done.4.refs_6_ = bf16[560,128]{1,0:T(8,128)(2,1)S(1)} collective-permute-done((bf16[560,128]{1,0:T(8,128)(2,1)S(1)}, bf16[560,128]{1,0:T(8,128)(2,1)S(1)}, u32[]{:S(2)}, u32[]{:S(2)}) %collective-permute-start.4) | collective-permute-done | bytes 143392 | tf_op jit(solution)/shard_map/ppermute | solution.py:242
  56.8 3.4 %collective-permute-done.3.refs_5_ = bf16[560,128]{1,0:T(8,128)(2,1)S(1)} collective-permute-done((bf16[560,128]{1,0:T(8,128)(2,1)S(1)}, bf16[560,128]{1,0:T(8,128)(2,1)S(1)}, u32[]{:S(2)}, u32[]{:S(2)}) %collective-permute-start.3) | collective-permute-done | bytes 143392 | tf_op jit(solution)/shard_map/ppermute | solution.py:242
  60.3 1.9 %shard_map.59 = (bf16[4,560,128]{2,1,0:T(8,128)(2,1)}, bf16[4,560,128]{2,1,0:T(8,128)(2,1)}, bf16[12,560,128]{2,1,0:T(8,128)(2,1)}) custom-call(bf16[2,560,128]{2,1,0:T(8,128)(2,1)S(1)} %get-tuple-element.12.refs_0_, bf16[2,560,128]{2,1,0:T(8,128)(2,1)S(1)} %collective-permute-done.refs_1_, bf16[2,560,128]{2,1,0:T(8,128)(2,1)S(1)} %collective-permute-done.1.refs_2_, ...), custom_call_target="tpu_custom_call" | custom-call | flops 1000000 | bytes 2000000 | tf_op jit(solution)/shard_map/pallas_call | solution.py:99
  62.1 1.3 collective-permute-start.7
  63.5 0.1 collective-permute-start.6
  63.6 2.2 %collective-permute-start.11 = (bf16[4,560,128]{2,1,0:T(8,128)(2,1)}, bf16[4,560,128]{2,1,0:T(8,128)(2,1)}, u32[]{:S(2)}, u32[]{:S(2)}) collective-permute-start(bf16[4,560,128]{2,1,0:T(8,128)(2,1)} %get-tuple-element.16), channel_id=1, source_target_pairs={{0,192},{64,0},{128,64},{192,128},{1,193},{65,1},{129,65},{193,129... | collective-permute-start | bytes 1720328 | tf_op jit(solution)/shard_map/ppermute | solution.py:242
  65.8 1.6 %collective-permute-start.12 = (bf16[12,560,128]{2,1,0:T(8,128)(2,1)}, bf16[12,560,128]{2,1,0:T(8,128)(2,1)S(1)}, u32[]{:S(2)}, u32[]{:S(2)}) collective-permute-start(bf16[12,560,128]{2,1,0:T(8,128)(2,1)} %get-tuple-element.14.refs_0_), channel_id=1, source_target_pairs={{0,1},{1,0},{2,3},{3,2},{4,5},{5,4},{6,7},{7,6},{8,9},{9,8},{10,11... | collective-permute-start | bytes 5160968 | tf_op jit(solution)/shard_map/ppermute | solution.py:242
  67.5 0.9 shard_map.56
  68.4 3.5 %all-to-all-start.2 = ((bf16[8,4,64,128]{3,2,1,0:T(8,128)(2,1)}), bf16[8,4,64,128]{3,2,1,0:T(8,128)(2,1)S(1)}, u32[]{:S(2)}, u32[]{:S(2)}) async-start(bf16[8,4,64,128]{3,2,1,0:T(8,128)(2,1)} %shard_map.56), calls=%async_computation.2 | async-start | bytes 1048576 | tf_op jit(solution)/shard_map/all_to_all | solution.py:237
  71.9 4.6 %collective-permute-done.8.refs_3_ = bf16[4,560,128]{2,1,0:T(8,128)(2,1)S(1)} collective-permute-done((bf16[4,560,128]{2,1,0:T(8,128)(2,1)}, bf16[4,560,128]{2,1,0:T(8,128)(2,1)S(1)}, u32[]{:S(2)}, u32[]{:S(2)}) %collective-permute-start.8) | collective-permute-done | bytes 573472 | tf_op jit(solution)/shard_map/ppermute | solution.py:242
  76.5 2.4 %collective-permute-start.10 = (bf16[4,560,128]{2,1,0:T(8,128)(2,1)}, bf16[4,560,128]{2,1,0:T(8,128)(2,1)}, u32[]{:S(2)}, u32[]{:S(2)}) collective-permute-start(bf16[4,560,128]{2,1,0:T(8,128)(2,1)} %get-tuple-element.16), channel_id=1, source_target_pairs={{0,128},{64,192},{128,0},{192,64},{1,129},{65,193},{129,1},{193,65... | collective-permute-start | bytes 1720328 | tf_op jit(solution)/shard_map/ppermute | solution.py:242
  78.9 0.2 collective-permute-start.9
  79.1 12.0 %collective-permute-done.6.refs_1_ = bf16[4,560,128]{2,1,0:T(8,128)(2,1)} collective-permute-done((bf16[4,560,128]{2,1,0:T(8,128)(2,1)}, bf16[4,560,128]{2,1,0:T(8,128)(2,1)}, u32[]{:S(2)}, u32[]{:S(2)}) %collective-permute-start.6) | collective-permute-done | bytes 573472 | tf_op jit(solution)/shard_map/ppermute | solution.py:242
  91.1 0.5 collective-permute-start.15
  91.6 0.0 collective-permute-start.14
  91.7 0.8 copy-done.3
  92.5 3.9 %collective-permute-start.13 = (bf16[4,560,128]{2,1,0:T(8,128)(2,1)}, bf16[4,560,128]{2,1,0:T(8,128)(2,1)}, u32[]{:S(2)}, u32[]{:S(2)}) collective-permute-start(bf16[4,560,128]{2,1,0:T(8,128)(2,1)} %collective-permute-done.6.refs_1_), channel_id=1, source_target_pairs={{0,1},{1,0},{2,3},{3,2},{4,5},{5,4},{6,7},{7,6},{8,9},{9,8},{10,11... | collective-permute-start | bytes 1720328 | tf_op jit(solution)/shard_map/ppermute | solution.py:242
  96.4 9.1 %collective-permute-done.9.refs_4_ = bf16[4,560,128]{2,1,0:T(8,128)(2,1)} collective-permute-done((bf16[4,560,128]{2,1,0:T(8,128)(2,1)}, bf16[4,560,128]{2,1,0:T(8,128)(2,1)}, u32[]{:S(2)}, u32[]{:S(2)}) %collective-permute-start.9) | collective-permute-done | bytes 573472 | tf_op jit(solution)/shard_map/ppermute | solution.py:242
  105.5 0.5 collective-permute-start.18
  106.0 0.8 copy-done.5
  106.8 0.0 collective-permute-start.17
  106.9 0.8 copy-done.7
  107.7 0.5 collective-permute-start.16
  108.2 0.9 shard_map.57
  109.1 8.4 %all-to-all-start.3 = ((bf16[32,64,128]{2,1,0:T(8,128)(2,1)}), bf16[32,64,128]{2,1,0:T(8,128)(2,1)S(1)}, u32[]{:S(2)}, u32[]{:S(2)}) async-start(bf16[32,64,128]{2,1,0:T(8,128)(2,1)} %bitcast.12), calls=%async_computation.3 | async-start | bytes 1048576 | tf_op jit(solution)/shard_map/all_to_all | solution.py:237
  117.6 0.3 reshape.20.g_ref
  117.9 0.1 pad_add_fusion.at_ref
  118.0 0.0 collective-permute-done.17.refs_12_
  118.0 11.1 %all-to-all-done.3 = bf16[32,64,128]{2,1,0:T(8,128)(2,1)S(1)} async-done(((bf16[32,64,128]{2,1,0:T(8,128)(2,1)}), bf16[32,64,128]{2,1,0:T(8,128)(2,1)S(1)}, u32[]{:S(2)}, u32[]{:S(2)}) %all-to-all-start.3) | async-done | bytes 524320 | tf_op jit(solution)/shard_map/all_to_all | solution.py:237
  129.2 1.1 copy-done.2
  130.2 1.1 copy-done.4
  131.3 1.1 copy-done.6
  132.3 1.1 copy-done.8
  133.4 15.0 %project.1 = bf16[2240,640]{1,0:T(8,128)(2,1)} custom-call(s32[3]{0:T(128)S(1)} %pad_add_fusion.at_ref, bf16[2240,640]{1,0:T(8,128)(2,1)} %bitcast.23, bf16[2048,128]{1,0:T(8,128)(2,1)S(1)} %bitcast.20, f32[2240,1]{1,0:T(8,128)S(1)} %reshape.20.g_ref, bf16[12,560,128]{2,1,0:T(8,128)(2,1)} %get-tuple-element.14.refs_0_, ...), custom_call_target="tpu_custom_call" | custom-call | flops 6422528000 | bytes 16056320 | tf_op jit(solution)/shard_map/project/pallas_call | solution.py:217
  (27 shorter events, 0.1 us)
Async XLA Ops:
  0.1 1.0 copy-start
  24.9 22.6 %collective-permute-start.5 = (bf16[560,128]{1,0:T(8,128)(2,1)S(1)}, bf16[560,128]{1,0:T(8,128)(2,1)S(1)}, u32[]{:S(2)}, u32[]{:S(2)}) collective-permute-start(bf16[560,128]{1,0:T(8,128)(2,1)S(1)} %get-tuple-element.13.refs_4_), channel_id=1, source_target_pairs={{0,6},{2,0},{4,2},{6,4},{1,7},{3,1},{5,3},{7,5},{8,14},{10,8},{12,... | collective-permute-start | bytes 430088 | tf_op jit(solution)/shard_map/ppermute | solution.py:242
  27.7 32.6 %collective-permute-start.2 = (bf16[2,560,128]{2,1,0:T(8,128)(2,1)S(1)}, bf16[2,560,128]{2,1,0:T(8,128)(2,1)S(1)}, u32[]{:S(2)}, u32[]{:S(2)}) collective-permute-start(bf16[2,560,128]{2,1,0:T(8,128)(2,1)S(1)} %get-tuple-element.12.refs_0_), channel_id=1, source_target_pairs={{0,192},{64,0},{128,64},{192,128},{1,193},{65,1},{129,65},{193,129... | collective-permute-start | bytes 860168 | tf_op jit(solution)/shard_map/ppermute | solution.py:242
  30.2 30.1 %collective-permute-start.1 = (bf16[2,560,128]{2,1,0:T(8,128)(2,1)S(1)}, bf16[2,560,128]{2,1,0:T(8,128)(2,1)S(1)}, u32[]{:S(2)}, u32[]{:S(2)}) collective-permute-start(bf16[2,560,128]{2,1,0:T(8,128)(2,1)S(1)} %get-tuple-element.12.refs_0_), channel_id=1, source_target_pairs={{0,128},{64,192},{128,0},{192,64},{1,129},{65,193},{129,1},{193,65... | collective-permute-start | bytes 860168 | tf_op jit(solution)/shard_map/ppermute | solution.py:242
  30.7 29.6 %collective-permute-start = (bf16[2,560,128]{2,1,0:T(8,128)(2,1)S(1)}, bf16[2,560,128]{2,1,0:T(8,128)(2,1)S(1)}, u32[]{:S(2)}, u32[]{:S(2)}) collective-permute-start(bf16[2,560,128]{2,1,0:T(8,128)(2,1)S(1)} %get-tuple-element.12.refs_0_), channel_id=1, source_target_pairs={{0,64},{64,128},{128,192},{192,0},{1,65},{65,129},{129,193},{193,1... | collective-permute-start | bytes 860168 | tf_op jit(solution)/shard_map/ppermute | solution.py:242
  37.1 30.4 %all-to-all-start.1 = ((bf16[32,64,128]{2,1,0:T(8,128)(2,1)}), bf16[32,64,128]{2,1,0:T(8,128)(2,1)S(1)}, u32[]{:S(2)}, u32[]{:S(2)}) async-start(bf16[32,64,128]{2,1,0:T(8,128)(2,1)} %bitcast.11), calls=%async_computation.1 | async-start | bytes 1048576 | tf_op jit(solution)/shard_map/all_to_all | solution.py:237
  44.5 73.1 %copy-start.9 = (f32[2240]{0:T(1024)S(1)}, f32[2240]{0:T(1024)}, u32[]{:S(2)}) copy-start(f32[2240]{0:T(1024)} %param.8) | copy-start | bytes 26884
  44.5 12.3 %collective-permute-start.4 = (bf16[560,128]{1,0:T(8,128)(2,1)S(1)}, bf16[560,128]{1,0:T(8,128)(2,1)S(1)}, u32[]{:S(2)}, u32[]{:S(2)}) collective-permute-start(bf16[560,128]{1,0:T(8,128)(2,1)S(1)} %get-tuple-element.13.refs_4_), channel_id=1, source_target_pairs={{0,4},{2,6},{4,0},{6,2},{1,5},{3,7},{5,1},{7,3},{8,12},{10,14},{12... | collective-permute-start | bytes 430088 | tf_op jit(solution)/shard_map/ppermute | solution.py:242
  47.5 12.8 %collective-permute-start.3 = (bf16[560,128]{1,0:T(8,128)(2,1)S(1)}, bf16[560,128]{1,0:T(8,128)(2,1)S(1)}, u32[]{:S(2)}, u32[]{:S(2)}) collective-permute-start(bf16[560,128]{1,0:T(8,128)(2,1)S(1)} %get-tuple-element.13.refs_4_), channel_id=1, source_target_pairs={{0,2},{2,4},{4,6},{6,0},{1,3},{3,5},{5,7},{7,1},{8,10},{10,12},{12... | collective-permute-start | bytes 430088 | tf_op jit(solution)/shard_map/ppermute | solution.py:242
  62.1 14.4 %collective-permute-start.8 = (bf16[4,560,128]{2,1,0:T(8,128)(2,1)}, bf16[4,560,128]{2,1,0:T(8,128)(2,1)S(1)}, u32[]{:S(2)}, u32[]{:S(2)}) collective-permute-start(bf16[4,560,128]{2,1,0:T(8,128)(2,1)} %get-tuple-element.15), channel_id=1, source_target_pairs={{0,6},{2,0},{4,2},{6,4},{1,7},{3,1},{5,3},{7,5},{8,14},{10,8},{12,... | collective-permute-start | bytes 1720328 | tf_op jit(solution)/shard_map/ppermute | solution.py:242
  62.1 16.8 %collective-permute-start.7 = (bf16[4,560,128]{2,1,0:T(8,128)(2,1)}, bf16[4,560,128]{2,1,0:T(8,128)(2,1)S(1)}, u32[]{:S(2)}, u32[]{:S(2)}) collective-permute-start(bf16[4,560,128]{2,1,0:T(8,128)(2,1)} %get-tuple-element.15), channel_id=1, source_target_pairs={{0,4},{2,6},{4,0},{6,2},{1,5},{3,7},{5,1},{7,3},{8,12},{10,14},{12... | collective-permute-start | bytes 1720328 | tf_op jit(solution)/shard_map/ppermute | solution.py:242
  63.5 27.7 %collective-permute-start.6 = (bf16[4,560,128]{2,1,0:T(8,128)(2,1)}, bf16[4,560,128]{2,1,0:T(8,128)(2,1)}, u32[]{:S(2)}, u32[]{:S(2)}) collective-permute-start(bf16[4,560,128]{2,1,0:T(8,128)(2,1)} %get-tuple-element.15), channel_id=1, source_target_pairs={{0,2},{2,4},{4,6},{6,0},{1,3},{3,5},{5,7},{7,1},{8,10},{10,12},{12... | collective-permute-start | bytes 1720328 | tf_op jit(solution)/shard_map/ppermute | solution.py:242
  63.6 28.0 %collective-permute-start.11 = (bf16[4,560,128]{2,1,0:T(8,128)(2,1)}, bf16[4,560,128]{2,1,0:T(8,128)(2,1)}, u32[]{:S(2)}, u32[]{:S(2)}) collective-permute-start(bf16[4,560,128]{2,1,0:T(8,128)(2,1)} %get-tuple-element.16), channel_id=1, source_target_pairs={{0,192},{64,0},{128,64},{192,128},{1,193},{65,1},{129,65},{193,129... | collective-permute-start | bytes 1720328 | tf_op jit(solution)/shard_map/ppermute | solution.py:242
  65.8 63.3 %collective-permute-start.12 = (bf16[12,560,128]{2,1,0:T(8,128)(2,1)}, bf16[12,560,128]{2,1,0:T(8,128)(2,1)S(1)}, u32[]{:S(2)}, u32[]{:S(2)}) collective-permute-start(bf16[12,560,128]{2,1,0:T(8,128)(2,1)} %get-tuple-element.14.refs_0_), channel_id=1, source_target_pairs={{0,1},{1,0},{2,3},{3,2},{4,5},{5,4},{6,7},{7,6},{8,9},{9,8},{10,11... | collective-permute-start | bytes 5160968 | tf_op jit(solution)/shard_map/ppermute | solution.py:242
  68.4 39.8 %all-to-all-start.2 = ((bf16[8,4,64,128]{3,2,1,0:T(8,128)(2,1)}), bf16[8,4,64,128]{3,2,1,0:T(8,128)(2,1)S(1)}, u32[]{:S(2)}, u32[]{:S(2)}) async-start(bf16[8,4,64,128]{3,2,1,0:T(8,128)(2,1)} %shard_map.56), calls=%async_computation.2 | async-start | bytes 1048576 | tf_op jit(solution)/shard_map/all_to_all | solution.py:237
  76.5 41.1 %copy-start.1 = (bf16[4,560,128]{2,1,0:T(8,128)(2,1)}, bf16[4,560,128]{2,1,0:T(8,128)(2,1)S(1)}, u32[]{:S(2)}) copy-start(bf16[4,560,128]{2,1,0:T(8,128)(2,1)S(1)} %collective-permute-done.8.refs_3_) | copy-start | bytes 1720324
  76.5 16.0 %collective-permute-start.10 = (bf16[4,560,128]{2,1,0:T(8,128)(2,1)}, bf16[4,560,128]{2,1,0:T(8,128)(2,1)}, u32[]{:S(2)}, u32[]{:S(2)}) collective-permute-start(bf16[4,560,128]{2,1,0:T(8,128)(2,1)} %get-tuple-element.16), channel_id=1, source_target_pairs={{0,128},{64,192},{128,0},{192,64},{1,129},{65,193},{129,1},{193,65... | collective-permute-start | bytes 1720328 | tf_op jit(solution)/shard_map/ppermute | solution.py:242
  78.9 26.6 %collective-permute-start.9 = (bf16[4,560,128]{2,1,0:T(8,128)(2,1)}, bf16[4,560,128]{2,1,0:T(8,128)(2,1)}, u32[]{:S(2)}, u32[]{:S(2)}) collective-permute-start(bf16[4,560,128]{2,1,0:T(8,128)(2,1)} %get-tuple-element.16), channel_id=1, source_target_pairs={{0,64},{64,128},{128,192},{192,0},{1,65},{65,129},{129,193},{193,1... | collective-permute-start | bytes 1720328 | tf_op jit(solution)/shard_map/ppermute | solution.py:242
  91.1 14.9 %collective-permute-start.15 = (bf16[4,560,128]{2,1,0:T(8,128)(2,1)S(1)}, bf16[4,560,128]{2,1,0:T(8,128)(2,1)S(1)}, u32[]{:S(2)}, u32[]{:S(2)}) collective-permute-start(bf16[4,560,128]{2,1,0:T(8,128)(2,1)S(1)} %collective-permute-done.8.refs_3_), channel_id=1, source_target_pairs={{0,1},{1,0},{2,3},{3,2},{4,5},{5,4},{6,7},{7,6},{8,9},{9,8},{10,11... | collective-permute-start | bytes 1720328 | tf_op jit(solution)/shard_map/ppermute | solution.py:242
  91.6 15.2 %collective-permute-start.14 = (bf16[4,560,128]{2,1,0:T(8,128)(2,1)S(1)}, bf16[4,560,128]{2,1,0:T(8,128)(2,1)S(1)}, u32[]{:S(2)}, u32[]{:S(2)}) collective-permute-start(bf16[4,560,128]{2,1,0:T(8,128)(2,1)S(1)} %collective-permute-done.7.refs_2_), channel_id=1, source_target_pairs={{0,1},{1,0},{2,3},{3,2},{4,5},{5,4},{6,7},{7,6},{8,9},{9,8},{10,11... | collective-permute-start | bytes 1720328 | tf_op jit(solution)/shard_map/ppermute | solution.py:242
  91.7 0.8 copy-start.3
  92.5 25.5 %collective-permute-start.13 = (bf16[4,560,128]{2,1,0:T(8,128)(2,1)}, bf16[4,560,128]{2,1,0:T(8,128)(2,1)}, u32[]{:S(2)}, u32[]{:S(2)}) collective-permute-start(bf16[4,560,128]{2,1,0:T(8,128)(2,1)} %collective-permute-done.6.refs_1_), channel_id=1, source_target_pairs={{0,1},{1,0},{2,3},{3,2},{4,5},{5,4},{6,7},{7,6},{8,9},{9,8},{10,11... | collective-permute-start | bytes 1720328 | tf_op jit(solution)/shard_map/ppermute | solution.py:242
  105.5 12.5 %collective-permute-start.18 = (bf16[4,560,128]{2,1,0:T(8,128)(2,1)}, bf16[4,560,128]{2,1,0:T(8,128)(2,1)}, u32[]{:S(2)}, u32[]{:S(2)}) collective-permute-start(bf16[4,560,128]{2,1,0:T(8,128)(2,1)} %collective-permute-done.11.refs_6_), channel_id=1, source_target_pairs={{0,1},{1,0},{2,3},{3,2},{4,5},{5,4},{6,7},{7,6},{8,9},{9,8},{10,11... | collective-permute-start | bytes 1720328 | tf_op jit(solution)/shard_map/ppermute | solution.py:242
  106.0 0.8 copy-start.5
  106.8 11.2 %collective-permute-start.17 = (bf16[4,560,128]{2,1,0:T(8,128)(2,1)}, bf16[4,560,128]{2,1,0:T(8,128)(2,1)}, u32[]{:S(2)}, u32[]{:S(2)}) collective-permute-start(bf16[4,560,128]{2,1,0:T(8,128)(2,1)} %collective-permute-done.10.refs_5_), channel_id=1, source_target_pairs={{0,1},{1,0},{2,3},{3,2},{4,5},{5,4},{6,7},{7,6},{8,9},{9,8},{10,11... | collective-permute-start | bytes 1720328 | tf_op jit(solution)/shard_map/ppermute | solution.py:242
  106.9 0.9 copy-start.7
  107.7 10.3 %collective-permute-start.16 = (bf16[4,560,128]{2,1,0:T(8,128)(2,1)}, bf16[4,560,128]{2,1,0:T(8,128)(2,1)}, u32[]{:S(2)}, u32[]{:S(2)}) collective-permute-start(bf16[4,560,128]{2,1,0:T(8,128)(2,1)} %collective-permute-done.9.refs_4_), channel_id=1, source_target_pairs={{0,1},{1,0},{2,3},{3,2},{4,5},{5,4},{6,7},{7,6},{8,9},{9,8},{10,11... | collective-permute-start | bytes 1720328 | tf_op jit(solution)/shard_map/ppermute | solution.py:242
  109.1 20.1 %all-to-all-start.3 = ((bf16[32,64,128]{2,1,0:T(8,128)(2,1)}), bf16[32,64,128]{2,1,0:T(8,128)(2,1)S(1)}, u32[]{:S(2)}, u32[]{:S(2)}) async-start(bf16[32,64,128]{2,1,0:T(8,128)(2,1)} %bitcast.12), calls=%async_computation.3 | async-start | bytes 1048576 | tf_op jit(solution)/shard_map/all_to_all | solution.py:237
  129.2 1.1 copy-start.2
  130.2 1.1 copy-start.4
  131.3 1.1 copy-start.6
  132.3 1.1 copy-start.8

commit v2 on v1

--- a/solution.py
+++ b/solution.py
@@ -131,28 +131,28 @@
         o_ref[t, :, 256:] = rest
 
 
-def compact_kernel(w_ref, x_ref, y_ref, rows_ref):
+def compact_kernel(w_ref, x_ref, y_ref, r_ref, rows_ref):
     rows = w_ref.shape[1]
     for t in range(NZ):
         rows_ref[pl.ds(t * rows, rows), :] = w_ref[t].astype(f32)
     slab = rows_ref[...].astype(bf16)
-    x_ref[0] = slab[:, :128]
-    x_ref[1] = slab[:, 256:]
+    x_ref[...] = slab[:, :128]
     y_ref[...] = slab[:, 128:256]
+    r_ref[...] = slab[:, 256:]
 
 
 def stack_kernel(*refs):
-    by_x, by_y, (main_x, main_y, every) = refs[:4], refs[4:8], refs[8:]
+    by_x, by_y, rest, (main_x, main_y, every) = refs[:4], refs[4:8], refs[8], refs[9:]
     for k in range(4):
-        main_x[k] = by_x[k][0]
+        main_x[k] = by_x[k][...]
         main_y[k] = by_y[k][...]
-        every[k] = by_x[k][1]
-        every[4 + k] = by_x[k][0]
-        every[8 + k] = by_y[k][...]
+        every[k] = by_x[k][...]
+        every[4 + k] = by_y[k][...]
+    every[8] = rest[...]
 
 
 def project_kernel(at_ref, q_ref, p_ref, g_ref, *refs):
-    parts, (o_ref, w_ref, mixed_ref, normed_ref, sem) = refs[:14], refs[14:]
+    parts, (o_ref, w_ref, mixed_ref, normed_ref, sem) = refs[:20], refs[20:]
     x, y, core = at_ref[0], at_ref[1], at_ref[2]
     copies = []
 
@@ -164,12 +164,13 @@
 
     for side in range(NC):
         which = core if side == 0 else 1 - core
-        every, *rest = parts[7 * side : 7 * side + 7]
-        by_y, by_x = (every.at[pl.ds(4, 4)], *rest[:3]), (every.at[pl.ds(8, 4)], *rest[3:])
+        every, *rest = parts[10 * side : 10 * side + 10]
+        by_y, by_x = (every.at[pl.ds(0, 4)], *rest[:3]), (every.at[pl.ds(4, 4)], *rest[3:6])
+        edges = (every.at[8], *rest[6:])
         for k in range(4):
             block = lax.rem(x - k + NX, NX)
             column = which * 1024 + lax.rem(y - k + NY, NY) * 256
-            fetch(every.at[k], block, 2048 + which * 128)
+            fetch(edges[k], block, 2048 + which * 128)
             for n in range(4):
                 turn = lax.rem(y - n + NY, NY)
                 fetch(by_y[n].at[k], block, which * 1024 + turn * 256)
@@ -216,7 +217,7 @@
     anyw = pl.BlockSpec(memory_space=pl.ANY)
     return pl.pallas_call(
         project_kernel,
-        in_specs=[pl.BlockSpec(memory_space=pltpu.SMEM), vmem, vmem, vmem] + [anyw] * 14,
+        in_specs=[pl.BlockSpec(memory_space=pltpu.SMEM), vmem, vmem, vmem] + [anyw] * 20,
         out_specs=vmem,
         out_shape=jax.ShapeDtypeStruct((D, tokens), bf16),
         scratch_shapes=[
@@ -262,9 +263,9 @@
     k_t, v_t = (pltpu.with_memory_space_constraint(a, pltpu.HBM) for a in (k_t, v_t))
     st = after(states(k_t, v_t), w_z)
     r1 = swap(st.reshape(32, PART, PAD), PIECES)
-    x0, y0 = small_call(
+    x0, y0, r0 = small_call(
         compact_kernel,
-        (jax.ShapeDtypeStruct((2, ROWS_X, 128), bf16), jax.ShapeDtypeStruct((ROWS_X, 128), bf16)),
+        (jax.ShapeDtypeStruct((ROWS_X, 128), bf16),) * 3,
         (),
         (w_z,),
         (pltpu.VMEM((NZ * rows, 384), f32),),
@@ -276,11 +277,11 @@
     four = jax.ShapeDtypeStruct((4, ROWS_X, 128), bf16)
     main_x, main_y, every = small_call(
         stack_kernel,
-        (four, four, jax.ShapeDtypeStruct((12, ROWS_X, 128), bf16)),
+        (four, four, jax.ShapeDtypeStruct((9, ROWS_X, 128), bf16)),
         (),
-        (*by_x, *by_y),
+        (*by_x, *by_y, r0),
     )
-    parts = [every, *shifted(main_x, "y"), *shifted(main_y, "x")]
+    parts = [every, *shifted(main_x, "y"), *shifted(main_y, "x"), *shifted(r0, "x")]
     r3 = small_call(prefix_kernel, jax.ShapeDtypeStruct((NX, 8, PART, PAD), bf16), (), (r2s,))
     prefix = swap(r3.reshape(32, PART, PAD), PIECES).reshape(2048, PAD)
     parts += [moved(part, "core", 1) for part in parts]

time: 149 us -> 149 us (level)
  waiting for transfers between devices: 49.4 us -> 43.8 us
  local copies, waits for them, and re-layouts: 8.04 us -> 12.6 us
    ppermute x19 -> x25, waiting for transfers between devices: 38.3 us -> 32.7 us  [moved(): return lax.ppermute(value, axis, [(i, (i + step) % n) for i in range(n)])]
    unnamed x20 -> x36, local copies, waits for them, and re-layouts: 7.69 us -> 12.3 us
    ppermute x19 -> x25, starting transfers between devices: 23 us -> 27.6 us  [moved(): return lax.ppermute(value, axis, [(i, (i + step) % n) for i in range(n)])]
    all_to_all x3, starting transfers between devices: 19.4 us -> 16.1 us  [swap(): return lax.all_to_all(value, axes, split_axis=0, concat_axis=0, tiled=True)]
  transfers between devices with their start and end apart: 22 -> 28, of which waited for: 6 -> 7; matrix products, arithmetic and copies ran while one was open for 0% -> 0% of each run, Pallas kernels for 6% -> 6%
where the time goes in v2:
time: 149 us; the launch traced here: 148 us
  waiting for transfers between devices  43.8 us (29%)
  starting transfers between devices  43.7 us (29%)
  Pallas kernels  24.5 us (16%)
  blocking collectives  23.1 us (16%)
  local copies, waits for them, and re-layouts  12.6 us (8%)
    ppermute x25, waiting for transfers between devices, moved(): return lax.ppermute(value, axis, [(i, (i + step) % n) for i in range(n)])  32.7 us
    ppermute x25, starting transfers between devices, moved(): return lax.ppermute(value, axis, [(i, (i + step) % n) for i in range(n)])  27.6 us
    all_to_all x1, blocking collectives, swap(): return lax.all_to_all(value, axes, split_axis=0, concat_axis=0, tiled=True)  23.1 us
    all_to_all x3, starting transfers between devices, swap(): return lax.all_to_all(value, axes, split_axis=0, concat_axis=0, tiled=True)  16.1 us
    pallas_call x1, Pallas kernels, project(): pl.pallas_call(project_kernel, in_specs=[pl.BlockSpec(memory_space=pltpu....  15.1 us
    unnamed x36, local copies, waits for them, and re-layouts  12.3 us
    all_to_all x3, waiting for transfers between devices, swap(): return lax.all_to_all(value, axes, split_axis=0, concat_axis=0, tiled=True)  11.1 us
    pallas_call x1, Pallas kernels, states(): pl.pallas_call(state_kernel, grid=(HEADS // GROUP,), in_specs=[spec, spec...  5.79 us
  transfers between devices with their start and end apart: 28, of which 7 were waited for; matrix products, arithmetic and copies ran while one was open for 0% of the time, Pallas kernels for 6%

profile of v2, /device:TPU:1, one launch (start us, length us, event | category | flops | bytes accessed | tf_op | source)
XLA Modules:
  0.0 148.3 jit_solution(11661763359658226112)
XLA Ops:
  0.1 1.0 copy-done
  1.1 0.6 shard_map.55
  1.6 23.1 %all_to_all.20.w_ref = bf16[8,70,384]{2,1,0:T(8,128)(2,1)S(1)} all-to-all(bf16[8,70,384]{2,1,0:T(8,128)(2,1)S(1)} %shard_map.55), channel_id=1, replica_groups=mesh['x'=4,'z'=8,'y'=4,'core'=2] {'z'}, dimensions={0} | all-to-all | bytes 860160 | tf_op jit(solution)/shard_map/all_to_all | solution.py:238
  24.9 2.6 %collective-permute-start.2 = (bf16[560,128]{1,0:T(8,128)(2,1)S(1)}, bf16[560,128]{1,0:T(8,128)(2,1)S(1)}, u32[]{:S(2)}, u32[]{:S(2)}) collective-permute-start(bf16[560,128]{1,0:T(8,128)(2,1)S(1)} %get-tuple-element.13.refs_0_), channel_id=1, source_target_pairs={{0,192},{64,0},{128,64},{192,128},{1,193},{65,1},{129,65},{193,129... | collective-permute-start | bytes 430088 | tf_op jit(solution)/shard_map/ppermute | solution.py:243
  27.5 0.5 collective-permute-start.1
  28.0 0.6 collective-permute-start
  28.6 2.7 %collective-permute-start.5 = (bf16[560,128]{1,0:T(8,128)(2,1)S(1)}, bf16[560,128]{1,0:T(8,128)(2,1)S(1)}, u32[]{:S(2)}, u32[]{:S(2)}) collective-permute-start(bf16[560,128]{1,0:T(8,128)(2,1)S(1)} %get-tuple-element.14.refs_4_), channel_id=1, source_target_pairs={{0,6},{2,0},{4,2},{6,4},{1,7},{3,1},{5,3},{7,5},{8,14},{10,8},{12,... | collective-permute-start | bytes 430088 | tf_op jit(solution)/shard_map/ppermute | solution.py:243
  31.3 5.8 %states.1 = bf16[2048,128]{1,0:T(8,128)(2,1)} custom-call(bf16[2240,640]{1,0:T(8,128)(2,1)} %bitcast.21, bf16[2240,640]{1,0:T(8,128)(2,1)} %bitcast.22), custom_call_target="tpu_custom_call" | custom-call | flops 419430400 | bytes 5734400 | tf_op jit(solution)/shard_map/states/pallas_call | solution.py:68
  37.1 7.4 %all-to-all-start.1 = ((bf16[32,64,128]{2,1,0:T(8,128)(2,1)}), bf16[32,64,128]{2,1,0:T(8,128)(2,1)S(1)}, u32[]{:S(2)}, u32[]{:S(2)}) async-start(bf16[32,64,128]{2,1,0:T(8,128)(2,1)} %bitcast.11), calls=%async_computation.1 | async-start | bytes 1048576 | tf_op jit(solution)/shard_map/all_to_all | solution.py:238
  44.5 2.9 %collective-permute-start.4 = (bf16[560,128]{1,0:T(8,128)(2,1)S(1)}, bf16[560,128]{1,0:T(8,128)(2,1)S(1)}, u32[]{:S(2)}, u32[]{:S(2)}) collective-permute-start(bf16[560,128]{1,0:T(8,128)(2,1)S(1)} %get-tuple-element.14.refs_4_), channel_id=1, source_target_pairs={{0,4},{2,6},{4,0},{6,2},{1,5},{3,7},{5,1},{7,3},{8,12},{10,14},{12... | collective-permute-start | bytes 430088 | tf_op jit(solution)/shard_map/ppermute | solution.py:243
  47.8 2.5 %collective-permute-start.14 = (bf16[560,128]{1,0:T(8,128)(2,1)S(1)}, bf16[560,128]{1,0:T(8,128)(2,1)S(1)}, u32[]{:S(2)}, u32[]{:S(2)}) collective-permute-start(bf16[560,128]{1,0:T(8,128)(2,1)S(1)} %get-tuple-element.15.refs_8_), channel_id=1, source_target_pairs={{0,192},{64,0},{128,64},{192,128},{1,193},{65,1},{129,65},{193,129... | collective-permute-start | bytes 430088 | tf_op jit(solution)/shard_map/ppermute | solution.py:243
  50.3 0.5 collective-permute-start.13
  50.8 0.6 collective-permute-start.12
  51.4 5.5 %collective-permute-done.4.refs_6_ = bf16[560,128]{1,0:T(8,128)(2,1)S(1)} collective-permute-done((bf16[560,128]{1,0:T(8,128)(2,1)S(1)}, bf16[560,128]{1,0:T(8,128)(2,1)S(1)}, u32[]{:S(2)}, u32[]{:S(2)}) %collective-permute-start.4) | collective-permute-done | bytes 143392 | tf_op jit(solution)/shard_map/ppermute | solution.py:243
  56.8 3.5 %collective-permute-done.3.refs_5_ = bf16[560,128]{1,0:T(8,128)(2,1)S(1)} collective-permute-done((bf16[560,128]{1,0:T(8,128)(2,1)S(1)}, bf16[560,128]{1,0:T(8,128)(2,1)S(1)}, u32[]{:S(2)}, u32[]{:S(2)}) %collective-permute-start.3) | collective-permute-done | bytes 143392 | tf_op jit(solution)/shard_map/ppermute | solution.py:243
  60.4 1.2 shard_map.59
  61.5 1.3 collective-permute-start.7
  63.1 1.0 collective-permute-start.24
  64.1 2.4 %collective-permute-start.11 = (bf16[4,560,128]{2,1,0:T(8,128)(2,1)}, bf16[4,560,128]{2,1,0:T(8,128)(2,1)}, u32[]{:S(2)}, u32[]{:S(2)}) collective-permute-start(bf16[4,560,128]{2,1,0:T(8,128)(2,1)} %get-tuple-element.18), channel_id=1, source_target_pairs={{0,192},{64,0},{128,64},{192,128},{1,193},{65,1},{129,65},{193,129... | collective-permute-start | bytes 1720328 | tf_op jit(solution)/shard_map/ppermute | solution.py:243
  66.5 0.7 copy-done.11
  67.5 0.7 copy-done.9
  68.5 0.4 collective-permute-start.22
  68.9 0.9 shard_map.56
  69.8 3.5 %all-to-all-start.2 = ((bf16[8,4,64,128]{3,2,1,0:T(8,128)(2,1)}), bf16[8,4,64,128]{3,2,1,0:T(8,128)(2,1)S(1)}, u32[]{:S(2)}, u32[]{:S(2)}) async-start(bf16[8,4,64,128]{3,2,1,0:T(8,128)(2,1)} %shard_map.56), calls=%async_computation.2 | async-start | bytes 1048576 | tf_op jit(solution)/shard_map/all_to_all | solution.py:238
  73.4 0.6 copy-done.15
  74.1 1.9 %collective-permute-done.8.refs_3_ = bf16[4,560,128]{2,1,0:T(8,128)(2,1)S(1)} collective-permute-done((bf16[4,560,128]{2,1,0:T(8,128)(2,1)}, bf16[4,560,128]{2,1,0:T(8,128)(2,1)S(1)}, u32[]{:S(2)}, u32[]{:S(2)}) %collective-permute-start.8) | collective-permute-done | bytes 573472 | tf_op jit(solution)/shard_map/ppermute | solution.py:243
  76.0 2.2 %collective-permute-start.10 = (bf16[4,560,128]{2,1,0:T(8,128)(2,1)}, bf16[4,560,128]{2,1,0:T(8,128)(2,1)}, u32[]{:S(2)}, u32[]{:S(2)}) collective-permute-start(bf16[4,560,128]{2,1,0:T(8,128)(2,1)} %get-tuple-element.18), channel_id=1, source_target_pairs={{0,128},{64,192},{128,0},{192,64},{1,129},{65,193},{129,1},{193,65... | collective-permute-start | bytes 1720328 | tf_op jit(solution)/shard_map/ppermute | solution.py:243
  78.4 12.1 %collective-permute-done.6.refs_1_ = bf16[4,560,128]{2,1,0:T(8,128)(2,1)} collective-permute-done((bf16[4,560,128]{2,1,0:T(8,128)(2,1)}, bf16[4,560,128]{2,1,0:T(8,128)(2,1)}, u32[]{:S(2)}, u32[]{:S(2)}) %collective-permute-start.6) | collective-permute-done | bytes 573472 | tf_op jit(solution)/shard_map/ppermute | solution.py:243
  90.6 0.5 collective-permute-start.18
  91.1 1.3 collective-permute-start.17
  92.3 3.4 %collective-permute-start.16 = (bf16[4,560,128]{2,1,0:T(8,128)(2,1)}, bf16[4,560,128]{2,1,0:T(8,128)(2,1)}, u32[]{:S(2)}, u32[]{:S(2)}) collective-permute-start(bf16[4,560,128]{2,1,0:T(8,128)(2,1)} %collective-permute-done.6.refs_1_), channel_id=1, source_target_pairs={{0,1},{1,0},{2,3},{3,2},{4,5},{5,4},{6,7},{7,6},{8,9},{9,8},{10,11... | collective-permute-start | bytes 1720328 | tf_op jit(solution)/shard_map/ppermute | solution.py:243
  95.7 9.3 %collective-permute-done.9.refs_4_ = bf16[4,560,128]{2,1,0:T(8,128)(2,1)} collective-permute-done((bf16[4,560,128]{2,1,0:T(8,128)(2,1)}, bf16[4,560,128]{2,1,0:T(8,128)(2,1)}, u32[]{:S(2)}, u32[]{:S(2)}) %collective-permute-start.9) | collective-permute-done | bytes 573472 | tf_op jit(solution)/shard_map/ppermute | solution.py:243
  105.0 0.5 collective-permute-start.21
  105.5 0.8 copy-done.3
  106.4 0.8 copy-done.5
  107.2 0.5 collective-permute-start.19
  107.7 0.9 shard_map.57
  108.5 5.2 %all-to-all-start.3 = ((bf16[32,64,128]{2,1,0:T(8,128)(2,1)}), bf16[32,64,128]{2,1,0:T(8,128)(2,1)S(1)}, u32[]{:S(2)}, u32[]{:S(2)}) async-start(bf16[32,64,128]{2,1,0:T(8,128)(2,1)} %bitcast.12), calls=%async_computation.3 | async-start | bytes 1048576 | tf_op jit(solution)/shard_map/all_to_all | solution.py:238
  114.3 11.1 %all-to-all-done.3 = bf16[32,64,128]{2,1,0:T(8,128)(2,1)S(1)} async-done(((bf16[32,64,128]{2,1,0:T(8,128)(2,1)}), bf16[32,64,128]{2,1,0:T(8,128)(2,1)S(1)}, u32[]{:S(2)}, u32[]{:S(2)}) %all-to-all-start.3) | async-done | bytes 524320 | tf_op jit(solution)/shard_map/all_to_all | solution.py:238
  125.4 1.1 copy-done.2
  126.4 1.1 copy-done.4
  127.5 1.1 copy-done.6
  128.5 0.9 copy-done.8
  129.5 0.9 copy-done.10
  130.4 0.9 copy-done.12
  131.3 0.9 copy-done.14
  132.2 0.9 copy-done.16
  133.1 15.1 %project.1 = bf16[2240,640]{1,0:T(8,128)(2,1)} custom-call(s32[3]{0:T(128)S(1)} %pad_add_fusion.at_ref, bf16[2240,640]{1,0:T(8,128)(2,1)} %bitcast.23, bf16[2048,128]{1,0:T(8,128)(2,1)S(1)} %bitcast.20, f32[2240,1]{1,0:T(8,128)S(1)} %reshape.20.g_ref, bf16[9,560,128]{2,1,0:T(8,128)(2,1)S(1)} %get-tuple-element.16.refs_0_, ...), custom_call_target="tpu_custom_call" | custom-call | flops 6422528000 | bytes 16056320 | tf_op jit(solution)/shard_map/project/pallas_call | solution.py:218
  (55 shorter events, 2.3 us)
Async XLA Ops:
  0.1 1.0 copy-start
  24.9 22.6 %collective-permute-start.2 = (bf16[560,128]{1,0:T(8,128)(2,1)S(1)}, bf16[560,128]{1,0:T(8,128)(2,1)S(1)}, u32[]{:S(2)}, u32[]{:S(2)}) collective-permute-start(bf16[560,128]{1,0:T(8,128)(2,1)S(1)} %get-tuple-element.13.refs_0_), channel_id=1, source_target_pairs={{0,192},{64,0},{128,64},{192,128},{1,193},{65,1},{129,65},{193,129... | collective-permute-start | bytes 430088 | tf_op jit(solution)/shard_map/ppermute | solution.py:243
  27.5 20.3 %collective-permute-start.1 = (bf16[560,128]{1,0:T(8,128)(2,1)S(1)}, bf16[560,128]{1,0:T(8,128)(2,1)S(1)}, u32[]{:S(2)}, u32[]{:S(2)}) collective-permute-start(bf16[560,128]{1,0:T(8,128)(2,1)S(1)} %get-tuple-element.13.refs_0_), channel_id=1, source_target_pairs={{0,128},{64,192},{128,0},{192,64},{1,129},{65,193},{129,1},{193,65... | collective-permute-start | bytes 430088 | tf_op jit(solution)/shard_map/ppermute | solution.py:243
  28.0 22.3 %collective-permute-start = (bf16[560,128]{1,0:T(8,128)(2,1)S(1)}, bf16[560,128]{1,0:T(8,128)(2,1)S(1)}, u32[]{:S(2)}, u32[]{:S(2)}) collective-permute-start(bf16[560,128]{1,0:T(8,128)(2,1)S(1)} %get-tuple-element.13.refs_0_), channel_id=1, source_target_pairs={{0,64},{64,128},{128,192},{192,0},{1,65},{65,129},{129,193},{193,1... | collective-permute-start | bytes 430088 | tf_op jit(solution)/shard_map/ppermute | solution.py:243
  28.6 22.2 %collective-permute-start.5 = (bf16[560,128]{1,0:T(8,128)(2,1)S(1)}, bf16[560,128]{1,0:T(8,128)(2,1)S(1)}, u32[]{:S(2)}, u32[]{:S(2)}) collective-permute-start(bf16[560,128]{1,0:T(8,128)(2,1)S(1)} %get-tuple-element.14.refs_4_), channel_id=1, source_target_pairs={{0,6},{2,0},{4,2},{6,4},{1,7},{3,1},{5,3},{7,5},{8,14},{10,8},{12,... | collective-permute-start | bytes 430088 | tf_op jit(solution)/shard_map/ppermute | solution.py:243
  37.1 31.8 %all-to-all-start.1 = ((bf16[32,64,128]{2,1,0:T(8,128)(2,1)}), bf16[32,64,128]{2,1,0:T(8,128)(2,1)S(1)}, u32[]{:S(2)}, u32[]{:S(2)}) async-start(bf16[32,64,128]{2,1,0:T(8,128)(2,1)} %bitcast.11), calls=%async_computation.1 | async-start | bytes 1048576 | tf_op jit(solution)/shard_map/all_to_all | solution.py:238
  44.5 69.3 %copy-start.17 = (f32[2240]{0:T(1024)S(1)}, f32[2240]{0:T(1024)}, u32[]{:S(2)}) copy-start(f32[2240]{0:T(1024)} %param.8) | copy-start | bytes 26884
  44.5 12.3 %collective-permute-start.4 = (bf16[560,128]{1,0:T(8,128)(2,1)S(1)}, bf16[560,128]{1,0:T(8,128)(2,1)S(1)}, u32[]{:S(2)}, u32[]{:S(2)}) collective-permute-start(bf16[560,128]{1,0:T(8,128)(2,1)S(1)} %get-tuple-element.14.refs_4_), channel_id=1, source_target_pairs={{0,4},{2,6},{4,0},{6,2},{1,5},{3,7},{5,1},{7,3},{8,12},{10,14},{12... | collective-permute-start | bytes 430088 | tf_op jit(solution)/shard_map/ppermute | solution.py:243
  47.5 12.9 %collective-permute-start.3 = (bf16[560,128]{1,0:T(8,128)(2,1)S(1)}, bf16[560,128]{1,0:T(8,128)(2,1)S(1)}, u32[]{:S(2)}, u32[]{:S(2)}) collective-permute-start(bf16[560,128]{1,0:T(8,128)(2,1)S(1)} %get-tuple-element.14.refs_4_), channel_id=1, source_target_pairs={{0,2},{2,4},{4,6},{6,0},{1,3},{3,5},{5,7},{7,1},{8,10},{10,12},{12... | collective-permute-start | bytes 430088 | tf_op jit(solution)/shard_map/ppermute | solution.py:243
  47.8 15.1 %collective-permute-start.14 = (bf16[560,128]{1,0:T(8,128)(2,1)S(1)}, bf16[560,128]{1,0:T(8,128)(2,1)S(1)}, u32[]{:S(2)}, u32[]{:S(2)}) collective-permute-start(bf16[560,128]{1,0:T(8,128)(2,1)S(1)} %get-tuple-element.15.refs_8_), channel_id=1, source_target_pairs={{0,192},{64,0},{128,64},{192,128},{1,193},{65,1},{129,65},{193,129... | collective-permute-start | bytes 430088 | tf_op jit(solution)/shard_map/ppermute | solution.py:243
  50.3 12.8 %collective-permute-start.13 = (bf16[560,128]{1,0:T(8,128)(2,1)S(1)}, bf16[560,128]{1,0:T(8,128)(2,1)S(1)}, u32[]{:S(2)}, u32[]{:S(2)}) collective-permute-start(bf16[560,128]{1,0:T(8,128)(2,1)S(1)} %get-tuple-element.15.refs_8_), channel_id=1, source_target_pairs={{0,128},{64,192},{128,0},{192,64},{1,129},{65,193},{129,1},{193,65... | collective-permute-start | bytes 430088 | tf_op jit(solution)/shard_map/ppermute | solution.py:243
  50.8 13.3 %collective-permute-start.12 = (bf16[560,128]{1,0:T(8,128)(2,1)S(1)}, bf16[560,128]{1,0:T(8,128)(2,1)}, u32[]{:S(2)}, u32[]{:S(2)}) collective-permute-start(bf16[560,128]{1,0:T(8,128)(2,1)S(1)} %get-tuple-element.15.refs_8_), channel_id=1, source_target_pairs={{0,64},{64,128},{128,192},{192,0},{1,65},{65,129},{129,193},{193,1... | collective-permute-start | bytes 430088 | tf_op jit(solution)/shard_map/ppermute | solution.py:243
  61.5 14.5 %collective-permute-start.8 = (bf16[4,560,128]{2,1,0:T(8,128)(2,1)}, bf16[4,560,128]{2,1,0:T(8,128)(2,1)S(1)}, u32[]{:S(2)}, u32[]{:S(2)}) collective-permute-start(bf16[4,560,128]{2,1,0:T(8,128)(2,1)} %get-tuple-element.17), channel_id=1, source_target_pairs={{0,6},{2,0},{4,2},{6,4},{1,7},{3,1},{5,3},{7,5},{8,14},{10,8},{12,... | collective-permute-start | bytes 1720328 | tf_op jit(solution)/shard_map/ppermute | solution.py:243
  61.5 16.7 %collective-permute-start.7 = (bf16[4,560,128]{2,1,0:T(8,128)(2,1)}, bf16[4,560,128]{2,1,0:T(8,128)(2,1)S(1)}, u32[]{:S(2)}, u32[]{:S(2)}) collective-permute-start(bf16[4,560,128]{2,1,0:T(8,128)(2,1)} %get-tuple-element.17), channel_id=1, source_target_pairs={{0,4},{2,6},{4,0},{6,2},{1,5},{3,7},{5,1},{7,3},{8,12},{10,14},{12... | collective-permute-start | bytes 1720328 | tf_op jit(solution)/shard_map/ppermute | solution.py:243
  62.9 45.7 %copy-start.7 = (bf16[560,128]{1,0:T(8,128)(2,1)}, bf16[560,128]{1,0:T(8,128)(2,1)S(1)}, u32[]{:S(2)}) copy-start(bf16[560,128]{1,0:T(8,128)(2,1)S(1)} %collective-permute-done.14.refs_9_) | copy-start | bytes 430084
  62.9 27.7 %collective-permute-start.6 = (bf16[4,560,128]{2,1,0:T(8,128)(2,1)}, bf16[4,560,128]{2,1,0:T(8,128)(2,1)}, u32[]{:S(2)}, u32[]{:S(2)}) collective-permute-start(bf16[4,560,128]{2,1,0:T(8,128)(2,1)} %get-tuple-element.17), channel_id=1, source_target_pairs={{0,2},{2,4},{4,6},{6,0},{1,3},{3,5},{5,7},{7,1},{8,10},{10,12},{12... | collective-permute-start | bytes 1720328 | tf_op jit(solution)/shard_map/ppermute | solution.py:243
  63.1 3.4 %collective-permute-start.24 = (bf16[560,128]{1,0:T(8,128)(2,1)S(1)}, bf16[560,128]{1,0:T(8,128)(2,1)S(1)}, u32[]{:S(2)}, u32[]{:S(2)}) collective-permute-start(bf16[560,128]{1,0:T(8,128)(2,1)S(1)} %collective-permute-done.14.refs_9_), channel_id=1, source_target_pairs={{0,1},{1,0},{2,3},{3,2},{4,5},{5,4},{6,7},{7,6},{8,9},{9,8},{10,11... | collective-permute-start | bytes 430088 | tf_op jit(solution)/shard_map/ppermute | solution.py:243
  64.1 27.0 %collective-permute-start.11 = (bf16[4,560,128]{2,1,0:T(8,128)(2,1)}, bf16[4,560,128]{2,1,0:T(8,128)(2,1)}, u32[]{:S(2)}, u32[]{:S(2)}) collective-permute-start(bf16[4,560,128]{2,1,0:T(8,128)(2,1)} %get-tuple-element.18), channel_id=1, source_target_pairs={{0,192},{64,0},{128,64},{192,128},{1,193},{65,1},{129,65},{193,129... | collective-permute-start | bytes 1720328 | tf_op jit(solution)/shard_map/ppermute | solution.py:243
  66.5 0.7 copy-start.11
  67.2 1.4 collective-permute-start.23
  67.5 0.7 copy-start.9
  68.5 45.3 %copy-start.13 = (bf16[560,128]{1,0:T(8,128)(2,1)}, bf16[560,128]{1,0:T(8,128)(2,1)S(1)}, u32[]{:S(2)}) copy-start(bf16[560,128]{1,0:T(8,128)(2,1)S(1)} %collective-permute-done.23.refs_18_) | copy-start | bytes 430084
  68.5 4.8 %collective-permute-start.22 = (bf16[560,128]{1,0:T(8,128)(2,1)}, bf16[560,128]{1,0:T(8,128)(2,1)S(1)}, u32[]{:S(2)}, u32[]{:S(2)}) collective-permute-start(bf16[560,128]{1,0:T(8,128)(2,1)} %collective-permute-done.12.refs_7_), channel_id=1, source_target_pairs={{0,1},{1,0},{2,3},{3,2},{4,5},{5,4},{6,7},{7,6},{8,9},{9,8},{10,11... | collective-permute-start | bytes 430088 | tf_op jit(solution)/shard_map/ppermute | solution.py:243
  69.8 37.8 %all-to-all-start.2 = ((bf16[8,4,64,128]{3,2,1,0:T(8,128)(2,1)}), bf16[8,4,64,128]{3,2,1,0:T(8,128)(2,1)S(1)}, u32[]{:S(2)}, u32[]{:S(2)}) async-start(bf16[8,4,64,128]{3,2,1,0:T(8,128)(2,1)} %shard_map.56), calls=%async_computation.2 | async-start | bytes 1048576 | tf_op jit(solution)/shard_map/all_to_all | solution.py:238
  73.3 0.7 copy-start.15
  74.0 40.3 %collective-permute-start.15 = (bf16[9,560,128]{2,1,0:T(8,128)(2,1)S(1)}, bf16[9,560,128]{2,1,0:T(8,128)(2,1)}, u32[]{:S(2)}, u32[]{:S(2)}) collective-permute-start(bf16[9,560,128]{2,1,0:T(8,128)(2,1)S(1)} %get-tuple-element.16.refs_0_), channel_id=1, source_target_pairs={{0,1},{1,0},{2,3},{3,2},{4,5},{5,4},{6,7},{7,6},{8,9},{9,8},{10,11... | collective-permute-start | bytes 3870728 | tf_op jit(solution)/shard_map/ppermute | solution.py:243
  76.0 16.3 %collective-permute-start.10 = (bf16[4,560,128]{2,1,0:T(8,128)(2,1)}, bf16[4,560,128]{2,1,0:T(8,128)(2,1)}, u32[]{:S(2)}, u32[]{:S(2)}) collective-permute-start(bf16[4,560,128]{2,1,0:T(8,128)(2,1)} %get-tuple-element.18), channel_id=1, source_target_pairs={{0,128},{64,192},{128,0},{192,64},{1,129},{65,193},{129,1},{193,65... | collective-permute-start | bytes 1720328 | tf_op jit(solution)/shard_map/ppermute | solution.py:243
  78.2 30.3 %copy-start.1 = (bf16[4,560,128]{2,1,0:T(8,128)(2,1)}, bf16[4,560,128]{2,1,0:T(8,128)(2,1)S(1)}, u32[]{:S(2)}) copy-start(bf16[4,560,128]{2,1,0:T(8,128)(2,1)S(1)} %collective-permute-done.7.refs_2_) | copy-start | bytes 1720324
  78.2 26.8 %collective-permute-start.9 = (bf16[4,560,128]{2,1,0:T(8,128)(2,1)}, bf16[4,560,128]{2,1,0:T(8,128)(2,1)}, u32[]{:S(2)}, u32[]{:S(2)}) collective-permute-start(bf16[4,560,128]{2,1,0:T(8,128)(2,1)} %get-tuple-element.18), channel_id=1, source_target_pairs={{0,64},{64,128},{128,192},{192,0},{1,65},{65,129},{129,193},{193,1... | collective-permute-start | bytes 1720328 | tf_op jit(solution)/shard_map/ppermute | solution.py:243
  90.6 15.0 %collective-permute-start.18 = (bf16[4,560,128]{2,1,0:T(8,128)(2,1)S(1)}, bf16[4,560,128]{2,1,0:T(8,128)(2,1)S(1)}, u32[]{:S(2)}, u32[]{:S(2)}) collective-permute-start(bf16[4,560,128]{2,1,0:T(8,128)(2,1)S(1)} %collective-permute-done.8.refs_3_), channel_id=1, source_target_pairs={{0,1},{1,0},{2,3},{3,2},{4,5},{5,4},{6,7},{7,6},{8,9},{9,8},{10,11... | collective-permute-start | bytes 1720328 | tf_op jit(solution)/shard_map/ppermute | solution.py:243
  91.1 15.3 %collective-permute-start.17 = (bf16[4,560,128]{2,1,0:T(8,128)(2,1)S(1)}, bf16[4,560,128]{2,1,0:T(8,128)(2,1)S(1)}, u32[]{:S(2)}, u32[]{:S(2)}) collective-permute-start(bf16[4,560,128]{2,1,0:T(8,128)(2,1)S(1)} %collective-permute-done.7.refs_2_), channel_id=1, source_target_pairs={{0,1},{1,0},{2,3},{3,2},{4,5},{5,4},{6,7},{7,6},{8,9},{9,8},{10,11... | collective-permute-start | bytes 1720328 | tf_op jit(solution)/shard_map/ppermute | solution.py:243
  92.3 21.9 %collective-permute-start.16 = (bf16[4,560,128]{2,1,0:T(8,128)(2,1)}, bf16[4,560,128]{2,1,0:T(8,128)(2,1)}, u32[]{:S(2)}, u32[]{:S(2)}) collective-permute-start(bf16[4,560,128]{2,1,0:T(8,128)(2,1)} %collective-permute-done.6.refs_1_), channel_id=1, source_target_pairs={{0,1},{1,0},{2,3},{3,2},{4,5},{5,4},{6,7},{7,6},{8,9},{9,8},{10,11... | collective-permute-start | bytes 1720328 | tf_op jit(solution)/shard_map/ppermute | solution.py:243
  105.0 9.2 %collective-permute-start.21 = (bf16[4,560,128]{2,1,0:T(8,128)(2,1)}, bf16[4,560,128]{2,1,0:T(8,128)(2,1)}, u32[]{:S(2)}, u32[]{:S(2)}) collective-permute-start(bf16[4,560,128]{2,1,0:T(8,128)(2,1)} %collective-permute-done.11.refs_6_), channel_id=1, source_target_pairs={{0,1},{1,0},{2,3},{3,2},{4,5},{5,4},{6,7},{7,6},{8,9},{9,8},{10,11... | collective-permute-start | bytes 1720328 | tf_op jit(solution)/shard_map/ppermute | solution.py:243
  105.5 0.8 copy-start.3
  106.3 7.9 %collective-permute-start.20 = (bf16[4,560,128]{2,1,0:T(8,128)(2,1)}, bf16[4,560,128]{2,1,0:T(8,128)(2,1)}, u32[]{:S(2)}, u32[]{:S(2)}) collective-permute-start(bf16[4,560,128]{2,1,0:T(8,128)(2,1)} %collective-permute-done.10.refs_5_), channel_id=1, source_target_pairs={{0,1},{1,0},{2,3},{3,2},{4,5},{5,4},{6,7},{7,6},{8,9},{9,8},{10,11... | collective-permute-start | bytes 1720328 | tf_op jit(solution)/shard_map/ppermute | solution.py:243
  106.4 0.8 copy-start.5
  107.2 7.1 %collective-permute-start.19 = (bf16[4,560,128]{2,1,0:T(8,128)(2,1)}, bf16[4,560,128]{2,1,0:T(8,128)(2,1)}, u32[]{:S(2)}, u32[]{:S(2)}) collective-permute-start(bf16[4,560,128]{2,1,0:T(8,128)(2,1)} %collective-permute-done.9.refs_4_), channel_id=1, source_target_pairs={{0,1},{1,0},{2,3},{3,2},{4,5},{5,4},{6,7},{7,6},{8,9},{9,8},{10,11... | collective-permute-start | bytes 1720328 | tf_op jit(solution)/shard_map/ppermute | solution.py:243
  108.5 16.8 %all-to-all-start.3 = ((bf16[32,64,128]{2,1,0:T(8,128)(2,1)}), bf16[32,64,128]{2,1,0:T(8,128)(2,1)S(1)}, u32[]{:S(2)}, u32[]{:S(2)}) async-start(bf16[32,64,128]{2,1,0:T(8,128)(2,1)} %bitcast.12), calls=%async_computation.3 | async-start | bytes 1048576 | tf_op jit(solution)/shard_map/all_to_all | solution.py:238
  125.4 1.1 copy-start.2
  126.4 1.1 copy-start.4
  127.5 1.1 copy-start.6
  128.5 0.9 copy-start.8
  129.5 0.9 copy-start.10
  130.4 0.9 copy-start.12
  131.3 0.9 copy-start.14
  132.2 0.9 copy-start.16

commit v3 on v2

--- a/solution.py
+++ b/solution.py
@@ -118,41 +118,57 @@
             o_ref[x, s] = total
 
 
-def slab_kernel(at_ref, w_ref, o_ref):
+def slab_kernel(at_ref, w_ref, o_ref, r_ref):
     slab, core = at_ref[0], at_ref[1]
     main = w_ref[:, pl.ds(pl.multiple_of(slab * 256, 256), 256)]
     first = w_ref[:, 2048:2176].astype(f32)
     last = w_ref[:, 2176:2240].astype(f32)
     last = jnp.concatenate([last, jnp.zeros_like(last)], axis=1)
     pick = jnp.full(first.shape, core, jnp.int32) == 0
-    rest = jnp.where(pick, first, last).astype(bf16)
+    r_ref[...] = jnp.where(pick, first, last).astype(bf16)
     for t in range(NZ):
-        o_ref[t, :, :256] = main
-        o_ref[t, :, 256:] = rest
-
-
-def compact_kernel(w_ref, x_ref, y_ref, r_ref, rows_ref):
+        o_ref[t] = main
+
+
+def compact_kernel(w_ref, r0, r1, r2, r3, x_ref, y_ref, r_ref, rows_ref):
     rows = w_ref.shape[1]
     for t in range(NZ):
         rows_ref[pl.ds(t * rows, rows), :] = w_ref[t].astype(f32)
     slab = rows_ref[...].astype(bf16)
     x_ref[...] = slab[:, :128]
-    y_ref[...] = slab[:, 128:256]
-    r_ref[...] = slab[:, 256:]
+    y_ref[...] = slab[:, 128:]
+    for k, piece in enumerate((r0, r1, r2, r3)):
+        r_ref[k] = piece[...]
+
+
+def edge_kernel(z_ref, *refs):
+    pieces, (o_ref, rows_ref) = refs[:NZ], refs[NZ:]
+    rows = pieces[0].shape[1]
+    z = z_ref[0]
+    for own in range(NZ):
+
+        @pl.when(z == own)
+        def _():
+            for t in range(NZ):
+                for k in range(NX):
+                    at = k * ROWS_X + (own - t) % NZ * rows
+                    rows_ref[pl.ds(at, rows), :] = pieces[t][k].astype(f32)
+
+    for k in range(NX):
+        o_ref[k] = rows_ref[pl.ds(k * ROWS_X, ROWS_X), :].astype(bf16)
 
 
 def stack_kernel(*refs):
-    by_x, by_y, rest, (main_x, main_y, every) = refs[:4], refs[4:8], refs[8], refs[9:]
+    by_x, by_y, (main_x, main_y, every) = refs[:4], refs[4:8], refs[8:]
     for k in range(4):
         main_x[k] = by_x[k][...]
         main_y[k] = by_y[k][...]
         every[k] = by_x[k][...]
         every[4 + k] = by_y[k][...]
-    every[8] = rest[...]
 
 
 def project_kernel(at_ref, q_ref, p_ref, g_ref, *refs):
-    parts, (o_ref, w_ref, mixed_ref, normed_ref, sem) = refs[:20], refs[20:]
+    parts, (o_ref, w_ref, mixed_ref, normed_ref, sem) = refs[:16], refs[16:]
     x, y, core = at_ref[0], at_ref[1], at_ref[2]
     copies = []
 
@@ -164,13 +180,13 @@
 
     for side in range(NC):
         which = core if side == 0 else 1 - core
-        every, *rest = parts[10 * side : 10 * side + 10]
+        every, *rest = parts[8 * side : 8 * side + 8]
         by_y, by_x = (every.at[pl.ds(0, 4)], *rest[:3]), (every.at[pl.ds(4, 4)], *rest[3:6])
-        edges = (every.at[8], *rest[6:])
+        edges = rest[6]
         for k in range(4):
             block = lax.rem(x - k + NX, NX)
             column = which * 1024 + lax.rem(y - k + NY, NY) * 256
-            fetch(edges[k], block, 2048 + which * 128)
+            fetch(edges.at[k], block, 2048 + which * 128)
             for n in range(4):
                 turn = lax.rem(y - n + NY, NY)
                 fetch(by_y[n].at[k], block, which * 1024 + turn * 256)
@@ -217,7 +233,7 @@
     anyw = pl.BlockSpec(memory_space=pl.ANY)
     return pl.pallas_call(
         project_kernel,
-        in_specs=[pl.BlockSpec(memory_space=pltpu.SMEM), vmem, vmem, vmem] + [anyw] * 20,
+        in_specs=[pl.BlockSpec(memory_space=pltpu.SMEM), vmem, vmem, vmem] + [anyw] * 16,
         out_specs=vmem,
         out_shape=jax.ShapeDtypeStruct((D, tokens), bf16),
         scratch_shapes=[
@@ -258,17 +274,24 @@
     at = jnp.stack([core * NY + y, core]).astype(jnp.int32)
     zs = z.astype(jnp.int32).reshape(1)
     rows = out_weight.shape[0]
-    slab = small_call(slab_kernel, jax.ShapeDtypeStruct((NZ, rows, 384), bf16), (at,), (out_weight,))
+    slab, rest = small_call(
+        slab_kernel,
+        (jax.ShapeDtypeStruct((NZ, rows, 256), bf16), jax.ShapeDtypeStruct((rows, 128), bf16)),
+        (at,),
+        (out_weight,),
+    )
     w_z = swap(slab, "z")
+    rest = [rest, *shifted(rest, "x")]
     k_t, v_t = (pltpu.with_memory_space_constraint(a, pltpu.HBM) for a in (k_t, v_t))
     st = after(states(k_t, v_t), w_z)
     r1 = swap(st.reshape(32, PART, PAD), PIECES)
     x0, y0, r0 = small_call(
         compact_kernel,
-        (jax.ShapeDtypeStruct((ROWS_X, 128), bf16),) * 3,
+        (jax.ShapeDtypeStruct((ROWS_X, 128), bf16),) * 2
+        + (jax.ShapeDtypeStruct((NX, rows, 128), bf16),),
         (),
-        (w_z,),
-        (pltpu.VMEM((NZ * rows, 384), f32),),
+        (w_z, *rest),
+        (pltpu.VMEM((NZ * rows, 256), f32),),
     )
     by_x = [x0, *shifted(x0, "x")]
     by_y = [y0, *shifted(y0, "y")]
@@ -276,12 +299,13 @@
     r2s = swap(r2, "z")
     four = jax.ShapeDtypeStruct((4, ROWS_X, 128), bf16)
     main_x, main_y, every = small_call(
-        stack_kernel,
-        (four, four, jax.ShapeDtypeStruct((9, ROWS_X, 128), bf16)),
-        (),
-        (*by_x, *by_y, r0),
-    )
-    parts = [every, *shifted(main_x, "y"), *shifted(main_y, "x"), *shifted(r0, "x")]
+        stack_kernel, (four, four, jax.ShapeDtypeStruct((8, ROWS_X, 128), bf16)), (), (*by_x, *by_y)
+    )
+    parts = [every, *shifted(main_x, "y"), *shifted(main_y, "x")]
+    edge = small_call(
+        edge_kernel, four, (zs,), (r0, *shifted(r0, "z")), (pltpu.VMEM((D, 128), f32),)
+    )
+    parts.append(edge)
     r3 = small_call(prefix_kernel, jax.ShapeDtypeStruct((NX, 8, PART, PAD), bf16), (), (r2s,))
     prefix = swap(r3.reshape(32, PART, PAD), PIECES).reshape(2048, PAD)
     parts += [moved(part, "core", 1) for part in parts]

time: 149 us -> 149 us (level)
  blocking collectives: 23.1 us -> 0 us
  starting transfers between devices: 43.7 us -> 64.6 us
  waiting for transfers between devices: 43.8 us -> 50.6 us
  local copies, waits for them, and re-layouts: 12.6 us -> 7.27 us
    all_to_all x1 -> x0, blocking collectives: 23.1 us -> none  [swap(): return lax.all_to_all(value, axes, split_axis=0, concat_axis=0, tiled=True)]
    all_to_all x3 -> x4, starting transfers between devices: 16.1 us -> 29.9 us  [swap(): return lax.all_to_all(value, axes, split_axis=0, concat_axis=0, tiled=True)]
    ppermute x25 -> x30, starting transfers between devices: 27.6 us -> 34.6 us  [moved(): return lax.ppermute(value, axis, [(i, (i + step) % n) for i in range(n)])]
    unnamed x36 -> x20, local copies, waits for them, and re-layouts: 12.3 us -> 6.92 us
    all_to_all x3 -> x4, waiting for transfers between devices: 11.1 us -> 15.2 us  [swap(): return lax.all_to_all(value, axes, split_axis=0, concat_axis=0, tiled=True)]
    ppermute x25 -> x30, waiting for transfers between devices: 32.7 us -> 35.4 us  [moved(): return lax.ppermute(value, axis, [(i, (i + step) % n) for i in range(n)])]
    pallas_call x5 -> x6, Pallas kernels: 3.67 us -> 4.63 us  [small_call(): pl.pallas_call(kernel, in_specs=[pl.BlockSpec(memory_space=pltpu.SMEM)] *...]
  transfers between devices with their start and end apart: 28 -> 34, of which waited for: 7 -> 11; matrix products, arithmetic and copies ran while one was open for 0% -> 0% of each run, Pallas kernels for 6% -> 6%
where the time goes in v3:
time: 149 us; the launch traced here: 148 us
  starting transfers between devices  64.6 us (43%)
  waiting for transfers between devices  50.6 us (34%)
  Pallas kernels  25.4 us (17%)
  local copies, waits for them, and re-layouts  7.27 us (5%)
    ppermute x30, waiting for transfers between devices, moved(): return lax.ppermute(value, axis, [(i, (i + step) % n) for i in range(n)])  35.4 us
    ppermute x30, starting transfers between devices, moved(): return lax.ppermute(value, axis, [(i, (i + step) % n) for i in range(n)])  34.6 us
    all_to_all x4, starting transfers between devices, swap(): return lax.all_to_all(value, axes, split_axis=0, concat_axis=0, tiled=True)  29.9 us
    all_to_all x4, waiting for transfers between devices, swap(): return lax.all_to_all(value, axes, split_axis=0, concat_axis=0, tiled=True)  15.2 us
    pallas_call x1, Pallas kernels, project(): pl.pallas_call(project_kernel, in_specs=[pl.BlockSpec(memory_space=pltpu....  15 us
    unnamed x20, local copies, waits for them, and re-layouts  6.92 us
    pallas_call x1, Pallas kernels, states(): pl.pallas_call(state_kernel, grid=(HEADS // GROUP,), in_specs=[spec, spec...  5.79 us
    pallas_call x6, Pallas kernels, small_call(): pl.pallas_call(kernel, in_specs=[pl.BlockSpec(memory_space=pltpu.SMEM)] *...  4.63 us
  transfers between devices with their start and end apart: 34, of which 11 were waited for; matrix products, arithmetic and copies ran while one was open for 0% of the time, Pallas kernels for 6%

profile of v3, /device:TPU:1, one launch (start us, length us, event | category | flops | bytes accessed | tf_op | source)
XLA Modules:
  0.0 148.4 jit_solution(13584497006755435822)
XLA Ops:
  0.1 1.0 copy-done
  1.1 1.3 shard_map.55
  2.3 9.0 %all-to-all-start = ((bf16[8,70,256]{2,1,0:T(8,128)(2,1)}), bf16[8,70,256]{2,1,0:T(8,128)(2,1)S(1)}, u32[]{:S(2)}, u32[]{:S(2)}) async-start(bf16[8,70,256]{2,1,0:T(8,128)(2,1)} %get-tuple-element.14), calls=%async_computation | async-start | bytes 589824 | tf_op jit(solution)/shard_map/all_to_all | solution.py:254
  11.3 2.5 %collective-permute-start.2 = (bf16[70,128]{1,0:T(8,128)(2,1)S(1)}, bf16[70,128]{1,0:T(8,128)(2,1)S(1)}, u32[]{:S(2)}, u32[]{:S(2)}) collective-permute-start(bf16[70,128]{1,0:T(8,128)(2,1)S(1)} %get-tuple-element.16.r0), channel_id=1, source_target_pairs={{0,192},{64,0},{128,64},{192,128},{1,193},{65,1},{129,65},{193,129... | collective-permute-start | bytes 53768 | tf_op jit(solution)/shard_map/ppermute | solution.py:259
  13.8 0.5 collective-permute-start.1
  14.3 0.6 collective-permute-start
  14.9 3.0 %collective-permute-done.1.r2 = bf16[70,128]{1,0:T(8,128)(2,1)S(1)} collective-permute-done((bf16[70,128]{1,0:T(8,128)(2,1)S(1)}, bf16[70,128]{1,0:T(8,128)(2,1)S(1)}, u32[]{:S(2)}, u32[]{:S(2)}) %collective-permute-start.1) | collective-permute-done | bytes 17952 | tf_op jit(solution)/shard_map/ppermute | solution.py:259
  17.9 0.5 collective-permute-done.r1
  18.5 4.1 %all-to-all-done.w_ref = bf16[8,70,256]{2,1,0:T(8,128)(2,1)S(1)} async-done(((bf16[8,70,256]{2,1,0:T(8,128)(2,1)}), bf16[8,70,256]{2,1,0:T(8,128)(2,1)S(1)}, u32[]{:S(2)}, u32[]{:S(2)}) %all-to-all-start) | async-done | bytes 286752 | tf_op jit(solution)/shard_map/all_to_all | solution.py:254
  22.8 1.3 collective-permute-start.20
  24.0 2.1 %collective-permute-start.19 = (bf16[4,70,128]{2,1,0:T(8,128)(2,1)S(1)}, bf16[4,70,128]{2,1,0:T(8,128)(2,1)S(1)}, u32[]{:S(2)}, u32[]{:S(2)}) collective-permute-start(bf16[4,70,128]{2,1,0:T(8,128)(2,1)S(1)} %get-tuple-element.22.refs_0_), channel_id=1, source_target_pairs={{0,40},{8,48},{16,56},{24,0},{32,8},{40,16},{48,24},{56,32},{1,41}... | collective-permute-start | bytes 215048 | tf_op jit(solution)/shard_map/ppermute | solution.py:259
  26.1 2.5 %collective-permute-start.5 = (bf16[560,128]{1,0:T(8,128)(2,1)S(1)}, bf16[560,128]{1,0:T(8,128)(2,1)S(1)}, u32[]{:S(2)}, u32[]{:S(2)}) collective-permute-start(bf16[560,128]{1,0:T(8,128)(2,1)S(1)} %get-tuple-element.17.refs_0_), channel_id=1, source_target_pairs={{0,192},{64,0},{128,64},{192,128},{1,193},{65,1},{129,65},{193,129... | collective-permute-start | bytes 430088 | tf_op jit(solution)/shard_map/ppermute | solution.py:259
  28.6 3.5 %collective-permute-start.18 = (bf16[4,70,128]{2,1,0:T(8,128)(2,1)S(1)}, bf16[4,70,128]{2,1,0:T(8,128)(2,1)S(1)}, u32[]{:S(2)}, u32[]{:S(2)}) collective-permute-start(bf16[4,70,128]{2,1,0:T(8,128)(2,1)S(1)} %get-tuple-element.22.refs_0_), channel_id=1, source_target_pairs={{0,32},{8,40},{16,48},{24,56},{32,0},{40,8},{48,16},{56,24},{1,33}... | collective-permute-start | bytes 215048 | tf_op jit(solution)/shard_map/ppermute | solution.py:259
  32.1 3.3 %collective-permute-start.16 = (bf16[4,70,128]{2,1,0:T(8,128)(2,1)S(1)}, bf16[4,70,128]{2,1,0:T(8,128)(2,1)S(1)}, u32[]{:S(2)}, u32[]{:S(2)}) collective-permute-start(bf16[4,70,128]{2,1,0:T(8,128)(2,1)S(1)} %get-tuple-element.22.refs_0_), channel_id=1, source_target_pairs={{0,16},{8,24},{16,32},{24,40},{32,48},{40,56},{48,0},{56,8},{1,17}... | collective-permute-start | bytes 215048 | tf_op jit(solution)/shard_map/ppermute | solution.py:259
  35.4 5.8 %states.1 = bf16[2048,128]{1,0:T(8,128)(2,1)} custom-call(bf16[2240,640]{1,0:T(8,128)(2,1)} %bitcast.21, bf16[2240,640]{1,0:T(8,128)(2,1)} %bitcast.22), custom_call_target="tpu_custom_call" | custom-call | flops 419430400 | bytes 5734400 | tf_op jit(solution)/shard_map/states/pallas_call | solution.py:68
  41.1 10.9 %all-to-all-start.1 = ((bf16[32,64,128]{2,1,0:T(8,128)(2,1)}), bf16[32,64,128]{2,1,0:T(8,128)(2,1)S(1)}, u32[]{:S(2)}, u32[]{:S(2)}) async-start(bf16[32,64,128]{2,1,0:T(8,128)(2,1)} %bitcast.11), calls=%async_computation.1 | async-start | bytes 1048576 | tf_op jit(solution)/shard_map/all_to_all | solution.py:254
  52.0 3.0 %collective-permute-start.4 = (bf16[560,128]{1,0:T(8,128)(2,1)S(1)}, bf16[560,128]{1,0:T(8,128)(2,1)S(1)}, u32[]{:S(2)}, u32[]{:S(2)}) collective-permute-start(bf16[560,128]{1,0:T(8,128)(2,1)S(1)} %get-tuple-element.17.refs_0_), channel_id=1, source_target_pairs={{0,128},{64,192},{128,0},{192,64},{1,129},{65,193},{129,1},{193,65... | collective-permute-start | bytes 430088 | tf_op jit(solution)/shard_map/ppermute | solution.py:259
  55.3 2.4 %collective-permute-start.8 = (bf16[560,128]{1,0:T(8,128)(2,1)S(1)}, bf16[560,128]{1,0:T(8,128)(2,1)S(1)}, u32[]{:S(2)}, u32[]{:S(2)}) collective-permute-start(bf16[560,128]{1,0:T(8,128)(2,1)S(1)} %get-tuple-element.18.refs_4_), channel_id=1, source_target_pairs={{0,6},{2,0},{4,2},{6,4},{1,7},{3,1},{5,3},{7,5},{8,14},{10,8},{12,... | collective-permute-start | bytes 430088 | tf_op jit(solution)/shard_map/ppermute | solution.py:259
  57.8 0.6 collective-permute-start.7
  58.3 0.6 collective-permute-start.6
  59.1 5.3 %collective-permute-done.4.refs_2_ = bf16[560,128]{1,0:T(8,128)(2,1)S(1)} collective-permute-done((bf16[560,128]{1,0:T(8,128)(2,1)S(1)}, bf16[560,128]{1,0:T(8,128)(2,1)S(1)}, u32[]{:S(2)}, u32[]{:S(2)}) %collective-permute-start.4) | collective-permute-done | bytes 143392 | tf_op jit(solution)/shard_map/ppermute | solution.py:259
  64.3 1.5 %collective-permute-start.29 = (bf16[4,560,128]{2,1,0:T(8,128)(2,1)S(1)}, bf16[4,560,128]{2,1,0:T(8,128)(2,1)}, u32[]{:S(2)}, u32[]{:S(2)}) collective-permute-start(bf16[4,560,128]{2,1,0:T(8,128)(2,1)S(1)} %shard_map.60.refs_7_), channel_id=1, source_target_pairs={{0,1},{1,0},{2,3},{3,2},{4,5},{5,4},{6,7},{7,6},{8,9},{9,8},{10,11... | collective-permute-start | bytes 1720328 | tf_op jit(solution)/shard_map/ppermute | solution.py:259
  65.9 1.3 collective-permute-done.3.refs_1_
  67.2 1.8 %collective-permute-done.6.refs_5_ = bf16[560,128]{1,0:T(8,128)(2,1)S(1)} collective-permute-done((bf16[560,128]{1,0:T(8,128)(2,1)S(1)}, bf16[560,128]{1,0:T(8,128)(2,1)S(1)}, u32[]{:S(2)}, u32[]{:S(2)}) %collective-permute-start.6) | collective-permute-done | bytes 143392 | tf_op jit(solution)/shard_map/ppermute | solution.py:259
  69.0 1.2 shard_map.59
  70.2 0.8 collective-permute-start.11
  71.4 0.7 collective-permute-start.9
  72.1 1.4 collective-permute-start.14
  73.6 1.0 shard_map.56
  74.5 4.5 %all-to-all-start.2 = ((bf16[8,4,64,128]{3,2,1,0:T(8,128)(2,1)}), bf16[8,4,64,128]{3,2,1,0:T(8,128)(2,1)S(1)}, u32[]{:S(2)}, u32[]{:S(2)}) async-start(bf16[8,4,64,128]{3,2,1,0:T(8,128)(2,1)} %shard_map.56), calls=%async_computation.2 | async-start | bytes 1048576 | tf_op jit(solution)/shard_map/all_to_all | solution.py:254
  79.6 4.8 %collective-permute-done.11.refs_3_ = bf16[4,560,128]{2,1,0:T(8,128)(2,1)S(1)} collective-permute-done((bf16[4,560,128]{2,1,0:T(8,128)(2,1)}, bf16[4,560,128]{2,1,0:T(8,128)(2,1)S(1)}, u32[]{:S(2)}, u32[]{:S(2)}) %collective-permute-start.11) | collective-permute-done | bytes 573472 | tf_op jit(solution)/shard_map/ppermute | solution.py:259
  84.3 0.8 collective-permute-start.12
  85.2 1.2 collective-permute-done.10.refs_2_
  86.3 3.3 %collective-permute-start.25 = (bf16[4,560,128]{2,1,0:T(8,128)(2,1)S(1)}, bf16[4,560,128]{2,1,0:T(8,128)(2,1)S(1)}, u32[]{:S(2)}, u32[]{:S(2)}) collective-permute-start(bf16[4,560,128]{2,1,0:T(8,128)(2,1)S(1)} %collective-permute-done.11.refs_3_), channel_id=1, source_target_pairs={{0,1},{1,0},{2,3},{3,2},{4,5},{5,4},{6,7},{7,6},{8,9},{9,8},{10,11... | collective-permute-start | bytes 1720328 | tf_op jit(solution)/shard_map/ppermute | solution.py:259
  89.7 10.3 %collective-permute-done.9.refs_1_ = bf16[4,560,128]{2,1,0:T(8,128)(2,1)} collective-permute-done((bf16[4,560,128]{2,1,0:T(8,128)(2,1)}, bf16[4,560,128]{2,1,0:T(8,128)(2,1)}, u32[]{:S(2)}, u32[]{:S(2)}) %collective-permute-start.9) | collective-permute-done | bytes 573472 | tf_op jit(solution)/shard_map/ppermute | solution.py:259
  100.0 0.5 collective-permute-start.24
  100.5 0.5 collective-permute-start.23
  101.0 7.1 %collective-permute-done.12.refs_4_ = bf16[4,560,128]{2,1,0:T(8,128)(2,1)} collective-permute-done((bf16[4,560,128]{2,1,0:T(8,128)(2,1)}, bf16[4,560,128]{2,1,0:T(8,128)(2,1)}, u32[]{:S(2)}, u32[]{:S(2)}) %collective-permute-start.12) | collective-permute-done | bytes 573472 | tf_op jit(solution)/shard_map/ppermute | solution.py:259
  108.7 0.9 copy-done.5
  109.6 0.8 copy-done.7
  110.9 0.9 shard_map.57
  111.8 5.5 %all-to-all-start.3 = ((bf16[32,64,128]{2,1,0:T(8,128)(2,1)}), bf16[32,64,128]{2,1,0:T(8,128)(2,1)S(1)}, u32[]{:S(2)}, u32[]{:S(2)}) async-start(bf16[32,64,128]{2,1,0:T(8,128)(2,1)} %bitcast.12), calls=%async_computation.3 | async-start | bytes 1048576 | tf_op jit(solution)/shard_map/all_to_all | solution.py:254
  117.8 11.1 %all-to-all-done.3 = bf16[32,64,128]{2,1,0:T(8,128)(2,1)S(1)} async-done(((bf16[32,64,128]{2,1,0:T(8,128)(2,1)}), bf16[32,64,128]{2,1,0:T(8,128)(2,1)S(1)}, u32[]{:S(2)}, u32[]{:S(2)}) %all-to-all-start.3) | async-done | bytes 524320 | tf_op jit(solution)/shard_map/all_to_all | solution.py:254
  128.9 1.1 copy-done.2
  130.0 1.1 copy-done.4
  131.1 1.1 copy-done.6
  132.1 1.1 copy-done.8
  133.2 15.0 %project.1 = bf16[2240,640]{1,0:T(8,128)(2,1)} custom-call(s32[3]{0:T(128)S(1)} %pad_add_fusion.at_ref, bf16[2240,640]{1,0:T(8,128)(2,1)} %bitcast.23, bf16[2048,128]{1,0:T(8,128)(2,1)S(1)} %bitcast.20, f32[2240,1]{1,0:T(8,128)S(1)} %reshape.20.g_ref, bf16[8,560,128]{2,1,0:T(8,128)(2,1)S(1)} %get-tuple-element.19.refs_0_, ...), custom_call_target="tpu_custom_call" | custom-call | flops 6422528000 | bytes 16056320 | tf_op jit(solution)/shard_map/project/pallas_call | solution.py:234
  (51 shorter events, 3.2 us)
Async XLA Ops:
  0.1 1.0 copy-start
  2.3 20.3 %all-to-all-start = ((bf16[8,70,256]{2,1,0:T(8,128)(2,1)}), bf16[8,70,256]{2,1,0:T(8,128)(2,1)S(1)}, u32[]{:S(2)}, u32[]{:S(2)}) async-start(bf16[8,70,256]{2,1,0:T(8,128)(2,1)} %get-tuple-element.14), calls=%async_computation | async-start | bytes 589824 | tf_op jit(solution)/shard_map/all_to_all | solution.py:254
  11.3 3.6 %collective-permute-start.2 = (bf16[70,128]{1,0:T(8,128)(2,1)S(1)}, bf16[70,128]{1,0:T(8,128)(2,1)S(1)}, u32[]{:S(2)}, u32[]{:S(2)}) collective-permute-start(bf16[70,128]{1,0:T(8,128)(2,1)S(1)} %get-tuple-element.16.r0), channel_id=1, source_target_pairs={{0,192},{64,0},{128,64},{192,128},{1,193},{65,1},{129,65},{193,129... | collective-permute-start | bytes 53768 | tf_op jit(solution)/shard_map/ppermute | solution.py:259
  13.8 4.1 %collective-permute-start.1 = (bf16[70,128]{1,0:T(8,128)(2,1)S(1)}, bf16[70,128]{1,0:T(8,128)(2,1)S(1)}, u32[]{:S(2)}, u32[]{:S(2)}) collective-permute-start(bf16[70,128]{1,0:T(8,128)(2,1)S(1)} %get-tuple-element.16.r0), channel_id=1, source_target_pairs={{0,128},{64,192},{128,0},{192,64},{1,129},{65,193},{129,1},{193,65... | collective-permute-start | bytes 53768 | tf_op jit(solution)/shard_map/ppermute | solution.py:259
  14.3 4.1 %collective-permute-start = (bf16[70,128]{1,0:T(8,128)(2,1)S(1)}, bf16[70,128]{1,0:T(8,128)(2,1)S(1)}, u32[]{:S(2)}, u32[]{:S(2)}) collective-permute-start(bf16[70,128]{1,0:T(8,128)(2,1)S(1)} %get-tuple-element.16.r0), channel_id=1, source_target_pairs={{0,64},{64,128},{128,192},{192,0},{1,65},{65,129},{129,193},{193,1... | collective-permute-start | bytes 53768 | tf_op jit(solution)/shard_map/ppermute | solution.py:259
  22.7 9.4 %collective-permute-start.21 = (bf16[4,70,128]{2,1,0:T(8,128)(2,1)S(1)}, bf16[4,70,128]{2,1,0:T(8,128)(2,1)S(1)}, u32[]{:S(2)}, u32[]{:S(2)}) collective-permute-start(bf16[4,70,128]{2,1,0:T(8,128)(2,1)S(1)} %get-tuple-element.22.refs_0_), channel_id=1, source_target_pairs={{0,56},{8,0},{16,8},{24,16},{32,24},{40,32},{48,40},{56,48},{1,57}... | collective-permute-start | bytes 215048 | tf_op jit(solution)/shard_map/ppermute | solution.py:259
  22.8 9.3 %collective-permute-start.20 = (bf16[4,70,128]{2,1,0:T(8,128)(2,1)S(1)}, bf16[4,70,128]{2,1,0:T(8,128)(2,1)S(1)}, u32[]{:S(2)}, u32[]{:S(2)}) collective-permute-start(bf16[4,70,128]{2,1,0:T(8,128)(2,1)S(1)} %get-tuple-element.22.refs_0_), channel_id=1, source_target_pairs={{0,48},{8,56},{16,0},{24,8},{32,16},{40,24},{48,32},{56,40},{1,49}... | collective-permute-start | bytes 215048 | tf_op jit(solution)/shard_map/ppermute | solution.py:259
  24.0 11.3 %collective-permute-start.19 = (bf16[4,70,128]{2,1,0:T(8,128)(2,1)S(1)}, bf16[4,70,128]{2,1,0:T(8,128)(2,1)S(1)}, u32[]{:S(2)}, u32[]{:S(2)}) collective-permute-start(bf16[4,70,128]{2,1,0:T(8,128)(2,1)S(1)} %get-tuple-element.22.refs_0_), channel_id=1, source_target_pairs={{0,40},{8,48},{16,56},{24,0},{32,8},{40,16},{48,24},{56,32},{1,41}... | collective-permute-start | bytes 215048 | tf_op jit(solution)/shard_map/ppermute | solution.py:259
  26.1 32.2 %collective-permute-start.5 = (bf16[560,128]{1,0:T(8,128)(2,1)S(1)}, bf16[560,128]{1,0:T(8,128)(2,1)S(1)}, u32[]{:S(2)}, u32[]{:S(2)}) collective-permute-start(bf16[560,128]{1,0:T(8,128)(2,1)S(1)} %get-tuple-element.17.refs_0_), channel_id=1, source_target_pairs={{0,192},{64,0},{128,64},{192,128},{1,193},{65,1},{129,65},{193,129... | collective-permute-start | bytes 430088 | tf_op jit(solution)/shard_map/ppermute | solution.py:259
  28.6 23.4 %collective-permute-start.18 = (bf16[4,70,128]{2,1,0:T(8,128)(2,1)S(1)}, bf16[4,70,128]{2,1,0:T(8,128)(2,1)S(1)}, u32[]{:S(2)}, u32[]{:S(2)}) collective-permute-start(bf16[4,70,128]{2,1,0:T(8,128)(2,1)S(1)} %get-tuple-element.22.refs_0_), channel_id=1, source_target_pairs={{0,32},{8,40},{16,48},{24,56},{32,0},{40,8},{48,16},{56,24},{1,33}... | collective-permute-start | bytes 215048 | tf_op jit(solution)/shard_map/ppermute | solution.py:259
  32.1 22.9 %collective-permute-start.17 = (bf16[4,70,128]{2,1,0:T(8,128)(2,1)S(1)}, bf16[4,70,128]{2,1,0:T(8,128)(2,1)S(1)}, u32[]{:S(2)}, u32[]{:S(2)}) collective-permute-start(bf16[4,70,128]{2,1,0:T(8,128)(2,1)S(1)} %get-tuple-element.22.refs_0_), channel_id=1, source_target_pairs={{0,24},{8,32},{16,40},{24,48},{32,56},{40,0},{48,8},{56,16},{1,25}... | collective-permute-start | bytes 215048 | tf_op jit(solution)/shard_map/ppermute | solution.py:259
  32.1 23.2 %collective-permute-start.16 = (bf16[4,70,128]{2,1,0:T(8,128)(2,1)S(1)}, bf16[4,70,128]{2,1,0:T(8,128)(2,1)S(1)}, u32[]{:S(2)}, u32[]{:S(2)}) collective-permute-start(bf16[4,70,128]{2,1,0:T(8,128)(2,1)S(1)} %get-tuple-element.22.refs_0_), channel_id=1, source_target_pairs={{0,16},{8,24},{16,32},{24,40},{32,48},{40,56},{48,0},{56,8},{1,17}... | collective-permute-start | bytes 215048 | tf_op jit(solution)/shard_map/ppermute | solution.py:259
  35.3 22.4 %collective-permute-start.15 = (bf16[4,70,128]{2,1,0:T(8,128)(2,1)S(1)}, bf16[4,70,128]{2,1,0:T(8,128)(2,1)S(1)}, u32[]{:S(2)}, u32[]{:S(2)}) collective-permute-start(bf16[4,70,128]{2,1,0:T(8,128)(2,1)S(1)} %get-tuple-element.22.refs_0_), channel_id=1, source_target_pairs={{0,8},{8,16},{16,24},{24,32},{32,40},{40,48},{48,56},{56,0},{1,9},... | collective-permute-start | bytes 215048 | tf_op jit(solution)/shard_map/ppermute | solution.py:259
  41.1 32.4 %all-to-all-start.1 = ((bf16[32,64,128]{2,1,0:T(8,128)(2,1)}), bf16[32,64,128]{2,1,0:T(8,128)(2,1)S(1)}, u32[]{:S(2)}, u32[]{:S(2)}) async-start(bf16[32,64,128]{2,1,0:T(8,128)(2,1)} %bitcast.11), calls=%async_computation.1 | async-start | bytes 1048576 | tf_op jit(solution)/shard_map/all_to_all | solution.py:254
  52.0 12.3 %collective-permute-start.4 = (bf16[560,128]{1,0:T(8,128)(2,1)S(1)}, bf16[560,128]{1,0:T(8,128)(2,1)S(1)}, u32[]{:S(2)}, u32[]{:S(2)}) collective-permute-start(bf16[560,128]{1,0:T(8,128)(2,1)S(1)} %get-tuple-element.17.refs_0_), channel_id=1, source_target_pairs={{0,128},{64,192},{128,0},{192,64},{1,129},{65,193},{129,1},{193,65... | collective-permute-start | bytes 430088 | tf_op jit(solution)/shard_map/ppermute | solution.py:259
  55.0 12.2 %collective-permute-start.3 = (bf16[560,128]{1,0:T(8,128)(2,1)S(1)}, bf16[560,128]{1,0:T(8,128)(2,1)S(1)}, u32[]{:S(2)}, u32[]{:S(2)}) collective-permute-start(bf16[560,128]{1,0:T(8,128)(2,1)S(1)} %get-tuple-element.17.refs_0_), channel_id=1, source_target_pairs={{0,64},{64,128},{128,192},{192,0},{1,65},{65,129},{129,193},{193,1... | collective-permute-start | bytes 430088 | tf_op jit(solution)/shard_map/ppermute | solution.py:259
  55.3 11.9 %collective-permute-start.8 = (bf16[560,128]{1,0:T(8,128)(2,1)S(1)}, bf16[560,128]{1,0:T(8,128)(2,1)S(1)}, u32[]{:S(2)}, u32[]{:S(2)}) collective-permute-start(bf16[560,128]{1,0:T(8,128)(2,1)S(1)} %get-tuple-element.18.refs_4_), channel_id=1, source_target_pairs={{0,6},{2,0},{4,2},{6,4},{1,7},{3,1},{5,3},{7,5},{8,14},{10,8},{12,... | collective-permute-start | bytes 430088 | tf_op jit(solution)/shard_map/ppermute | solution.py:259
  57.8 9.5 %collective-permute-start.7 = (bf16[560,128]{1,0:T(8,128)(2,1)S(1)}, bf16[560,128]{1,0:T(8,128)(2,1)S(1)}, u32[]{:S(2)}, u32[]{:S(2)}) collective-permute-start(bf16[560,128]{1,0:T(8,128)(2,1)S(1)} %get-tuple-element.18.refs_4_), channel_id=1, source_target_pairs={{0,4},{2,6},{4,0},{6,2},{1,5},{3,7},{5,1},{7,3},{8,12},{10,14},{12... | collective-permute-start | bytes 430088 | tf_op jit(solution)/shard_map/ppermute | solution.py:259
  58.3 10.7 %collective-permute-start.6 = (bf16[560,128]{1,0:T(8,128)(2,1)S(1)}, bf16[560,128]{1,0:T(8,128)(2,1)S(1)}, u32[]{:S(2)}, u32[]{:S(2)}) collective-permute-start(bf16[560,128]{1,0:T(8,128)(2,1)S(1)} %get-tuple-element.18.refs_4_), channel_id=1, source_target_pairs={{0,2},{2,4},{4,6},{6,0},{1,3},{3,5},{5,7},{7,1},{8,10},{10,12},{12... | collective-permute-start | bytes 430088 | tf_op jit(solution)/shard_map/ppermute | solution.py:259
  59.1 58.3 %copy-start.9 = (f32[2240]{0:T(1024)S(1)}, f32[2240]{0:T(1024)}, u32[]{:S(2)}) copy-start(f32[2240]{0:T(1024)} %param.8) | copy-start | bytes 26884
  64.3 14.7 %collective-permute-start.29 = (bf16[4,560,128]{2,1,0:T(8,128)(2,1)S(1)}, bf16[4,560,128]{2,1,0:T(8,128)(2,1)}, u32[]{:S(2)}, u32[]{:S(2)}) collective-permute-start(bf16[4,560,128]{2,1,0:T(8,128)(2,1)S(1)} %shard_map.60.refs_7_), channel_id=1, source_target_pairs={{0,1},{1,0},{2,3},{3,2},{4,5},{5,4},{6,7},{7,6},{8,9},{9,8},{10,11... | collective-permute-start | bytes 1720328 | tf_op jit(solution)/shard_map/ppermute | solution.py:259
  70.2 14.1 %collective-permute-start.11 = (bf16[4,560,128]{2,1,0:T(8,128)(2,1)}, bf16[4,560,128]{2,1,0:T(8,128)(2,1)S(1)}, u32[]{:S(2)}, u32[]{:S(2)}) collective-permute-start(bf16[4,560,128]{2,1,0:T(8,128)(2,1)} %get-tuple-element.20), channel_id=1, source_target_pairs={{0,6},{2,0},{4,2},{6,4},{1,7},{3,1},{5,3},{7,5},{8,14},{10,8},{12,... | collective-permute-start | bytes 1720328 | tf_op jit(solution)/shard_map/ppermute | solution.py:259
  71.0 15.3 %collective-permute-start.10 = (bf16[4,560,128]{2,1,0:T(8,128)(2,1)}, bf16[4,560,128]{2,1,0:T(8,128)(2,1)S(1)}, u32[]{:S(2)}, u32[]{:S(2)}) collective-permute-start(bf16[4,560,128]{2,1,0:T(8,128)(2,1)} %get-tuple-element.20), channel_id=1, source_target_pairs={{0,4},{2,6},{4,0},{6,2},{1,5},{3,7},{5,1},{7,3},{8,12},{10,14},{12... | collective-permute-start | bytes 1720328 | tf_op jit(solution)/shard_map/ppermute | solution.py:259
  71.4 28.5 %collective-permute-start.9 = (bf16[4,560,128]{2,1,0:T(8,128)(2,1)}, bf16[4,560,128]{2,1,0:T(8,128)(2,1)}, u32[]{:S(2)}, u32[]{:S(2)}) collective-permute-start(bf16[4,560,128]{2,1,0:T(8,128)(2,1)} %get-tuple-element.20), channel_id=1, source_target_pairs={{0,2},{2,4},{4,6},{6,0},{1,3},{3,5},{5,7},{7,1},{8,10},{10,12},{12... | collective-permute-start | bytes 1720328 | tf_op jit(solution)/shard_map/ppermute | solution.py:259
  72.1 28.4 %collective-permute-start.14 = (bf16[4,560,128]{2,1,0:T(8,128)(2,1)}, bf16[4,560,128]{2,1,0:T(8,128)(2,1)}, u32[]{:S(2)}, u32[]{:S(2)}) collective-permute-start(bf16[4,560,128]{2,1,0:T(8,128)(2,1)} %get-tuple-element.21), channel_id=1, source_target_pairs={{0,192},{64,0},{128,64},{192,128},{1,193},{65,1},{129,65},{193,129... | collective-permute-start | bytes 1720328 | tf_op jit(solution)/shard_map/ppermute | solution.py:259
  74.5 36.3 %all-to-all-start.2 = ((bf16[8,4,64,128]{3,2,1,0:T(8,128)(2,1)}), bf16[8,4,64,128]{3,2,1,0:T(8,128)(2,1)S(1)}, u32[]{:S(2)}, u32[]{:S(2)}) async-start(bf16[8,4,64,128]{3,2,1,0:T(8,128)(2,1)} %shard_map.56), calls=%async_computation.2 | async-start | bytes 1048576 | tf_op jit(solution)/shard_map/all_to_all | solution.py:254
  79.1 21.5 %collective-permute-start.13 = (bf16[4,560,128]{2,1,0:T(8,128)(2,1)}, bf16[4,560,128]{2,1,0:T(8,128)(2,1)}, u32[]{:S(2)}, u32[]{:S(2)}) collective-permute-start(bf16[4,560,128]{2,1,0:T(8,128)(2,1)} %get-tuple-element.21), channel_id=1, source_target_pairs={{0,128},{64,192},{128,0},{192,64},{1,129},{65,193},{129,1},{193,65... | collective-permute-start | bytes 1720328 | tf_op jit(solution)/shard_map/ppermute | solution.py:259
  84.3 27.5 %copy-start.1 = (bf16[4,560,128]{2,1,0:T(8,128)(2,1)}, bf16[4,560,128]{2,1,0:T(8,128)(2,1)S(1)}, u32[]{:S(2)}) copy-start(bf16[4,560,128]{2,1,0:T(8,128)(2,1)S(1)} %collective-permute-done.11.refs_3_) | copy-start | bytes 1720324
  84.3 23.8 %collective-permute-start.12 = (bf16[4,560,128]{2,1,0:T(8,128)(2,1)}, bf16[4,560,128]{2,1,0:T(8,128)(2,1)}, u32[]{:S(2)}, u32[]{:S(2)}) collective-permute-start(bf16[4,560,128]{2,1,0:T(8,128)(2,1)} %get-tuple-element.21), channel_id=1, source_target_pairs={{0,64},{64,128},{128,192},{192,0},{1,65},{65,129},{129,193},{193,1... | collective-permute-start | bytes 1720328 | tf_op jit(solution)/shard_map/ppermute | solution.py:259
  86.3 31.0 %copy-start.3 = (bf16[4,560,128]{2,1,0:T(8,128)(2,1)}, bf16[4,560,128]{2,1,0:T(8,128)(2,1)S(1)}, u32[]{:S(2)}) copy-start(bf16[4,560,128]{2,1,0:T(8,128)(2,1)S(1)} %collective-permute-done.10.refs_2_) | copy-start | bytes 1720324
  86.3 22.3 %collective-permute-start.25 = (bf16[4,560,128]{2,1,0:T(8,128)(2,1)S(1)}, bf16[4,560,128]{2,1,0:T(8,128)(2,1)S(1)}, u32[]{:S(2)}, u32[]{:S(2)}) collective-permute-start(bf16[4,560,128]{2,1,0:T(8,128)(2,1)S(1)} %collective-permute-done.11.refs_3_), channel_id=1, source_target_pairs={{0,1},{1,0},{2,3},{3,2},{4,5},{5,4},{6,7},{7,6},{8,9},{9,8},{10,11... | collective-permute-start | bytes 1720328 | tf_op jit(solution)/shard_map/ppermute | solution.py:259
  100.0 9.6 %collective-permute-start.24 = (bf16[4,560,128]{2,1,0:T(8,128)(2,1)S(1)}, bf16[4,560,128]{2,1,0:T(8,128)(2,1)S(1)}, u32[]{:S(2)}, u32[]{:S(2)}) collective-permute-start(bf16[4,560,128]{2,1,0:T(8,128)(2,1)S(1)} %collective-permute-done.10.refs_2_), channel_id=1, source_target_pairs={{0,1},{1,0},{2,3},{3,2},{4,5},{5,4},{6,7},{7,6},{8,9},{9,8},{10,11... | collective-permute-start | bytes 1720328 | tf_op jit(solution)/shard_map/ppermute | solution.py:259
  100.5 17.3 %collective-permute-start.22 = (bf16[8,560,128]{2,1,0:T(8,128)(2,1)S(1)}, bf16[8,560,128]{2,1,0:T(8,128)(2,1)}, u32[]{:S(2)}, u32[]{:S(2)}) collective-permute-start(bf16[8,560,128]{2,1,0:T(8,128)(2,1)S(1)} %get-tuple-element.19.refs_0_), channel_id=1, source_target_pairs={{0,1},{1,0},{2,3},{3,2},{4,5},{5,4},{6,7},{7,6},{8,9},{9,8},{10,11... | collective-permute-start | bytes 3440648 | tf_op jit(solution)/shard_map/ppermute | solution.py:259
  100.5 17.3 %collective-permute-start.23 = (bf16[4,560,128]{2,1,0:T(8,128)(2,1)}, bf16[4,560,128]{2,1,0:T(8,128)(2,1)}, u32[]{:S(2)}, u32[]{:S(2)}) collective-permute-start(bf16[4,560,128]{2,1,0:T(8,128)(2,1)} %collective-permute-done.9.refs_1_), channel_id=1, source_target_pairs={{0,1},{1,0},{2,3},{3,2},{4,5},{5,4},{6,7},{7,6},{8,9},{9,8},{10,11... | collective-permute-start | bytes 1720328 | tf_op jit(solution)/shard_map/ppermute | solution.py:259
  108.2 9.7 %collective-permute-start.28 = (bf16[4,560,128]{2,1,0:T(8,128)(2,1)}, bf16[4,560,128]{2,1,0:T(8,128)(2,1)}, u32[]{:S(2)}, u32[]{:S(2)}) collective-permute-start(bf16[4,560,128]{2,1,0:T(8,128)(2,1)} %collective-permute-done.14.refs_6_), channel_id=1, source_target_pairs={{0,1},{1,0},{2,3},{3,2},{4,5},{5,4},{6,7},{7,6},{8,9},{9,8},{10,11... | collective-permute-start | bytes 1720328 | tf_op jit(solution)/shard_map/ppermute | solution.py:259
  108.7 0.9 copy-start.5
  109.5 8.3 %collective-permute-start.27 = (bf16[4,560,128]{2,1,0:T(8,128)(2,1)}, bf16[4,560,128]{2,1,0:T(8,128)(2,1)}, u32[]{:S(2)}, u32[]{:S(2)}) collective-permute-start(bf16[4,560,128]{2,1,0:T(8,128)(2,1)} %collective-permute-done.13.refs_5_), channel_id=1, source_target_pairs={{0,1},{1,0},{2,3},{3,2},{4,5},{5,4},{6,7},{7,6},{8,9},{9,8},{10,11... | collective-permute-start | bytes 1720328 | tf_op jit(solution)/shard_map/ppermute | solution.py:259
  109.6 0.8 copy-start.7
  110.4 7.5 %collective-permute-start.26 = (bf16[4,560,128]{2,1,0:T(8,128)(2,1)}, bf16[4,560,128]{2,1,0:T(8,128)(2,1)}, u32[]{:S(2)}, u32[]{:S(2)}) collective-permute-start(bf16[4,560,128]{2,1,0:T(8,128)(2,1)} %collective-permute-done.12.refs_4_), channel_id=1, source_target_pairs={{0,1},{1,0},{2,3},{3,2},{4,5},{5,4},{6,7},{7,6},{8,9},{9,8},{10,11... | collective-permute-start | bytes 1720328 | tf_op jit(solution)/shard_map/ppermute | solution.py:259
  111.8 17.1 %all-to-all-start.3 = ((bf16[32,64,128]{2,1,0:T(8,128)(2,1)}), bf16[32,64,128]{2,1,0:T(8,128)(2,1)S(1)}, u32[]{:S(2)}, u32[]{:S(2)}) async-start(bf16[32,64,128]{2,1,0:T(8,128)(2,1)} %bitcast.12), calls=%async_computation.3 | async-start | bytes 1048576 | tf_op jit(solution)/shard_map/all_to_all | solution.py:254
  128.9 1.1 copy-start.2
  130.0 1.1 copy-start.4
  131.1 1.1 copy-start.6
  132.1 1.1 copy-start.8

commit v4 on v3

--- a/solution.py
+++ b/solution.py
@@ -1,3 +1,5 @@
+import functools
+
 import jax
 import jax.numpy as jnp
 from jax import lax
@@ -20,7 +22,7 @@
 NX, NZ, NY, NC = 4, 8, 4, 2
 ROWS_X = D // NX
 COLS = 2304
-BIG = 40 * 1024 * 1024
+BIG = 16 * 1024 * 1024
 SMALL = 12 * 1024 * 1024
 
 
@@ -167,31 +169,7 @@
         every[4 + k] = by_y[k][...]
 
 
-def project_kernel(at_ref, q_ref, p_ref, g_ref, *refs):
-    parts, (o_ref, w_ref, mixed_ref, normed_ref, sem) = refs[:16], refs[16:]
-    x, y, core = at_ref[0], at_ref[1], at_ref[2]
-    copies = []
-
-    def fetch(source, block, column):
-        rows = pl.ds(pl.multiple_of(block * ROWS_X, 16), ROWS_X)
-        target = w_ref.at[rows, pl.ds(pl.multiple_of(column, 128), 128)]
-        copies.append(pltpu.make_async_copy(source, target, sem.at[len(copies)]))
-        copies[-1].start()
-
-    for side in range(NC):
-        which = core if side == 0 else 1 - core
-        every, *rest = parts[8 * side : 8 * side + 8]
-        by_y, by_x = (every.at[pl.ds(0, 4)], *rest[:3]), (every.at[pl.ds(4, 4)], *rest[3:6])
-        edges = rest[6]
-        for k in range(4):
-            block = lax.rem(x - k + NX, NX)
-            column = which * 1024 + lax.rem(y - k + NY, NY) * 256
-            fetch(edges.at[k], block, 2048 + which * 128)
-            for n in range(4):
-                turn = lax.rem(y - n + NY, NY)
-                fetch(by_y[n].at[k], block, which * 1024 + turn * 256)
-                turn = lax.rem(x - n + NX, NX)
-                fetch(by_x[n].at[k], turn, column + 128)
+def mix_kernel(q_ref, p_ref, g_ref, o_ref, mixed_ref):
     tokens = q_ref.shape[1]
     squares = jnp.zeros((1, tokens), f32)
     lane = lax.broadcasted_iota(jnp.int32, (HEAD_DIM, PAD), 1) // 16
@@ -218,36 +196,91 @@
         width = min(256, D - i)
         rows = pl.ds(i, width)
         normed = (mixed_ref[rows, :] * scale * g_ref[rows, :]).astype(bf16)
-        normed_ref[:, pl.ds(i, width)] = normed.T
+        o_ref[:, pl.ds(i, width)] = normed.T
+
+
+def mix(q_t, prefix, gain):
+    tokens = q_t.shape[1]
+    vmem = pl.BlockSpec(memory_space=pltpu.VMEM)
+    return pl.pallas_call(
+        mix_kernel,
+        in_specs=[vmem] * 3,
+        out_specs=vmem,
+        out_shape=jax.ShapeDtypeStruct((tokens, D), bf16),
+        scratch_shapes=[pltpu.VMEM((D, tokens), f32)],
+        compiler_params=pltpu.CompilerParams(vmem_limit_bytes=BIG),
+        name="mix",
+        cost_estimate=pl.CostEstimate(
+            flops=2 * D * PAD * tokens, bytes_accessed=4 * D * tokens, transcendentals=0
+        ),
+    )(q_t, prefix, gain)
+
+
+def project_kernel(count, at_ref, n_ref, every, y1, y2, y3, x1, x2, x3, *refs):
+    edges = refs[: count - 4]
+    o_ref, w_ref, out_ref, sem, out_sem = refs[-5:]
+    x, y, which = at_ref[0], at_ref[1], at_ref[2]
+    by_y, by_x = (every.at[pl.ds(0, 4)], y1, y2, y3), (every.at[pl.ds(4, 4)], x1, x2, x3)
+    copies = []
+
+    def fetch(source, block, column):
+        rows = pl.ds(pl.multiple_of(block * ROWS_X, 16), ROWS_X)
+        target = w_ref.at[rows, pl.ds(pl.multiple_of(column, 128), 128)]
+        copies.append(pltpu.make_async_copy(source, target, sem.at[len(copies)]))
+        copies[-1].start()
+
+    for k in range(4):
+        block = lax.rem(x - k + NX, NX)
+        for n in range(4):
+            fetch(by_y[n].at[k], block, n * 256)
+            fetch(by_x[k].at[n], block, n * 256 + 128)
+        for side, edge in zip((which, 1 - which), edges):
+            fetch(edge.at[k], block, 1024 + side * 128)
     for copy in copies:
         copy.wait()
-    for j in range(0, D, 256):
-        width = min(256, D - j)
-        total = jnp.dot(normed_ref[...], w_ref[:, pl.ds(j, 256)], preferred_element_type=f32)
-        o_ref[pl.ds(j, width), :] = total.astype(bf16).T[:width]
-
-
-def project(at, q_t, prefix, gain, parts):
-    tokens = q_t.shape[1]
+    for n in range(4 + len(edges) // 2):
+        total = jnp.dot(n_ref[...], w_ref[:, pl.ds(n * 256, 256)], preferred_element_type=f32)
+        out_ref[pl.ds(n * 256, 256), :] = total.astype(bf16).T
+    stores = []
+    for n in range(4):
+        at = pl.multiple_of(which * 1024 + lax.rem(y - n + NY, NY) * 256, 256)
+        stores.append((n * 256, at, 256))
+    if edges:
+        stores.append((1024, 2048, D - 2048))
+    stores = [
+        pltpu.make_async_copy(
+            out_ref.at[pl.ds(start, size), :], o_ref.at[pl.ds(at, size), :], out_sem.at[i]
+        )
+        for i, (start, at, size) in enumerate(stores)
+    ]
+    for store in stores:
+        store.start()
+    for store in stores:
+        store.wait()
+
+
+def project(at, normed, parts, edges=(), out=None):
+    tokens = normed.shape[0]
     vmem = pl.BlockSpec(memory_space=pltpu.VMEM)
     anyw = pl.BlockSpec(memory_space=pl.ANY)
+    extra = [*edges] if out is None else [*edges, out]
     return pl.pallas_call(
-        project_kernel,
-        in_specs=[pl.BlockSpec(memory_space=pltpu.SMEM), vmem, vmem, vmem] + [anyw] * 16,
-        out_specs=vmem,
+        functools.partial(project_kernel, 4 + len(edges)),
+        in_specs=[pl.BlockSpec(memory_space=pltpu.SMEM), vmem] + [anyw] * (7 + len(extra)),
+        out_specs=anyw,
         out_shape=jax.ShapeDtypeStruct((D, tokens), bf16),
+        input_output_aliases={} if out is None else {8 + len(extra): 0},
         scratch_shapes=[
-            pltpu.VMEM((D, COLS), bf16),
-            pltpu.VMEM((D, tokens), f32),
-            pltpu.VMEM((tokens, D), bf16),
-            pltpu.SemaphoreType.DMA((72,)),
+            pltpu.VMEM((D, 1280), bf16),
+            pltpu.VMEM((1280, tokens), bf16),
+            pltpu.SemaphoreType.DMA((40,)),
+            pltpu.SemaphoreType.DMA((5,)),
         ],
-        compiler_params=pltpu.CompilerParams(vmem_limit_bytes=BIG),
-        name="project",
+        compiler_params=pltpu.CompilerParams(vmem_limit_bytes=16 * 1024 * 1024),
         cost_estimate=pl.CostEstimate(
-            flops=2 * D * D * tokens, bytes_accessed=2 * D * COLS + 4 * D * tokens, transcendentals=0
+            flops=D * D * tokens, bytes_accessed=D * COLS + 3 * D * tokens, transcendentals=0
         ),
-    )(at, q_t, prefix, gain, *parts)
+    )(at, normed, *parts, *extra)
 
 
 def swap(value, axes):
@@ -308,9 +341,13 @@
     parts.append(edge)
     r3 = small_call(prefix_kernel, jax.ShapeDtypeStruct((NX, 8, PART, PAD), bf16), (), (r2s,))
     prefix = swap(r3.reshape(32, PART, PAD), PIECES).reshape(2048, PAD)
-    parts += [moved(part, "core", 1) for part in parts]
-    at = jnp.stack([lax.axis_index("x"), y, core]).astype(jnp.int32)
-    out = project(at, q_t, prefix, gain.reshape(D, 1), parts)
+    *other, edge2 = [moved(part, "core", 1) for part in parts]
+    *parts, edge = parts
+    normed = mix(q_t, prefix, gain.reshape(D, 1))
+    place = [lax.axis_index("x"), y]
+    at = [jnp.stack([*place, side]).astype(jnp.int32) for side in (core, 1 - core)]
+    out = project(at[0], normed, parts)
+    out = project(at[1], normed, other, (edge2, edge), out)
     return jnp.swapaxes(out, 0, 1)[None]
 
 

time: 149 us -> 146 us (0.980)
  the two profiles are of different devices: /device:TPU:1 before, /device:TPU:2 now
where the time goes in v4:
time: 146 us; the launch traced here: 144 us
  starting transfers between devices  61.9 us (42%)
  waiting for transfers between devices  49.9 us (34%)
  Pallas kernels  28.8 us (20%)
  local copies, waits for them, and re-layouts  3.14 us (2%)
    ppermute x30, waiting for transfers between devices, moved(): return lax.ppermute(value, axis, [(i, (i + step) % n) for i in range(n)])  39.1 us
    ppermute x30, starting transfers between devices, moved(): return lax.ppermute(value, axis, [(i, (i + step) % n) for i in range(n)])  36 us
    all_to_all x4, starting transfers between devices, swap(): return lax.all_to_all(value, axes, split_axis=0, concat_axis=0, tiled=True)  26 us
    pallas_call x2, Pallas kernels, project(): pl.pallas_call(functools.partial(project_kernel, 4 + len(edges)), in_spec...  15.9 us
    all_to_all x4, waiting for transfers between devices, swap(): return lax.all_to_all(value, axes, split_axis=0, concat_axis=0, tiled=True)  10.9 us
    pallas_call x1, Pallas kernels, states(): pl.pallas_call(state_kernel, grid=(HEADS // GROUP,), in_specs=[spec, spec...  5.78 us
    pallas_call x6, Pallas kernels, small_call(): pl.pallas_call(kernel, in_specs=[pl.BlockSpec(memory_space=pltpu.SMEM)] *...  4.74 us
  transfers between devices with their start and end apart: 34, of which 10 were waited for; matrix products, arithmetic and copies ran while one was open for 0% of the time, Pallas kernels for 13%

profile of v4, /device:TPU:2, one launch (start us, length us, event | category | flops | bytes accessed | tf_op | source)
XLA Modules:
  0.0 144.4 jit_solution(14133334104505304521)
XLA Ops:
  0.1 1.0 copy-done.3
  1.1 1.3 shard_map.55
  2.3 8.5 %all-to-all-start = ((bf16[8,70,256]{2,1,0:T(8,128)(2,1)}), bf16[8,70,256]{2,1,0:T(8,128)(2,1)S(1)}, u32[]{:S(2)}, u32[]{:S(2)}) async-start(bf16[8,70,256]{2,1,0:T(8,128)(2,1)} %get-tuple-element.14), calls=%async_computation | async-start | bytes 589824 | tf_op jit(solution)/shard_map/all_to_all | solution.py:287
  10.8 5.8 %states.1 = bf16[2048,128]{1,0:T(8,128)(2,1)} custom-call(bf16[2240,640]{1,0:T(8,128)(2,1)} %bitcast.23, bf16[2240,640]{1,0:T(8,128)(2,1)} %bitcast.24), custom_call_target="tpu_custom_call" | custom-call | flops 419430400 | bytes 5734400 | tf_op jit(solution)/shard_map/states/pallas_call | solution.py:70
  16.6 6.8 %all-to-all-done.w_ref = bf16[8,70,256]{2,1,0:T(8,128)(2,1)S(1)} async-done(((bf16[8,70,256]{2,1,0:T(8,128)(2,1)}), bf16[8,70,256]{2,1,0:T(8,128)(2,1)S(1)}, u32[]{:S(2)}, u32[]{:S(2)}) %all-to-all-start) | async-done | bytes 286752 | tf_op jit(solution)/shard_map/all_to_all | solution.py:287
  23.4 7.6 %all-to-all-start.1 = ((bf16[32,64,128]{2,1,0:T(8,128)(2,1)}), bf16[32,64,128]{2,1,0:T(8,128)(2,1)S(1)}, u32[]{:S(2)}, u32[]{:S(2)}) async-start(bf16[32,64,128]{2,1,0:T(8,128)(2,1)} %bitcast.12), calls=%async_computation.1 | async-start | bytes 1048576 | tf_op jit(solution)/shard_map/all_to_all | solution.py:287
  31.0 1.5 %collective-permute-start = (bf16[70,128]{1,0:T(8,128)(2,1)S(1)}, bf16[70,128]{1,0:T(8,128)(2,1)S(1)}, u32[]{:S(2)}, u32[]{:S(2)}) collective-permute-start(bf16[70,128]{1,0:T(8,128)(2,1)S(1)} %get-tuple-element.16.r0), channel_id=1, source_target_pairs={{0,64},{64,128},{128,192},{192,0},{1,65},{65,129},{129,193},{193,1... | collective-permute-start | bytes 53768 | tf_op jit(solution)/shard_map/ppermute | solution.py:292
  32.6 0.8 collective-permute-start.1
  33.4 2.4 %collective-permute-start.2 = (bf16[70,128]{1,0:T(8,128)(2,1)S(1)}, bf16[70,128]{1,0:T(8,128)(2,1)S(1)}, u32[]{:S(2)}, u32[]{:S(2)}) collective-permute-start(bf16[70,128]{1,0:T(8,128)(2,1)S(1)} %get-tuple-element.16.r0), channel_id=1, source_target_pairs={{0,192},{64,0},{128,64},{192,128},{1,193},{65,1},{129,65},{193,129... | collective-permute-start | bytes 53768 | tf_op jit(solution)/shard_map/ppermute | solution.py:292
  35.8 2.8 %collective-permute-done.r1 = bf16[70,128]{1,0:T(8,128)(2,1)S(1)} collective-permute-done((bf16[70,128]{1,0:T(8,128)(2,1)S(1)}, bf16[70,128]{1,0:T(8,128)(2,1)S(1)}, u32[]{:S(2)}, u32[]{:S(2)}) %collective-permute-start) | collective-permute-done | bytes 17952 | tf_op jit(solution)/shard_map/ppermute | solution.py:292
  38.7 1.7 %collective-permute-done.1.r2 = bf16[70,128]{1,0:T(8,128)(2,1)S(1)} collective-permute-done((bf16[70,128]{1,0:T(8,128)(2,1)S(1)}, bf16[70,128]{1,0:T(8,128)(2,1)S(1)}, u32[]{:S(2)}, u32[]{:S(2)}) %collective-permute-start.1) | collective-permute-done | bytes 17952 | tf_op jit(solution)/shard_map/ppermute | solution.py:292
  40.5 0.6 collective-permute-start.22
  41.3 2.5 %collective-permute-start.24 = (bf16[4,70,128]{2,1,0:T(8,128)(2,1)S(1)}, bf16[4,70,128]{2,1,0:T(8,128)(2,1)S(1)}, u32[]{:S(2)}, u32[]{:S(2)}) collective-permute-start(bf16[4,70,128]{2,1,0:T(8,128)(2,1)S(1)} %get-tuple-element.22.refs_0_), channel_id=1, source_target_pairs={{0,24},{8,32},{16,40},{24,48},{32,56},{40,0},{48,8},{56,16},{1,25}... | collective-permute-start | bytes 215048 | tf_op jit(solution)/shard_map/ppermute | solution.py:292
  43.8 0.8 collective-permute-start.3
  44.5 3.4 %collective-permute-start.25 = (bf16[4,70,128]{2,1,0:T(8,128)(2,1)S(1)}, bf16[4,70,128]{2,1,0:T(8,128)(2,1)S(1)}, u32[]{:S(2)}, u32[]{:S(2)}) collective-permute-start(bf16[4,70,128]{2,1,0:T(8,128)(2,1)S(1)} %get-tuple-element.22.refs_0_), channel_id=1, source_target_pairs={{0,32},{8,40},{16,48},{24,56},{32,0},{40,8},{48,16},{56,24},{1,33}... | collective-permute-start | bytes 215048 | tf_op jit(solution)/shard_map/ppermute | solution.py:292
  47.9 0.3 collective-permute-done.22.refs_1_
  48.2 0.9 collective-permute-start.26
  49.1 4.3 %collective-permute-done.23.refs_2_ = bf16[4,70,128]{2,1,0:T(8,128)(2,1)S(1)} collective-permute-done((bf16[4,70,128]{2,1,0:T(8,128)(2,1)S(1)}, bf16[4,70,128]{2,1,0:T(8,128)(2,1)S(1)}, u32[]{:S(2)}, u32[]{:S(2)}) %collective-permute-start.23) | collective-permute-done | bytes 71712 | tf_op jit(solution)/shard_map/ppermute | solution.py:292
  53.4 2.5 %collective-permute-start.28 = (bf16[4,70,128]{2,1,0:T(8,128)(2,1)S(1)}, bf16[4,70,128]{2,1,0:T(8,128)(2,1)S(1)}, u32[]{:S(2)}, u32[]{:S(2)}) collective-permute-start(bf16[4,70,128]{2,1,0:T(8,128)(2,1)S(1)} %get-tuple-element.22.refs_0_), channel_id=1, source_target_pairs={{0,56},{8,0},{16,8},{24,16},{32,24},{40,32},{48,40},{56,48},{1,57}... | collective-permute-start | bytes 215048 | tf_op jit(solution)/shard_map/ppermute | solution.py:292
  55.9 1.4 collective-permute-start.4
  57.5 1.5 %collective-permute-start.5 = (bf16[560,128]{1,0:T(8,128)(2,1)S(1)}, bf16[560,128]{1,0:T(8,128)(2,1)S(1)}, u32[]{:S(2)}, u32[]{:S(2)}) collective-permute-start(bf16[560,128]{1,0:T(8,128)(2,1)S(1)} %get-tuple-element.17.refs_0_), channel_id=1, source_target_pairs={{0,192},{64,0},{128,64},{192,128},{1,193},{65,1},{129,65},{193,129... | collective-permute-start | bytes 430088 | tf_op jit(solution)/shard_map/ppermute | solution.py:292
  59.0 2.0 %collective-permute-done.27.refs_6_ = bf16[4,70,128]{2,1,0:T(8,128)(2,1)S(1)} collective-permute-done((bf16[4,70,128]{2,1,0:T(8,128)(2,1)S(1)}, bf16[4,70,128]{2,1,0:T(8,128)(2,1)S(1)}, u32[]{:S(2)}, u32[]{:S(2)}) %collective-permute-start.27) | collective-permute-done | bytes 71712 | tf_op jit(solution)/shard_map/ppermute | solution.py:292
  61.0 1.4 collective-permute-start.6
  62.4 2.7 %collective-permute-start.7 = (bf16[560,128]{1,0:T(8,128)(2,1)S(1)}, bf16[560,128]{1,0:T(8,128)(2,1)S(1)}, u32[]{:S(2)}, u32[]{:S(2)}) collective-permute-start(bf16[560,128]{1,0:T(8,128)(2,1)S(1)} %get-tuple-element.18.refs_4_), channel_id=1, source_target_pairs={{0,4},{2,6},{4,0},{6,2},{1,5},{3,7},{5,1},{7,3},{8,12},{10,14},{12... | collective-permute-start | bytes 430088 | tf_op jit(solution)/shard_map/ppermute | solution.py:292
  65.1 1.4 collective-permute-start.8
  66.5 0.9 shard_map.56
  67.4 4.2 %all-to-all-start.2 = ((bf16[8,4,64,128]{3,2,1,0:T(8,128)(2,1)}), bf16[8,4,64,128]{3,2,1,0:T(8,128)(2,1)S(1)}, u32[]{:S(2)}, u32[]{:S(2)}) async-start(bf16[8,4,64,128]{3,2,1,0:T(8,128)(2,1)} %shard_map.56), calls=%async_computation.2 | async-start | bytes 1048576 | tf_op jit(solution)/shard_map/all_to_all | solution.py:287
  72.0 1.4 shard_map.59
  73.4 0.7 collective-permute-start.10
  74.0 1.7 %collective-permute-start.12 = (bf16[4,560,128]{2,1,0:T(8,128)(2,1)S(1)}, bf16[4,560,128]{2,1,0:T(8,128)(2,1)}, u32[]{:S(2)}, u32[]{:S(2)}) collective-permute-start(bf16[4,560,128]{2,1,0:T(8,128)(2,1)S(1)} %get-tuple-element.20), channel_id=1, source_target_pairs={{0,4},{2,6},{4,0},{6,2},{1,5},{3,7},{5,1},{7,3},{8,12},{10,14},{12... | collective-permute-start | bytes 1720328 | tf_op jit(solution)/shard_map/ppermute | solution.py:292
  75.8 1.3 collective-permute-start.14
  77.1 0.9 collective-permute-start.16
  78.0 3.2 %collective-permute-start.18 = (bf16[4,560,128]{2,1,0:T(8,128)(2,1)}, bf16[4,560,128]{2,1,0:T(8,128)(2,1)}, u32[]{:S(2)}, u32[]{:S(2)}) collective-permute-start(bf16[4,560,128]{2,1,0:T(8,128)(2,1)} %get-tuple-element.21), channel_id=1, source_target_pairs={{0,128},{64,192},{128,0},{192,64},{1,129},{65,193},{129,1},{193,65... | collective-permute-start | bytes 1720328 | tf_op jit(solution)/shard_map/ppermute | solution.py:292
  81.2 21.2 %collective-permute-done.10.y1 = bf16[4,560,128]{2,1,0:T(8,128)(2,1)} collective-permute-done((bf16[4,560,128]{2,1,0:T(8,128)(2,1)S(1)}, bf16[4,560,128]{2,1,0:T(8,128)(2,1)}, u32[]{:S(2)}, u32[]{:S(2)}) %collective-permute-start.10) | collective-permute-done | bytes 573472 | tf_op jit(solution)/shard_map/ppermute | solution.py:292
  102.3 2.4 %collective-permute-start.20 = (bf16[4,560,128]{2,1,0:T(8,128)(2,1)}, bf16[4,560,128]{2,1,0:T(8,128)(2,1)}, u32[]{:S(2)}, u32[]{:S(2)}) collective-permute-start(bf16[4,560,128]{2,1,0:T(8,128)(2,1)} %get-tuple-element.21), channel_id=1, source_target_pairs={{0,192},{64,0},{128,64},{192,128},{1,193},{65,1},{129,65},{193,129... | collective-permute-start | bytes 1720328 | tf_op jit(solution)/shard_map/ppermute | solution.py:292
  104.7 0.5 collective-permute-start.13
  105.3 0.9 shard_map.57
  106.2 5.7 %all-to-all-start.3 = ((bf16[32,64,128]{2,1,0:T(8,128)(2,1)}), bf16[32,64,128]{2,1,0:T(8,128)(2,1)S(1)}, u32[]{:S(2)}, u32[]{:S(2)}) async-start(bf16[32,64,128]{2,1,0:T(8,128)(2,1)} %bitcast.13), calls=%async_computation.3 | async-start | bytes 1048576 | tf_op jit(solution)/shard_map/all_to_all | solution.py:287
  111.9 0.2 collective-permute-start.15
  112.1 6.6 %collective-permute-done.20.x3 = bf16[4,560,128]{2,1,0:T(8,128)(2,1)} collective-permute-done((bf16[4,560,128]{2,1,0:T(8,128)(2,1)}, bf16[4,560,128]{2,1,0:T(8,128)(2,1)}, u32[]{:S(2)}, u32[]{:S(2)}) %collective-permute-start.20) | collective-permute-done | bytes 573472 | tf_op jit(solution)/shard_map/ppermute | solution.py:292
  118.7 0.5 collective-permute-start.19
  119.2 0.3 collective-permute-start.21
  119.5 0.3 reshape.20.g_ref
  120.0 4.0 %all-to-all-done.3 = bf16[32,64,128]{2,1,0:T(8,128)(2,1)S(1)} async-done(((bf16[32,64,128]{2,1,0:T(8,128)(2,1)}), bf16[32,64,128]{2,1,0:T(8,128)(2,1)S(1)}, u32[]{:S(2)}, u32[]{:S(2)}) %all-to-all-start.3) | async-done | bytes 524320 | tf_op jit(solution)/shard_map/all_to_all | solution.py:287
  124.1 1.8 %copy-done = bf16[1,640,2240]{1,2,0:T(8,128)(2,1)S(1)} copy-done((bf16[1,640,2240]{1,2,0:T(8,128)(2,1)S(1)}, bf16[1,640,2240]{1,2,0:T(8,128)(2,1)}, u32[]{:S(2)}) %copy-start) | copy-done | bytes 2867224
  125.9 2.4 %mix.1.n_ref = bf16[640,2240]{1,0:T(8,128)(2,1)S(1)} custom-call(bf16[2240,640]{1,0:T(8,128)(2,1)S(1)} %bitcast.21, bf16[2048,128]{1,0:T(8,128)(2,1)S(1)} %bitcast.22, f32[2240,1]{1,0:T(8,128)S(1)} %reshape.20.g_ref), custom_call_target="tpu_custom_call" | custom-call | flops 367001600 | bytes 5734400 | tf_op jit(solution)/shard_map/mix/pallas_call | solution.py:205
  128.3 7.6 %shard_map.61.refs_2_ = bf16[2240,640]{1,0:T(8,128)(2,1)} custom-call(s32[3]{0:T(128)S(1)} %pad_add_fusion.3.at_ref, bf16[640,2240]{1,0:T(8,128)(2,1)S(1)} %mix.1.n_ref, bf16[8,560,128]{2,1,0:T(8,128)(2,1)} %get-tuple-element.19.every, bf16[4,560,128]{2,1,0:T(8,128)(2,1)} %collective-permute-done.10.y1, bf16[4,560,128]{2,1,0:T(8,128)(2,1)} %collective-permute-done.12.y2, ...), custom_call_target="tpu_custom_call" | custom-call | flops 3211264000 | bytes 9461760 | tf_op jit(solution)/shard_map/pallas_call | solution.py:267
  136.0 8.2 %shard_map.62 = bf16[2240,640]{1,0:T(8,128)(2,1)} custom-call(s32[3]{0:T(128)S(1)} %pad_add_fusion.at_ref, bf16[640,2240]{1,0:T(8,128)(2,1)S(1)} %mix.1.n_ref, bf16[8,560,128]{2,1,0:T(8,128)(2,1)S(1)} %collective-permute-done.9.every, bf16[4,560,128]{2,1,0:T(8,128)(2,1)} %collective-permute-done.11.y1, ...), custom_call_target="tpu_custom_call", output_to_operand_aliasing={{}: (11, {})} | custom-call | flops 3211264000 | bytes 9461760 | tf_op jit(solution)/shard_map/pallas_call | solution.py:267
  (44 shorter events, 1.0 us)
Async XLA Ops:
  0.1 1.0 copy-start.3
  2.3 21.0 %all-to-all-start = ((bf16[8,70,256]{2,1,0:T(8,128)(2,1)}), bf16[8,70,256]{2,1,0:T(8,128)(2,1)S(1)}, u32[]{:S(2)}, u32[]{:S(2)}) async-start(bf16[8,70,256]{2,1,0:T(8,128)(2,1)} %get-tuple-element.14), calls=%async_computation | async-start | bytes 589824 | tf_op jit(solution)/shard_map/all_to_all | solution.py:287
  23.4 43.1 %all-to-all-start.1 = ((bf16[32,64,128]{2,1,0:T(8,128)(2,1)}), bf16[32,64,128]{2,1,0:T(8,128)(2,1)S(1)}, u32[]{:S(2)}, u32[]{:S(2)}) async-start(bf16[32,64,128]{2,1,0:T(8,128)(2,1)} %bitcast.12), calls=%async_computation.1 | async-start | bytes 1048576 | tf_op jit(solution)/shard_map/all_to_all | solution.py:287
  31.0 7.7 %collective-permute-start = (bf16[70,128]{1,0:T(8,128)(2,1)S(1)}, bf16[70,128]{1,0:T(8,128)(2,1)S(1)}, u32[]{:S(2)}, u32[]{:S(2)}) collective-permute-start(bf16[70,128]{1,0:T(8,128)(2,1)S(1)} %get-tuple-element.16.r0), channel_id=1, source_target_pairs={{0,64},{64,128},{128,192},{192,0},{1,65},{65,129},{129,193},{193,1... | collective-permute-start | bytes 53768 | tf_op jit(solution)/shard_map/ppermute | solution.py:292
  32.6 7.8 %collective-permute-start.1 = (bf16[70,128]{1,0:T(8,128)(2,1)S(1)}, bf16[70,128]{1,0:T(8,128)(2,1)S(1)}, u32[]{:S(2)}, u32[]{:S(2)}) collective-permute-start(bf16[70,128]{1,0:T(8,128)(2,1)S(1)} %get-tuple-element.16.r0), channel_id=1, source_target_pairs={{0,128},{64,192},{128,0},{192,64},{1,129},{65,193},{129,1},{193,65... | collective-permute-start | bytes 53768 | tf_op jit(solution)/shard_map/ppermute | solution.py:292
  33.4 7.0 %collective-permute-start.2 = (bf16[70,128]{1,0:T(8,128)(2,1)S(1)}, bf16[70,128]{1,0:T(8,128)(2,1)S(1)}, u32[]{:S(2)}, u32[]{:S(2)}) collective-permute-start(bf16[70,128]{1,0:T(8,128)(2,1)S(1)} %get-tuple-element.16.r0), channel_id=1, source_target_pairs={{0,192},{64,0},{128,64},{192,128},{1,193},{65,1},{129,65},{193,129... | collective-permute-start | bytes 53768 | tf_op jit(solution)/shard_map/ppermute | solution.py:292
  40.5 7.7 %collective-permute-start.22 = (bf16[4,70,128]{2,1,0:T(8,128)(2,1)S(1)}, bf16[4,70,128]{2,1,0:T(8,128)(2,1)S(1)}, u32[]{:S(2)}, u32[]{:S(2)}) collective-permute-start(bf16[4,70,128]{2,1,0:T(8,128)(2,1)S(1)} %get-tuple-element.22.refs_0_), channel_id=1, source_target_pairs={{0,8},{8,16},{16,24},{24,32},{32,40},{40,48},{48,56},{56,0},{1,9},... | collective-permute-start | bytes 215048 | tf_op jit(solution)/shard_map/ppermute | solution.py:292
  41.1 12.3 %collective-permute-start.23 = (bf16[4,70,128]{2,1,0:T(8,128)(2,1)S(1)}, bf16[4,70,128]{2,1,0:T(8,128)(2,1)S(1)}, u32[]{:S(2)}, u32[]{:S(2)}) collective-permute-start(bf16[4,70,128]{2,1,0:T(8,128)(2,1)S(1)} %get-tuple-element.22.refs_0_), channel_id=1, source_target_pairs={{0,16},{8,24},{16,32},{24,40},{32,48},{40,56},{48,0},{56,8},{1,17}... | collective-permute-start | bytes 215048 | tf_op jit(solution)/shard_map/ppermute | solution.py:292
  41.3 12.1 %collective-permute-start.24 = (bf16[4,70,128]{2,1,0:T(8,128)(2,1)S(1)}, bf16[4,70,128]{2,1,0:T(8,128)(2,1)S(1)}, u32[]{:S(2)}, u32[]{:S(2)}) collective-permute-start(bf16[4,70,128]{2,1,0:T(8,128)(2,1)S(1)} %get-tuple-element.22.refs_0_), channel_id=1, source_target_pairs={{0,24},{8,32},{16,40},{24,48},{32,56},{40,0},{48,8},{56,16},{1,25}... | collective-permute-start | bytes 215048 | tf_op jit(solution)/shard_map/ppermute | solution.py:292
  43.8 21.3 %collective-permute-start.3 = (bf16[560,128]{1,0:T(8,128)(2,1)S(1)}, bf16[560,128]{1,0:T(8,128)(2,1)S(1)}, u32[]{:S(2)}, u32[]{:S(2)}) collective-permute-start(bf16[560,128]{1,0:T(8,128)(2,1)S(1)} %get-tuple-element.17.refs_0_), channel_id=1, source_target_pairs={{0,64},{64,128},{128,192},{192,0},{1,65},{65,129},{129,193},{193,1... | collective-permute-start | bytes 430088 | tf_op jit(solution)/shard_map/ppermute | solution.py:292
  44.5 11.4 %collective-permute-start.25 = (bf16[4,70,128]{2,1,0:T(8,128)(2,1)S(1)}, bf16[4,70,128]{2,1,0:T(8,128)(2,1)S(1)}, u32[]{:S(2)}, u32[]{:S(2)}) collective-permute-start(bf16[4,70,128]{2,1,0:T(8,128)(2,1)S(1)} %get-tuple-element.22.refs_0_), channel_id=1, source_target_pairs={{0,32},{8,40},{16,48},{24,56},{32,0},{40,8},{48,16},{56,24},{1,33}... | collective-permute-start | bytes 215048 | tf_op jit(solution)/shard_map/ppermute | solution.py:292
  48.2 9.2 %collective-permute-start.26 = (bf16[4,70,128]{2,1,0:T(8,128)(2,1)S(1)}, bf16[4,70,128]{2,1,0:T(8,128)(2,1)S(1)}, u32[]{:S(2)}, u32[]{:S(2)}) collective-permute-start(bf16[4,70,128]{2,1,0:T(8,128)(2,1)S(1)} %get-tuple-element.22.refs_0_), channel_id=1, source_target_pairs={{0,40},{8,48},{16,56},{24,0},{32,8},{40,16},{48,24},{56,32},{1,41}... | collective-permute-start | bytes 215048 | tf_op jit(solution)/shard_map/ppermute | solution.py:292
  53.4 7.6 %collective-permute-start.27 = (bf16[4,70,128]{2,1,0:T(8,128)(2,1)S(1)}, bf16[4,70,128]{2,1,0:T(8,128)(2,1)S(1)}, u32[]{:S(2)}, u32[]{:S(2)}) collective-permute-start(bf16[4,70,128]{2,1,0:T(8,128)(2,1)S(1)} %get-tuple-element.22.refs_0_), channel_id=1, source_target_pairs={{0,48},{8,56},{16,0},{24,8},{32,16},{40,24},{48,32},{56,40},{1,49}... | collective-permute-start | bytes 215048 | tf_op jit(solution)/shard_map/ppermute | solution.py:292
  53.4 9.0 %collective-permute-start.28 = (bf16[4,70,128]{2,1,0:T(8,128)(2,1)S(1)}, bf16[4,70,128]{2,1,0:T(8,128)(2,1)S(1)}, u32[]{:S(2)}, u32[]{:S(2)}) collective-permute-start(bf16[4,70,128]{2,1,0:T(8,128)(2,1)S(1)} %get-tuple-element.22.refs_0_), channel_id=1, source_target_pairs={{0,56},{8,0},{16,8},{24,16},{32,24},{40,32},{48,40},{56,48},{1,57}... | collective-permute-start | bytes 215048 | tf_op jit(solution)/shard_map/ppermute | solution.py:292
  55.9 15.9 %collective-permute-start.4 = (bf16[560,128]{1,0:T(8,128)(2,1)S(1)}, bf16[560,128]{1,0:T(8,128)(2,1)S(1)}, u32[]{:S(2)}, u32[]{:S(2)}) collective-permute-start(bf16[560,128]{1,0:T(8,128)(2,1)S(1)} %get-tuple-element.17.refs_0_), channel_id=1, source_target_pairs={{0,128},{64,192},{128,0},{192,64},{1,129},{65,193},{129,1},{193,65... | collective-permute-start | bytes 430088 | tf_op jit(solution)/shard_map/ppermute | solution.py:292
  57.5 14.4 %collective-permute-start.5 = (bf16[560,128]{1,0:T(8,128)(2,1)S(1)}, bf16[560,128]{1,0:T(8,128)(2,1)S(1)}, u32[]{:S(2)}, u32[]{:S(2)}) collective-permute-start(bf16[560,128]{1,0:T(8,128)(2,1)S(1)} %get-tuple-element.17.refs_0_), channel_id=1, source_target_pairs={{0,192},{64,0},{128,64},{192,128},{1,193},{65,1},{129,65},{193,129... | collective-permute-start | bytes 430088 | tf_op jit(solution)/shard_map/ppermute | solution.py:292
  61.0 10.9 %collective-permute-start.6 = (bf16[560,128]{1,0:T(8,128)(2,1)S(1)}, bf16[560,128]{1,0:T(8,128)(2,1)S(1)}, u32[]{:S(2)}, u32[]{:S(2)}) collective-permute-start(bf16[560,128]{1,0:T(8,128)(2,1)S(1)} %get-tuple-element.18.refs_4_), channel_id=1, source_target_pairs={{0,2},{2,4},{4,6},{6,0},{1,3},{3,5},{5,7},{7,1},{8,10},{10,12},{12... | collective-permute-start | bytes 430088 | tf_op jit(solution)/shard_map/ppermute | solution.py:292
  62.4 9.6 %collective-permute-start.7 = (bf16[560,128]{1,0:T(8,128)(2,1)S(1)}, bf16[560,128]{1,0:T(8,128)(2,1)S(1)}, u32[]{:S(2)}, u32[]{:S(2)}) collective-permute-start(bf16[560,128]{1,0:T(8,128)(2,1)S(1)} %get-tuple-element.18.refs_4_), channel_id=1, source_target_pairs={{0,4},{2,6},{4,0},{6,2},{1,5},{3,7},{5,1},{7,3},{8,12},{10,14},{12... | collective-permute-start | bytes 430088 | tf_op jit(solution)/shard_map/ppermute | solution.py:292
  65.1 6.8 %collective-permute-start.8 = (bf16[560,128]{1,0:T(8,128)(2,1)S(1)}, bf16[560,128]{1,0:T(8,128)(2,1)S(1)}, u32[]{:S(2)}, u32[]{:S(2)}) collective-permute-start(bf16[560,128]{1,0:T(8,128)(2,1)S(1)} %get-tuple-element.18.refs_4_), channel_id=1, source_target_pairs={{0,6},{2,0},{4,2},{6,4},{1,7},{3,1},{5,3},{7,5},{8,14},{10,8},{12,... | collective-permute-start | bytes 430088 | tf_op jit(solution)/shard_map/ppermute | solution.py:292
  67.4 52.1 %copy-start.4 = (f32[2240]{0:T(1024)S(1)}, f32[2240]{0:T(1024)}, u32[]{:S(2)}) copy-start(f32[2240]{0:T(1024)} %param.8) | copy-start | bytes 26884
  67.4 37.9 %all-to-all-start.2 = ((bf16[8,4,64,128]{3,2,1,0:T(8,128)(2,1)}), bf16[8,4,64,128]{3,2,1,0:T(8,128)(2,1)S(1)}, u32[]{:S(2)}, u32[]{:S(2)}) async-start(bf16[8,4,64,128]{3,2,1,0:T(8,128)(2,1)} %shard_map.56), calls=%async_computation.2 | async-start | bytes 1048576 | tf_op jit(solution)/shard_map/all_to_all | solution.py:287
  71.8 6.2 %collective-permute-start.29 = (bf16[4,560,128]{2,1,0:T(8,128)(2,1)S(1)}, bf16[4,560,128]{2,1,0:T(8,128)(2,1)S(1)}, u32[]{:S(2)}, u32[]{:S(2)}) collective-permute-start(bf16[4,560,128]{2,1,0:T(8,128)(2,1)S(1)} %shard_map.60.refs_1_), channel_id=1, source_target_pairs={{0,1},{1,0},{2,3},{3,2},{4,5},{5,4},{6,7},{7,6},{8,9},{9,8},{10,11... | collective-permute-start | bytes 1720328 | tf_op jit(solution)/shard_map/ppermute | solution.py:292
  73.4 29.0 %collective-permute-start.10 = (bf16[4,560,128]{2,1,0:T(8,128)(2,1)S(1)}, bf16[4,560,128]{2,1,0:T(8,128)(2,1)}, u32[]{:S(2)}, u32[]{:S(2)}) collective-permute-start(bf16[4,560,128]{2,1,0:T(8,128)(2,1)S(1)} %get-tuple-element.20), channel_id=1, source_target_pairs={{0,2},{2,4},{4,6},{6,0},{1,3},{3,5},{5,7},{7,1},{8,10},{10,12},{12... | collective-permute-start | bytes 1720328 | tf_op jit(solution)/shard_map/ppermute | solution.py:292
  74.0 30.7 %collective-permute-start.12 = (bf16[4,560,128]{2,1,0:T(8,128)(2,1)S(1)}, bf16[4,560,128]{2,1,0:T(8,128)(2,1)}, u32[]{:S(2)}, u32[]{:S(2)}) collective-permute-start(bf16[4,560,128]{2,1,0:T(8,128)(2,1)S(1)} %get-tuple-element.20), channel_id=1, source_target_pairs={{0,4},{2,6},{4,0},{6,2},{1,5},{3,7},{5,1},{7,3},{8,12},{10,14},{12... | collective-permute-start | bytes 1720328 | tf_op jit(solution)/shard_map/ppermute | solution.py:292
  75.8 29.0 %collective-permute-start.14 = (bf16[4,560,128]{2,1,0:T(8,128)(2,1)S(1)}, bf16[4,560,128]{2,1,0:T(8,128)(2,1)}, u32[]{:S(2)}, u32[]{:S(2)}) collective-permute-start(bf16[4,560,128]{2,1,0:T(8,128)(2,1)S(1)} %get-tuple-element.20), channel_id=1, source_target_pairs={{0,6},{2,0},{4,2},{6,4},{1,7},{3,1},{5,3},{7,5},{8,14},{10,8},{12,... | collective-permute-start | bytes 1720328 | tf_op jit(solution)/shard_map/ppermute | solution.py:292
  77.1 28.2 %collective-permute-start.16 = (bf16[4,560,128]{2,1,0:T(8,128)(2,1)}, bf16[4,560,128]{2,1,0:T(8,128)(2,1)}, u32[]{:S(2)}, u32[]{:S(2)}) collective-permute-start(bf16[4,560,128]{2,1,0:T(8,128)(2,1)} %get-tuple-element.21), channel_id=1, source_target_pairs={{0,64},{64,128},{128,192},{192,0},{1,65},{65,129},{129,193},{193,1... | collective-permute-start | bytes 1720328 | tf_op jit(solution)/shard_map/ppermute | solution.py:292
  78.0 41.2 %copy-start.1 = (bf16[4,560,128]{2,1,0:T(8,128)(2,1)}, bf16[4,560,128]{2,1,0:T(8,128)(2,1)S(1)}, u32[]{:S(2)}) copy-start(bf16[4,560,128]{2,1,0:T(8,128)(2,1)S(1)} %collective-permute-done.29.refs_0_) | copy-start | bytes 1720324
  78.0 33.9 %collective-permute-start.18 = (bf16[4,560,128]{2,1,0:T(8,128)(2,1)}, bf16[4,560,128]{2,1,0:T(8,128)(2,1)}, u32[]{:S(2)}, u32[]{:S(2)}) collective-permute-start(bf16[4,560,128]{2,1,0:T(8,128)(2,1)} %get-tuple-element.21), channel_id=1, source_target_pairs={{0,128},{64,192},{128,0},{192,64},{1,129},{65,193},{129,1},{193,65... | collective-permute-start | bytes 1720328 | tf_op jit(solution)/shard_map/ppermute | solution.py:292
  102.3 16.3 %collective-permute-start.20 = (bf16[4,560,128]{2,1,0:T(8,128)(2,1)}, bf16[4,560,128]{2,1,0:T(8,128)(2,1)}, u32[]{:S(2)}, u32[]{:S(2)}) collective-permute-start(bf16[4,560,128]{2,1,0:T(8,128)(2,1)} %get-tuple-element.21), channel_id=1, source_target_pairs={{0,192},{64,0},{128,64},{192,128},{1,193},{65,1},{129,65},{193,129... | collective-permute-start | bytes 1720328 | tf_op jit(solution)/shard_map/ppermute | solution.py:292
  104.7 14.0 %collective-permute-start.11 = (bf16[4,560,128]{2,1,0:T(8,128)(2,1)}, bf16[4,560,128]{2,1,0:T(8,128)(2,1)}, u32[]{:S(2)}, u32[]{:S(2)}) collective-permute-start(bf16[4,560,128]{2,1,0:T(8,128)(2,1)} %collective-permute-done.10.y1), channel_id=1, source_target_pairs={{0,1},{1,0},{2,3},{3,2},{4,5},{5,4},{6,7},{7,6},{8,9},{9,8},{10,11... | collective-permute-start | bytes 1720328 | tf_op jit(solution)/shard_map/ppermute | solution.py:292
  104.7 14.5 %collective-permute-start.13 = (bf16[4,560,128]{2,1,0:T(8,128)(2,1)}, bf16[4,560,128]{2,1,0:T(8,128)(2,1)}, u32[]{:S(2)}, u32[]{:S(2)}) collective-permute-start(bf16[4,560,128]{2,1,0:T(8,128)(2,1)} %collective-permute-done.12.y2), channel_id=1, source_target_pairs={{0,1},{1,0},{2,3},{3,2},{4,5},{5,4},{6,7},{7,6},{8,9},{9,8},{10,11... | collective-permute-start | bytes 1720328 | tf_op jit(solution)/shard_map/ppermute | solution.py:292
  105.2 30.7 %collective-permute-start.9 = (bf16[8,560,128]{2,1,0:T(8,128)(2,1)}, bf16[8,560,128]{2,1,0:T(8,128)(2,1)S(1)}, u32[]{:S(2)}, u32[]{:S(2)}) collective-permute-start(bf16[8,560,128]{2,1,0:T(8,128)(2,1)} %get-tuple-element.19.every), channel_id=1, source_target_pairs={{0,1},{1,0},{2,3},{3,2},{4,5},{5,4},{6,7},{7,6},{8,9},{9,8},{10,11... | collective-permute-start | bytes 3440648 | tf_op jit(solution)/shard_map/ppermute | solution.py:292
  106.2 17.9 %all-to-all-start.3 = ((bf16[32,64,128]{2,1,0:T(8,128)(2,1)}), bf16[32,64,128]{2,1,0:T(8,128)(2,1)S(1)}, u32[]{:S(2)}, u32[]{:S(2)}) async-start(bf16[32,64,128]{2,1,0:T(8,128)(2,1)} %bitcast.13), calls=%async_computation.3 | async-start | bytes 1048576 | tf_op jit(solution)/shard_map/all_to_all | solution.py:287
  111.9 24.0 %collective-permute-start.15 = (bf16[4,560,128]{2,1,0:T(8,128)(2,1)}, bf16[4,560,128]{2,1,0:T(8,128)(2,1)}, u32[]{:S(2)}, u32[]{:S(2)}) collective-permute-start(bf16[4,560,128]{2,1,0:T(8,128)(2,1)} %collective-permute-done.14.y3), channel_id=1, source_target_pairs={{0,1},{1,0},{2,3},{3,2},{4,5},{5,4},{6,7},{7,6},{8,9},{9,8},{10,11... | collective-permute-start | bytes 1720328 | tf_op jit(solution)/shard_map/ppermute | solution.py:292
  118.7 17.2 %collective-permute-start.17 = (bf16[4,560,128]{2,1,0:T(8,128)(2,1)}, bf16[4,560,128]{2,1,0:T(8,128)(2,1)}, u32[]{:S(2)}, u32[]{:S(2)}) collective-permute-start(bf16[4,560,128]{2,1,0:T(8,128)(2,1)} %collective-permute-done.16.x1), channel_id=1, source_target_pairs={{0,1},{1,0},{2,3},{3,2},{4,5},{5,4},{6,7},{7,6},{8,9},{9,8},{10,11... | collective-permute-start | bytes 1720328 | tf_op jit(solution)/shard_map/ppermute | solution.py:292
  118.7 17.3 %collective-permute-start.19 = (bf16[4,560,128]{2,1,0:T(8,128)(2,1)}, bf16[4,560,128]{2,1,0:T(8,128)(2,1)}, u32[]{:S(2)}, u32[]{:S(2)}) collective-permute-start(bf16[4,560,128]{2,1,0:T(8,128)(2,1)} %collective-permute-done.18.x2), channel_id=1, source_target_pairs={{0,1},{1,0},{2,3},{3,2},{4,5},{5,4},{6,7},{7,6},{8,9},{9,8},{10,11... | collective-permute-start | bytes 1720328 | tf_op jit(solution)/shard_map/ppermute | solution.py:292
  119.2 16.7 %collective-permute-start.21 = (bf16[4,560,128]{2,1,0:T(8,128)(2,1)}, bf16[4,560,128]{2,1,0:T(8,128)(2,1)}, u32[]{:S(2)}, u32[]{:S(2)}) collective-permute-start(bf16[4,560,128]{2,1,0:T(8,128)(2,1)} %collective-permute-done.20.x3), channel_id=1, source_target_pairs={{0,1},{1,0},{2,3},{3,2},{4,5},{5,4},{6,7},{7,6},{8,9},{9,8},{10,11... | collective-permute-start | bytes 1720328 | tf_op jit(solution)/shard_map/ppermute | solution.py:292
  124.1 1.8 %copy-start = (bf16[1,640,2240]{1,2,0:T(8,128)(2,1)S(1)}, bf16[1,640,2240]{1,2,0:T(8,128)(2,1)}, u32[]{:S(2)}) copy-start(bf16[1,640,2240]{1,2,0:T(8,128)(2,1)} %param.5) | copy-start | bytes 8601604
  128.3 7.7 %copy-start.2 = (bf16[4,560,128]{2,1,0:T(8,128)(2,1)S(1)}, bf16[4,560,128]{2,1,0:T(8,128)(2,1)}, u32[]{:S(2)}) copy-start(bf16[4,560,128]{2,1,0:T(8,128)(2,1)} %copy-done.1) | copy-start | bytes 1720324
